TPU v7x, 256 devices: a whole 4x4x8 slice. The times are simulated.
256 devices in a mesh: gx: 32 (over z, x_hi, core), gy: 8 (over x_lo, y).
Axes of the slice: x: 4 (x_hi: 2, x_lo: 2; x = x_hi * 2 + x_lo), y: 4, z: 8, core: 2. Of those that a mesh axis runs over, the one named last changes fastest.
Arguments:
- conc: float32 [32, 2048, 1024], P(None, 'gx', 'gy'), may hold values from -4 to 4
- mobility: float32 [32, 2048, 1024], P(None, 'gx', 'gy'), may hold values from 0.3 to 3
- block_x: float32 [32, 2048, 64], P(None, 'gx'), may hold values from -0.75 to 0.75
- spike_x: float32 [32, 2048, 4], P(None, 'gx'), may hold values from -3 to 3
- reduced_x: float32 [32, 128, 128], replicated, may hold values from -0.5 to 0.5
- block_y: float32 [32, 1024, 128], P(None, 'gy'), may hold values from -0.5 to 0.5
- spike_y: float32 [32, 1024, 4], P(None, 'gy'), may hold values from -3 to 3
- reduced_y: float32 [32, 32, 32], replicated, may hold values from -1 to 1
Outputs:
- conc_next: float32 [32, 2048, 1024], P(None, 'gx', 'gy')
All inputs are finite; a program needn't handle non-finite values.
Results may differ from a plain program's by a relative error of at most 0.00012.
Values sent between devices are 32-bit elements; how exact they have to be, the bound alone decides.
No kernel may reach another device: no remote copies, remote signals or barrier semaphores. Data moves between devices by JAX's collectives and lax.ppermute only.
A program may use at most 64 MiB of HBM per device.

v0:
```python
import jax
import jax.numpy as jnp
from jax import lax
from jax.sharding import PartitionSpec as P

HIGH = lax.Precision.HIGHEST


def extended_2(shard, sides, width):
    for axis, dim in sides:
        devices, length = (lax.axis_size(axis), shard.shape[dim])
        up = [(i, (i + 1) % devices) for i in range(devices)]
        down = [(j, i) for i, j in up]
        last = lax.slice_in_dim(shard, length - width, length, axis=dim)
        leading = lax.slice_in_dim(shard, 0, width, axis=dim)
        before = lax.ppermute(last, axis, up)
        after = lax.ppermute(leading, axis, down)
        shard = jnp.concatenate([before, shard, after], axis=dim)
    return shard


def divergence(conc, mu_ext, mob_ext):
    mu_mid = mu_ext[:, 1:-1, 1:-1]
    mob_mid = mob_ext[:, 1:-1, 1:-1]
    total = jnp.zeros_like(conc)
    for lo_x, hi_x, lo_y, hi_y in (
        (2, None, 1, -1),
        (0, -2, 1, -1),
        (1, -1, 2, None),
        (1, -1, 0, -2),
    ):
        mu_side = mu_ext[:, lo_x:hi_x, lo_y:hi_y]
        mob_side = mob_ext[:, lo_x:hi_x, lo_y:hi_y]
        total = total + 0.5 * (mob_side + mob_mid) * (mu_side - mu_mid)
    return conc + 0.02 * total


def laplace(padded):
    return (
        padded[:, 2:, 1:-1]
        + padded[:, :-2, 1:-1]
        + padded[:, 1:-1, 2:]
        + padded[:, 1:-1, :-2]
        - 4.0 * padded[:, 1:-1, 1:-1]
    )


def potential(centre, lap):
    return centre * centre * centre - centre - 1.0 * lap


def mobile(prefactor, centre):
    sq = centre * centre
    return prefactor * (0.25 + sq) / (1.0 + sq)


def solve_x(field, block_x, spike_x, reduced_x):
    width = field.shape[1]
    lin = jnp.einsum("zij,zjn->zin", block_x, field, precision=HIGH)
    rims = jnp.concatenate([lin[:, 0:2], lin[:, width - 2 :]], axis=1)
    whole = reduced_x.shape[1]
    place = lax.axis_index("gx")
    gathered = lax.all_gather(rims, "gx", axis=1, tiled=True)
    offsets = jnp.array([-2, -1, 4, 5], jnp.int32)
    picks = (4 * place + offsets) % whole
    rows_used = jnp.take(reduced_x, picks, axis=1)
    coupled = jnp.einsum("zrk,zkn->zrn", rows_used, gathered, precision=HIGH)
    return lin - jnp.einsum("zik,zkn->zin", spike_x, coupled, precision=HIGH)


def solve_y(field, block_y, spike_y, reduced_y):
    width = field.shape[2]
    lin = jnp.einsum("zij,zxj->zxi", block_y, field, precision=HIGH)
    rims = jnp.transpose(
        jnp.concatenate([lin[:, :, 0:2], lin[:, :, width - 2 :]], axis=2), (0, 2, 1)
    )
    gathered = lax.all_gather(rims, "gy", axis=1, tiled=True)
    whole = reduced_y.shape[1]
    place = lax.axis_index("gy")
    offsets = jnp.array([-2, -1, 4, 5], jnp.int32)
    picks = (4 * place + offsets) % whole
    rows_used = jnp.take(reduced_y, picks, axis=1)
    coupled = jnp.einsum("zrk,zkx->zrx", rows_used, gathered, precision=HIGH)
    return lin - jnp.einsum("zik,zkx->zxi", spike_y, coupled, precision=HIGH)


def body(conc, mobility, block_x, spike_x, reduced_x, block_y, spike_y, reduced_y):
    padded = extended_2(conc, (("gx", 1), ("gy", 2)), 1)
    mu_here = potential(conc, laplace(padded))
    mob_here = mobile(mobility, conc)
    extended = extended_2(jnp.stack([mu_here, mob_here]), (("gx", 2), ("gy", 3)), 1)
    rhs = divergence(conc, extended[0], extended[1])
    xsol = solve_x(rhs, block_x, spike_x, reduced_x)
    return solve_y(xsol, block_y, spike_y, reduced_y)


def solution(mesh):
    in_specs = (
        P(None, "gx", "gy"),
        P(None, "gx", "gy"),
        P(None, "gx", None),
        P(None, "gx", None),
        P(),
        P(None, "gy", None),
        P(None, "gy", None),
        P(),
    )
    out_specs = P(None, "gx", "gy")
    return jax.shard_map(body, mesh=mesh, in_specs=in_specs, out_specs=out_specs, check_vma=False)
```

profile of v0, /device:TPU:24, one launch (start us, length us, event | category | flops | bytes accessed | tf_op | source)
XLA Modules:
  0.0 214.3 jit_solution(208142378381438117)
XLA Ops:
  7.7 7.8 %collective-permute-start = (f32[32,1,128]{2,0,1:T(8,128)S(1)}, f32[32,1,128]{2,0,1:T(8,128)S(1)}, u32[]{:S(2)}, u32[]{:S(2)}) collective-permute-start(f32[32,1,128]{2,0,1:T(8,128)S(1)} %bitcast.50), channel_id=1, source_target_pairs={{8,0},{16,8},{24,16},{32,24},{40,32},{48,40},{56,48},{64,56},{72,6... | collective-permute-start | bytes 49160 | tf_op jit(solution)/shard_map/ppermute | solution.py:17
  15.5 1.4 collective-permute-done
  17.0 5.3 %collective-permute-done.1 = f32[32,1,128]{2,0,1:T(8,128)S(1)} collective-permute-done((f32[32,1,128]{2,0,1:T(8,128)S(1)}, f32[32,1,128]{2,0,1:T(8,128)S(1)}, u32[]{:S(2)}, u32[]{:S(2)}) %collective-permute-start.1) | collective-permute-done | bytes 16416 | tf_op jit(solution)/shard_map/ppermute | solution.py:16
  22.3 1.3 pad_maximum_fusion.2
  23.6 1.4 fusion.54
  25.1 1.7 copy.61
  28.0 3.4 %collective-permute-start.3 = (f32[32,66,1]{1,0,2:T(8,128)S(1)}, f32[32,66,1]{1,0,2:T(8,128)S(1)}, u32[]{:S(2)}, u32[]{:S(2)}) collective-permute-start(f32[32,66,1]{1,0,2:T(8,128)S(1)} %copy.63), channel_id=1, source_target_pairs={{0,1},{1,2},{2,3},{3,4},{4,5},{5,6},{6,7},{7,0},{8,9},{9,10},{10,1... | collective-permute-start | bytes 25352 | tf_op jit(solution)/shard_map/ppermute | solution.py:16
  32.6 1.5 copy.62
  34.2 1.5 copy.64
  35.7 5.3 %fusion.7 = (f32[1,32,64,128]{3,2,1,0:T(8,128)S(1)}, f32[1,32,64,128]{3,2,1,0:T(8,128)S(1)}) fusion(f32[32,64,128]{2,1,0:T(8,128)} %param.10, f32[32,66,1]{2,1,0:T(8,128)} %copy.64, f32[32,1,128]{2,1,0:T(1,128)S(1)} %bitcast.44, f32[32,1,128]{2,1,0:T(1,128)S(1)} %bitcast.46, f32[32,66,1]{2,1,0:T(8,128)} %copy.62, f32[32,64,128]{2,1,0:T(8,128)} %param.11), kind=kLoop, calls=%fused_computation.20 | loop fusion | flops 5505024 | bytes 4243968 | tf_op jit(solution)/shard_map/stack | solution.py:91
  41.2 5.3 %collective-permute-start.5 = (f32[2,32,1,128]{3,1,2,0:T(8,128)S(1)}, f32[2,32,1,128]{3,1,2,0:T(8,128)S(1)}, u32[]{:S(2)}, u32[]{:S(2)}) collective-permute-start(f32[2,32,1,128]{3,1,2,0:T(8,128)S(1)} %bitcast.47), channel_id=1, source_target_pairs={{8,0},{16,8},{24,16},{32,24},{40,32},{48,40},{56,48},{64,56},{72,6... | collective-permute-start | bytes 98312 | tf_op jit(solution)/shard_map/ppermute | solution.py:17
  46.5 1.6 collective-permute-done.4
  48.5 2.9 %fusion.53 = (f32[2,32,66,1]{3,2,1,0:T(8,128)}, f32[2,32,66,1]{3,2,1,0:T(8,128)}) fusion(f32[2,32,66,128]{3,2,1,0:T(8,128)S(1)} %pad_maximum_fusion.1), kind=kLoop, calls=%fused_computation.90 | loop fusion | bytes 67584 | tf_op jit(solution)/shard_map/slice | solution.py:14
  51.4 2.4 %copy.69 = f32[2,32,66,1]{2,1,3,0:T(8,128)S(1)} copy(f32[2,32,66,1]{3,2,1,0:T(8,128)} %get-tuple-element.11) | data formatting | bytes 33792 | tf_op jit(solution)/shard_map/slice | solution.py:14
  53.8 3.2 %collective-permute-start.6 = (f32[2,32,66,1]{2,1,3,0:T(8,128)S(1)}, f32[2,32,66,1]{2,1,3,0:T(8,128)S(1)}, u32[]{:S(2)}, u32[]{:S(2)}) collective-permute-start(f32[2,32,66,1]{2,1,3,0:T(8,128)S(1)} %copy.69), channel_id=1, source_target_pairs={{0,1},{1,2},{2,3},{3,4},{4,5},{5,6},{6,7},{7,0},{8,9},{9,10},{10,1... | collective-permute-start | bytes 50696 | tf_op jit(solution)/shard_map/ppermute | solution.py:16
  57.0 2.4 %copy.70 = f32[2,32,66,1]{2,1,3,0:T(8,128)S(1)} copy(f32[2,32,66,1]{3,2,1,0:T(8,128)} %get-tuple-element.12) | data formatting | bytes 33792 | tf_op jit(solution)/shard_map/slice | solution.py:15
  59.7 2.3 %copy.71 = f32[2,32,66,1]{3,2,1,0:T(8,128)} copy(f32[2,32,66,1]{2,1,3,0:T(8,128)S(1)} %collective-permute-done.6) | data formatting | bytes 33792 | tf_op jit(solution)/shard_map/ppermute | solution.py:16
  62.0 3.7 %collective-permute-done.7 = f32[2,32,66,1]{2,1,3,0:T(8,128)S(1)} collective-permute-done((f32[2,32,66,1]{2,1,3,0:T(8,128)S(1)}, f32[2,32,66,1]{2,1,3,0:T(8,128)S(1)}, u32[]{:S(2)}, u32[]{:S(2)}) %collective-permute-start.7) | collective-permute-done | bytes 16928 | tf_op jit(solution)/shard_map/ppermute | solution.py:17
  65.7 2.3 %copy.72 = f32[2,32,66,1]{3,2,1,0:T(8,128)} copy(f32[2,32,66,1]{2,1,3,0:T(8,128)S(1)} %collective-permute-done.7) | data formatting | bytes 33792 | tf_op jit(solution)/shard_map/ppermute | solution.py:17
  68.0 5.2 %pad_maximum_fusion = f32[2,32,66,130]{3,2,1,0:T(8,128)S(1)} fusion(f32[2,32,66,1]{3,2,1,0:T(8,128)} %copy.72, f32[2,32,1,128]{3,2,1,0:T(1,128)S(1)} %bitcast.42, f32[1,32,64,128]{3,2,1,0:T(8,128)} %copy-done.1, f32[1,32,64,128]{3,2,1,0:T(8,128)S(1)} %get-tuple-element.21, f32[2,32,1,128]{3,2,1,0:T(1,128)S(1)} %bitcast.40, f32[2,32,66,1]{3,2,1,0:T(8,128)} %copy.71), kind=kLoop, calls=%fused_computation.2 | loop fusion | flops 2745600 | bytes 4392960 | tf_op jit(solution)/shard_map/concatenate | solution.py:18
  74.4 5.3 %convolution_bitcast_fusion.1 = f32[32,64,128]{2,1,0:T(8,128)} fusion(f32[32,64,64]{2,1,0:T(8,128)} %param.12, f32[32,64,128]{2,1,0:T(8,128)S(1)} %copy-done.2, f32[32,66,130]{2,1,0:T(8,128)S(1)} %get-tuple-element.10, f32[32,66,130]{2,1,0:T(8,128)S(1)} %get-tuple-element.9), kind=kOutput, calls=%fused_computation.14 | convolution fusion | flops 206831616 | bytes 13107200 | tf_op jit(solution)/shard_map/zij,zjn->zin/dot_general | solution.py:59
  81.6 1.6 gather_fusion
  83.2 1.7 gather_fusion.1
  84.9 74.2 %all-gather.2.cloned.1.call-done = f32[32,128,128]{2,0,1:T(8,128)} async-done(((f32[32,4,128]{2,0,1:T(8,128)}), f32[32,128,128]{2,0,1:T(8,128)}) %all-gather.2.cloned.1.call-update) | async-done | bytes 2097168 | tf_op jit(solution)/shard_map/all_gather | solution.py:63
  159.1 4.4 %fusion = f32[32,4,128]{2,1,0:T(4,128)S(1)} fusion(f32[32,128,128]{2,0,1:T(8,128)} %all-gather.2.cloned.1.call-done, f32[4,32,128]{2,0,1:T(4,128)S(1)} %gather_fusion, pred[4]{0:T(512)(128)(4,1)S(1)} %get-tuple-element.25), kind=kOutput, calls=%fused_computation.6 | convolution fusion | flops 25182208 | bytes 2228228 | tf_op jit(solution)/shard_map/zrk,zkn->zrn/dot_general | solution.py:67
  163.4 1.8 fusion.2
  165.3 4.1 %fusion.58 = f32[32,64,128]{2,1,0:T(8,128)S(1)} fusion(f32[32,64,128]{2,1,0:T(8,128)S(1)} %fusion.2, f32[32,128,128]{2,1,0:T(8,128)S(1)} %copy-done), kind=kOutput, calls=%fused_computation.95 | convolution fusion | flops 402653184 | bytes 4194304 | tf_op jit(solution)/shard_map/zij,zxj->zxi/dot_general | solution.py:73
  169.4 1.7 fusion.55
  171.2 1.6 copy.75
  172.8 1.6 copy.76
  174.4 29.4 %all_gather.7 = f32[32,32,64]{2,0,1:T(8,128)S(1)} all-gather(f32[32,4,64]{2,0,1:T(8,128)S(1)} %maximum_bitcast_fusion), channel_id=1, replica_groups=mesh['gx'=32,'gy'=8] {'gy'}, dimensions={1}, use_global_device_ids=true | all-gather | bytes 294912 | tf_op jit(solution)/shard_map/all_gather | solution.py:77
  204.6 2.8 %convolution_subtract_fusion = f32[32,64,128]{2,1,0:T(8,128)} fusion(f32[32,64,128]{2,1,0:T(8,128)S(1)} %fusion.58, f32[32,4,64]{2,1,0:T(4,128)S(1)} %fusion.35, f32[32,128,4]{1,2,0:T(4,128)S(1)} %copy-done.5), kind=kOutput, calls=%fused_computation.11 | convolution fusion | flops 12845056 | bytes 2195456 | tf_op jit(solution)/shard_map/zik,zkx->zxi/dot_general | solution.py:84
  (37 shorter events, 8.2 us)
Async XLA Ops:
  6.5 158.7 %copy-start = (f32[32,128,128]{2,1,0:T(8,128)S(1)}, f32[32,128,128]{2,1,0:T(8,128)}, u32[]{:S(2)}) copy-start(f32[32,128,128]{2,1,0:T(8,128)} %param.15) | copy-start | bytes 6291460
  6.5 152.5 %all-gather.2.cloned.1.call-start = ((), (), s32[]{:S(2)}) async-start(), calls=%async_computation | async-start | bytes 2162688 | tf_op jit(solution)/shard_map/all_gather | solution.py:63
  7.7 9.3 %collective-permute-start = (f32[32,1,128]{2,0,1:T(8,128)S(1)}, f32[32,1,128]{2,0,1:T(8,128)S(1)}, u32[]{:S(2)}, u32[]{:S(2)}) collective-permute-start(f32[32,1,128]{2,0,1:T(8,128)S(1)} %bitcast.50), channel_id=1, source_target_pairs={{8,0},{16,8},{24,16},{32,24},{40,32},{48,40},{56,48},{64,56},{72,6... | collective-permute-start | bytes 49160 | tf_op jit(solution)/shard_map/ppermute | solution.py:17
  15.5 6.8 %collective-permute-start.1 = (f32[32,1,128]{2,0,1:T(8,128)S(1)}, f32[32,1,128]{2,0,1:T(8,128)S(1)}, u32[]{:S(2)}, u32[]{:S(2)}) collective-permute-start(f32[32,1,128]{2,0,1:T(8,128)S(1)} %bitcast.49), channel_id=1, source_target_pairs={{0,8},{8,16},{16,24},{24,32},{32,40},{40,48},{48,56},{56,64},{64,7... | collective-permute-start | bytes 49160 | tf_op jit(solution)/shard_map/ppermute | solution.py:16
  26.7 5.9 %collective-permute-start.2 = (f32[32,66,1]{1,0,2:T(8,128)S(1)}, f32[32,66,1]{1,0,2:T(8,128)S(1)}, u32[]{:S(2)}, u32[]{:S(2)}) collective-permute-start(f32[32,66,1]{1,0,2:T(8,128)S(1)} %copy.61), channel_id=1, source_target_pairs={{1,0},{2,1},{3,2},{4,3},{5,4},{6,5},{7,6},{0,7},{9,8},{10,9},{11,1... | collective-permute-start | bytes 25352 | tf_op jit(solution)/shard_map/ppermute | solution.py:17
  28.0 6.2 %collective-permute-start.3 = (f32[32,66,1]{1,0,2:T(8,128)S(1)}, f32[32,66,1]{1,0,2:T(8,128)S(1)}, u32[]{:S(2)}, u32[]{:S(2)}) collective-permute-start(f32[32,66,1]{1,0,2:T(8,128)S(1)} %copy.63), channel_id=1, source_target_pairs={{0,1},{1,2},{2,3},{3,4},{4,5},{5,6},{6,7},{7,0},{8,9},{9,10},{10,1... | collective-permute-start | bytes 25352 | tf_op jit(solution)/shard_map/ppermute | solution.py:16
  41.0 7.5 %copy-start.1 = (f32[1,32,64,128]{3,2,1,0:T(8,128)}, f32[1,32,64,128]{3,2,1,0:T(8,128)S(1)}, u32[]{:S(2)}) copy-start(f32[1,32,64,128]{3,2,1,0:T(8,128)S(1)} %get-tuple-element.22) | copy-start | bytes 3145732
  41.1 7.0 %collective-permute-start.4 = (f32[2,32,1,128]{3,1,2,0:T(8,128)S(1)}, f32[2,32,1,128]{3,1,2,0:T(8,128)S(1)}, u32[]{:S(2)}, u32[]{:S(2)}) collective-permute-start(f32[2,32,1,128]{3,1,2,0:T(8,128)S(1)} %bitcast.48), channel_id=1, source_target_pairs={{0,8},{8,16},{16,24},{24,32},{32,40},{40,48},{48,56},{56,64},{64,7... | collective-permute-start | bytes 98312 | tf_op jit(solution)/shard_map/ppermute | solution.py:16
  41.2 6.9 %collective-permute-start.5 = (f32[2,32,1,128]{3,1,2,0:T(8,128)S(1)}, f32[2,32,1,128]{3,1,2,0:T(8,128)S(1)}, u32[]{:S(2)}, u32[]{:S(2)}) collective-permute-start(f32[2,32,1,128]{3,1,2,0:T(8,128)S(1)} %bitcast.47), channel_id=1, source_target_pairs={{8,0},{16,8},{24,16},{32,24},{40,32},{48,40},{56,48},{64,56},{72,6... | collective-permute-start | bytes 98312 | tf_op jit(solution)/shard_map/ppermute | solution.py:17
  53.8 5.9 %collective-permute-start.6 = (f32[2,32,66,1]{2,1,3,0:T(8,128)S(1)}, f32[2,32,66,1]{2,1,3,0:T(8,128)S(1)}, u32[]{:S(2)}, u32[]{:S(2)}) collective-permute-start(f32[2,32,66,1]{2,1,3,0:T(8,128)S(1)} %copy.69), channel_id=1, source_target_pairs={{0,1},{1,2},{2,3},{3,4},{4,5},{5,6},{6,7},{7,0},{8,9},{9,10},{10,1... | collective-permute-start | bytes 50696 | tf_op jit(solution)/shard_map/ppermute | solution.py:16
  59.4 6.3 %collective-permute-start.7 = (f32[2,32,66,1]{2,1,3,0:T(8,128)S(1)}, f32[2,32,66,1]{2,1,3,0:T(8,128)S(1)}, u32[]{:S(2)}, u32[]{:S(2)}) collective-permute-start(f32[2,32,66,1]{2,1,3,0:T(8,128)S(1)} %copy.70), channel_id=1, source_target_pairs={{1,0},{2,1},{3,2},{4,3},{5,4},{6,5},{7,6},{0,7},{9,8},{10,9},{11,1... | collective-permute-start | bytes 50696 | tf_op jit(solution)/shard_map/ppermute | solution.py:17
  73.2 1.2 copy-start.2
  74.4 7.1 %copy-start.6 = (s32[4]{0:T(128)S(1)}, s32[4]{0:T(128)}, u32[]{:S(2)}) copy-start(s32[4]{0:T(128)} %constant.74.clone) | copy-start | bytes 52
  79.7 83.7 %copy-start.3 = (f32[32,64,128]{2,1,0:T(8,128)S(1)}, f32[32,64,128]{2,1,0:T(8,128)}, u32[]{:S(2)}) copy-start(f32[32,64,128]{2,1,0:T(8,128)} %convolution_bitcast_fusion.1) | copy-start | bytes 3145732
  79.7 83.7 %copy-start.4 = (f32[32,64,4]{1,2,0:T(4,128)S(1)}, f32[32,64,4]{1,2,0:T(4,128)}, u32[]{:S(2)}) copy-start(f32[32,64,4]{1,2,0:T(4,128)} %param.13) | copy-start | bytes 98308
  171.2 33.5 %copy-start.5 = (f32[32,128,4]{1,2,0:T(4,128)S(1)}, f32[32,128,4]{1,2,0:T(4,128)}, u32[]{:S(2)}) copy-start(f32[32,128,4]{1,2,0:T(4,128)} %param.16) | copy-start | bytes 196612
Sparse Core Ops, SparseCore 0:
  81.7 77.3 all-gather.1
where the time goes:
time: 215 us; the launch traced here: 214 us
  waiting for transfers between devices  87.5 us (41%)
  local copies, waits for them, and re-layouts  31.3 us (15%)
  blocking collectives  29.4 us (14%)
  starting transfers between devices  20.9 us (10%)
  matrix products  19.3 us (9%)
  between operations  13.6 us (6%)
  other arithmetic  12.3 us (6%)
    all_gather x1, waiting for transfers between devices, solve_x(): gathered = lax.all_gather(rims, 'gx', axis=1, tiled=True)  74.2 us
    all_gather x1, blocking collectives, solve_y(): gathered = lax.all_gather(rims, 'gy', axis=1, tiled=True)  29.4 us
    ppermute x4, starting transfers between devices, extended_2(): after = lax.ppermute(leading, axis, down)  14.2 us
    ppermute x4, waiting for transfers between devices, extended_2(): before = lax.ppermute(last, axis, up)  6.93 us
    slice x4, local copies, waits for them, and re-layouts, extended_2(): last = lax.slice_in_dim(shard, length - width, length, axis=dim)  6.9 us
    concatenate x3, other arithmetic, extended_2(): shard = jnp.concatenate([before, shard, after], axis=dim)  6.88 us
    ppermute x4, starting transfers between devices, extended_2(): before = lax.ppermute(last, axis, up)  6.69 us
    ppermute x4, waiting for transfers between devices, extended_2(): after = lax.ppermute(leading, axis, down)  6.4 us
  transfers between devices with their start and end apart: 9, of which 6 were waited for; matrix products, arithmetic and copies ran while one was open for 5% of the time, Pallas kernels for 0%

commit v1 on v0

v1 whole, which is shorter than its diff:
```python
import jax
import jax.numpy as jnp
from jax import lax
from jax.experimental import pallas as pl
from jax.experimental.pallas import tpu as pltpu
from jax.sharding import PartitionSpec as P

NZ, CX, CY = 32, 64, 128
STEP = 4
F32, BF16 = jnp.float32, jnp.bfloat16
CALL = pltpu.CompilerParams(vmem_limit_bytes=48 * 1024 * 1024)


def halves(a):
    hi = a.astype(BF16)
    return hi, (a - hi.astype(F32)).astype(BF16)


def dot3(a, b, dims):
    ah, al = halves(a)
    bh, bl = halves(b)
    one = lambda x, y: lax.dot_general(x, y, (dims, ((), ())), preferred_element_type=F32)
    return one(ah, bh) + (one(ah, bl) + one(al, bh))


def iota(shape, axis):
    return lax.broadcasted_iota(jnp.int32, shape, axis)


def roll(a, shift, axis):
    if isinstance(shift, int) and shift % a.shape[axis] == 0:
        return a
    if isinstance(shift, int):
        shift = shift % a.shape[axis]
    return pltpu.roll(a, shift, axis)


def potential(c, lap):
    return c * c * c - c - lap


def mobile(prefactor, c):
    sq = c * c
    return prefactor * (0.25 + sq) / (1.0 + sq)


def pack_kernel(c_ref, m_ref, ylo_ref, yhi_ref, xlo_ref, xhi_ref):
    lane = iota((CX, CY), 1)
    lo = jnp.zeros((CX, CY), F32)
    hi = jnp.zeros((CX, CY), F32)
    for z in range(NZ):
        c = roll(c_ref[z], 4 * z, 1)
        m = roll(m_ref[z], 4 * z + 2, 1)
        a, b = (4 * z - 2) % CY, 4 * z
        lo = jnp.where((lane >= b) & (lane <= b + 1), c, lo)
        lo = jnp.where(lane == b + 2, m, lo)
        hi = jnp.where((lane >= a) & (lane <= a + 1), c, hi)
        hi = jnp.where(lane == b + 1, m, hi)
    ylo_ref[...] = lo
    yhi_ref[...] = hi
    xlo_ref[0:32] = c_ref[:, 0, :]
    xlo_ref[32:64] = c_ref[:, 1, :]
    xlo_ref[64:96] = m_ref[:, 0, :]
    xhi_ref[0:32] = c_ref[:, CX - 1, :]
    xhi_ref[32:64] = c_ref[:, CX - 2, :]
    xhi_ref[64:96] = m_ref[:, CX - 1, :]


def lines_kernel(c_ref, m_ref, bx_ref, own_lo, own_hi, ylo_ref, yhi_ref, yl_ref, yr_ref,
                 xl_ref, xr_ref, lin_ref, rim_ref, ch, fh, mul, mobl, mur, mobr):
    row = iota((CX, CY), 0)
    lane = iota((CX, CY), 1)
    pid = pl.program_id(0)

    @pl.when(pid == 0)
    def _():
        lo, hi, left, right = ylo_ref[...], yhi_ref[...], yl_ref[...], yr_ref[...]

        def around(a, k):
            up = jnp.where(row == 0, xl_ref[96 + k:97 + k], roll(a, 1, 0))
            down = jnp.where(row == CX - 1, xr_ref[96 + k:97 + k], roll(a, -1, 0))
            return up + down

        c0, c1, m0 = lo, roll(lo, -1, 1), roll(lo, -2, 1)
        cm1, cm2, mm1 = roll(left, 1, 1), roll(left, 2, 1), roll(left, -1, 1)
        mu0 = potential(c0, cm1 + c1 + around(lo, 0) - 4.0 * c0)
        mum1 = potential(cm1, cm2 + c0 + roll(around(left, 2), 1, 1) - 4.0 * cm1)
        flux_l = 0.5 * (mobile(mm1, cm1) + mobile(m0, c0)) * (mu0 - mum1)
        cn, cn1, mn = hi, roll(hi, 1, 1), roll(hi, -2, 1)
        cp, cp2, mp = roll(right, -1, 1), roll(right, -2, 1), roll(right, -3, 1)
        mun = potential(cn, cn1 + cp + around(hi, 1) - 4.0 * cn)
        mup = potential(cp, cn + cp2 + roll(around(right, 3), -1, 1) - 4.0 * cp)
        flux_r = 0.5 * (mobile(mp, cp) + mobile(mn, cn)) * (mup - mun)
        first = (lane & 3) == 0
        fh[...] = jnp.where(first, flux_l, flux_r)
        ch[...] = jnp.where(first, cm1, cp)

        sub, ln = iota((NZ, CY), 0), iota((NZ, CY), 1)

        def halo_row(x_ref, own, mu_out, mob_out):
            a = x_ref[0:32]
            west = jnp.sum(jnp.where(ln == ((4 * sub - 1) & 127), x_ref[98:99], 0.0), axis=1, keepdims=True)
            east = jnp.sum(jnp.where(ln == 4 * sub, x_ref[99:100], 0.0), axis=1, keepdims=True)
            lf = jnp.where(ln == 0, west, roll(a, 1, 1))
            rt = jnp.where(ln == CY - 1, east, roll(a, -1, 1))
            mu_out[...] = potential(a, x_ref[32:64] + own[0:32] + lf + rt - 4.0 * a)
            mob_out[...] = mobile(x_ref[64:96], a)

        halo_row(xl_ref, own_lo, mul, mobl)
        halo_row(xr_ref, own_hi, mur, mobr)

    for i in range(STEP):
        z = pid * STEP + i
        at = pl.ds(z, 1)
        turn = (CY - 4 * z) & (CY - 1)
        c = c_ref[i]
        hz = roll(ch[...], turn, 1)
        fz = roll(fh[...], turn, 1)
        up = jnp.where(row == 0, xl_ref[at], roll(c, 1, 0))
        down = jnp.where(row == CX - 1, xr_ref[at], roll(c, -1, 0))
        lf = jnp.where(lane == 0, hz, roll(c, 1, 1))
        rt = jnp.where(lane == CY - 1, hz, roll(c, -1, 1))
        mu = potential(c, up + down + lf + rt - 4.0 * c)
        mob = mobile(m_ref[i], c)
        mu_d = jnp.where(row == CX - 1, mur[at], roll(mu, -1, 0))
        mob_d = jnp.where(row == CX - 1, mobr[at], roll(mob, -1, 0))
        fx = 0.5 * (mob_d + mob) * (mu_d - mu)
        f0 = 0.5 * (mob[0:1] + mobl[at]) * (mu[0:1] - mul[at])
        fx_up = jnp.where(row == 0, f0, roll(fx, 1, 0))
        fy = 0.5 * (roll(mob, -1, 1) + mob) * (roll(mu, -1, 1) - mu)
        fy = jnp.where(lane == CY - 1, fz, fy)
        fy_lf = jnp.where(lane == 0, fz, roll(fy, 1, 1))
        rhs = c + 0.02 * ((fx - fx_up) + (fy - fy_lf))
        lin = dot3(bx_ref[i], rhs, ((1,), (0,)))
        lin_ref[i] = lin
        rim_ref[i, 0:2] = lin[0:2]
        rim_ref[i, 2:4] = lin[CX - 2:CX]


def reduced_kernel(r_ref, rim_ref, out_ref):
    r = r_ref[...]
    use = jnp.where((iota((4 * NZ, 4 * NZ), 0) & 3) < 2, roll(r, 2, 0), roll(r, -2, 0))
    out_ref[...] = dot3(use, rim_ref[...], ((1,), (0,)))


def middle_kernel(lin_ref, cx_ref, sx_ref, by_ref, y_ref, rim_ref):
    pid = pl.program_id(0)
    lane = iota((CX, CY), 1)

    @pl.when(pid == 0)
    def _():
        rim_ref[...] = jnp.zeros_like(rim_ref)

    acc = rim_ref[...]
    for i in range(STEP):
        z = pid * STEP + i
        v = lin_ref[i] - lax.dot_general(sx_ref[i], cx_ref[i], (((0,), (0,)), ((), ())),
                                         precision=lax.Precision.HIGHEST, preferred_element_type=F32)
        y = dot3(v, by_ref[i], ((1,), (1,)))
        y_ref[i] = y
        acc = jnp.where((lane >> 2) == z, roll(y, (4 * z + 2) & (CY - 1), 1), acc)
    rim_ref[...] = acc


def last_kernel(y_ref, g_ref, bd_ref, sy_ref, out_ref, cy):
    pid = pl.program_id(0)
    lane = iota((CX, CY), 1)

    @pl.when(pid == 0)
    def _():
        total = jnp.zeros((CX, CY), F32)
        for q in range(8):
            total = total + dot3(g_ref[q], bd_ref[q], ((1,), (0,)))
        cy[...] = total

    c = cy[...]
    for i in range(STEP):
        z = pid * STEP + i
        mine = jnp.where((lane >> 2) == z, c, 0.0)
        out_ref[i] = y_ref[i] - dot3(mine, sy_ref[...], ((1,), (0,)))


def planes(rows, cols):
    return pl.BlockSpec((STEP, rows, cols), lambda i: (i, 0, 0))


def whole(*shape):
    return pl.BlockSpec(shape, lambda i: (0,) * len(shape))


def shape(*dims):
    return jax.ShapeDtypeStruct(dims, F32)


def body(conc, mobility, block_x, spike_x, reduced_x, block_y, spike_y, reduced_y):
    nx, ny = lax.axis_size("gx"), lax.axis_size("gy")
    p, q = lax.axis_index("gx"), lax.axis_index("gy")
    ring = lambda n, s: [(i, (i + s) % n) for i in range(n)]
    grid = (NZ // STEP,)

    ylo, yhi, xlo, xhi = pl.pallas_call(
        pack_kernel,
        out_shape=(shape(CX, CY), shape(CX, CY), shape(96, CY), shape(96, CY)),
        compiler_params=CALL,
        name="pack",
    )(conc, mobility)
    yl = lax.ppermute(yhi, "gy", ring(ny, 1))
    yr = lax.ppermute(ylo, "gy", ring(ny, -1))
    pad = jnp.zeros((4, CY), F32)
    send_lo = jnp.concatenate([xlo, ylo[:1], yhi[:1], yl[:1], yr[:1], pad])
    send_hi = jnp.concatenate([xhi, ylo[-1:], yhi[-1:], yl[-1:], yr[-1:], pad])
    xl = lax.ppermute(send_hi, "gx", ring(nx, 1))
    xr = lax.ppermute(send_lo, "gx", ring(nx, -1))

    lin, rims = pl.pallas_call(
        lines_kernel,
        grid=grid,
        in_specs=[planes(CX, CY), planes(CX, CY), planes(CX, CX), whole(96, CY), whole(96, CY),
                  whole(CX, CY), whole(CX, CY), whole(CX, CY), whole(CX, CY), whole(104, CY), whole(104, CY)],
        out_specs=(planes(CX, CY), planes(4, CY)),
        out_shape=(shape(NZ, CX, CY), shape(NZ, 4, CY)),
        scratch_shapes=[pltpu.VMEM((CX, CY), F32)] * 2 + [pltpu.VMEM((NZ, CY), F32)] * 4,
        compiler_params=CALL,
        name="lines",
    )(conc, mobility, block_x, xlo, xhi, ylo, yhi, yl, yr, xl, xr)

    mine = lax.dynamic_index_in_dim(reduced_x, p, 0, keepdims=False)
    rims = lax.all_to_all(rims, "gx", 0, 0, tiled=True)
    solved = pl.pallas_call(
        reduced_kernel, out_shape=shape(4 * NZ, CY), compiler_params=CALL, name="reduced"
    )(mine, rims.reshape(4 * NZ, CY))
    cx = lax.all_to_all(solved.reshape(NZ, 4, CY), "gx", 0, 0, tiled=True)

    ylin, yrim = pl.pallas_call(
        middle_kernel,
        grid=grid,
        in_specs=[planes(CX, CY), planes(4, CY), planes(4, CX), planes(CY, CY)],
        out_specs=(planes(CX, CY), whole(CX, CY)),
        out_shape=(shape(NZ, CX, CY), shape(CX, CY)),
        compiler_params=CALL,
        name="middle",
    )(lin, cx, jnp.transpose(spike_x, (0, 2, 1)), block_y)

    picks = (4 * q + jnp.array([-2, -1, 4, 5], jnp.int32)) % (4 * ny)
    rows = jnp.take(reduced_y, picks, axis=1).reshape(NZ, 4, ny, 4)
    rows = jnp.roll(rows, 2, axis=3)
    blocks = jnp.transpose(rows, (2, 0, 3, 1))[:, :, :, None, :]
    same = jnp.eye(NZ, dtype=F32)[None, :, None, :, None]
    diag = (blocks * same).reshape(ny, 4 * NZ, 4 * NZ)

    yall = lax.all_to_all(jnp.broadcast_to(yrim[None], (ny, CX, CY)), "gy", 0, 0, tiled=True)
    return pl.pallas_call(
        last_kernel,
        grid=grid,
        in_specs=[planes(CX, CY), whole(ny, CX, CY), whole(ny, CY, CY), whole(4 * NZ, CY)],
        out_specs=planes(CX, CY),
        out_shape=shape(NZ, CX, CY),
        scratch_shapes=[pltpu.VMEM((CX, CY), F32)],
        compiler_params=CALL,
        name="last",
    )(ylin, yall, diag, jnp.transpose(spike_y, (0, 2, 1)).reshape(4 * NZ, CY))


def solution(mesh):
    in_specs = (
        P(None, "gx", "gy"),
        P(None, "gx", "gy"),
        P(None, "gx", None),
        P(None, "gx", None),
        P(),
        P(None, "gy", None),
        P(None, "gy", None),
        P(),
    )
    out_specs = P(None, "gx", "gy")
    return jax.shard_map(body, mesh=mesh, in_specs=in_specs, out_specs=out_specs, check_vma=False)
```

time: 215 us -> 99.5 us (0.46)
  the two profiles are of different devices: /device:TPU:24 before, /device:TPU:1 now
where the time goes in v1:
time: 99.5 us; the launch traced here: 97.6 us
  local copies, waits for them, and re-layouts  32.5 us (33%)
  starting transfers between devices  26.5 us (27%)
  waiting for transfers between devices  19.6 us (20%)
  Pallas kernels  17 us (17%)
  other arithmetic  1.85 us (2%)
    mul x4, local copies, waits for them, and re-layouts, body(): diag = (blocks * same).reshape(ny, 4 * NZ, 4 * NZ)  15.1 us
    all_to_all x1, starting transfers between devices, body(): rims = lax.all_to_all(rims, 'gx', 0, 0, tiled=True)  9.94 us
    all_to_all x1, waiting for transfers between devices, body(): rims = lax.all_to_all(rims, 'gx', 0, 0, tiled=True)  9.85 us
    unnamed x30, local copies, waits for them, and re-layouts  9.83 us
    pallas_call x1, Pallas kernels, body(): pl.pallas_call(middle_kernel, grid=grid, in_specs=[planes(CX, CY), planes...  6.21 us
    pallas_call x1, Pallas kernels, body(): pl.pallas_call(lines_kernel, grid=grid, in_specs=[planes(CX, CY), planes(...  5.2 us
    all_to_all x1, waiting for transfers between devices, body(): lax.all_to_all(jnp.broadcast_to(yrim[None], (ny, CX, CY)), 'gy', 0, 0, ti...  5.12 us
    ppermute x1, starting transfers between devices, body(): yr = lax.ppermute(ylo, 'gy', ring(ny, -1))  4.57 us
  transfers between devices with their start and end apart: 7, of which 4 were waited for; matrix products, arithmetic and copies ran while one was open for 24% of the time, Pallas kernels for 0%

profile of v1, /device:TPU:1, one launch (start us, length us, event | category | flops | bytes accessed | tf_op | source)
XLA Modules:
  0.0 97.6 jit_solution(117722890178755940)
XLA Ops:
  0.0 1.4 %copy-done.1 = f32[32,64,128]{2,1,0:T(8,128)S(1)} copy-done((f32[32,64,128]{2,1,0:T(8,128)S(1)}, f32[32,64,128]{2,1,0:T(8,128)}, u32[]{:S(2)}) %copy-start.1) | copy-done | bytes 1048600
  1.4 1.2 %copy-done.3 = f32[32,64,128]{2,1,0:T(8,128)S(1)} copy-done((f32[32,64,128]{2,1,0:T(8,128)S(1)}, f32[32,64,128]{2,1,0:T(8,128)}, u32[]{:S(2)}) %copy-start.3) | copy-done | bytes 1048600
  3.2 4.6 %collective-permute-start.1 = (f32[64,128]{1,0:T(8,128)S(1)}, f32[64,128]{1,0:T(8,128)S(1)}, u32[]{:S(2)}, u32[]{:S(2)}) collective-permute-start(f32[64,128]{1,0:T(8,128)S(1)} %get-tuple-element.15.ylo_ref), channel_id=1, source_target_pairs={{0,7},{1,0},{2,1},{3,2},{4,3},{5,4},{6,5},{7,6},{8,15},{9,8},{10,9... | collective-permute-start | bytes 98312 | tf_op jit(solution)/shard_map/ppermute | solution.py:208
  8.4 2.1 %gather_fusion = f32[4,32,32]{2,0,1:T(4,128)} fusion(f32[32,32,32]{2,1,0:T(8,128)} %param.16, s32[1024]{0:T(1024)S(1)} %pad_clamp_fusion), kind=kCustom, calls=%fused_computation | custom fusion | bytes 32784 | tf_op jit(solution)/shard_map/jit(_take)/gather | solution.py:245
  10.6 0.9 copy.11
  12.0 0.7 collective-permute-done.yl_ref
  13.3 2.2 %collective-permute-start.3 = (f32[104,128]{1,0:T(8,128)S(1)}, f32[104,128]{1,0:T(8,128)S(1)}, u32[]{:S(2)}, u32[]{:S(2)}) collective-permute-start(f32[104,128]{1,0:T(8,128)S(1)} %concatenate.11), channel_id=1, source_target_pairs={{0,248},{8,0},{16,8},{24,16},{32,24},{40,32},{48,40},{56,48},{64,5... | collective-permute-start | bytes 159752 | tf_op jit(solution)/shard_map/ppermute | solution.py:213
  15.4 1.9 %concatenate.10 = f32[104,128]{1,0:T(8,128)} concatenate(f32[96,128]{1,0:T(8,128)S(1)} %get-tuple-element.14.own_hi, f32[1,128]{1,0:T(1,128)} %get-tuple-element.33, f32[1,128]{1,0:T(1,128)} %get-tuple-element.30, f32[1,128]{1,0:T(1,128)} %get-tuple-element.28, f32[1,128]{1,0:T(1,128)} %get-tuple-element.26, f32[4,128]{1,0:T(4,128)S(1)} %broadcast_in_dim.23), dimensions={0} | concatenate | bytes 106496 | tf_op jit(solution)/shard_map/concatenate | solution.py:211
  17.3 2.4 %collective-permute-start.2 = (f32[104,128]{1,0:T(8,128)}, f32[104,128]{1,0:T(8,128)S(1)}, u32[]{:S(2)}, u32[]{:S(2)}) collective-permute-start(f32[104,128]{1,0:T(8,128)} %concatenate.10), channel_id=1, source_target_pairs={{0,8},{8,16},{16,24},{24,32},{32,40},{40,48},{48,56},{56,64},{64,7... | collective-permute-start | bytes 159752 | tf_op jit(solution)/shard_map/ppermute | solution.py:212
  19.7 0.7 broadcast_select_fusion
  20.4 3.9 %collective-permute-done.2.xl_ref = f32[104,128]{1,0:T(8,128)S(1)} collective-permute-done((f32[104,128]{1,0:T(8,128)}, f32[104,128]{1,0:T(8,128)S(1)}, u32[]{:S(2)}, u32[]{:S(2)}) %collective-permute-start.2) | collective-permute-done | bytes 53280 | tf_op jit(solution)/shard_map/ppermute | solution.py:212
  24.3 1.2 %copy-done.4 = f32[32,64,128]{2,1,0:T(8,128)S(1)} copy-done((f32[32,64,128]{2,1,0:T(8,128)S(1)}, f32[32,64,128]{2,1,0:T(8,128)}, u32[]{:S(2)}) %copy-start.4) | copy-done | bytes 1048600
  25.5 1.2 %copy-done.10 = f32[32,64,64]{2,1,0:T(8,128)S(1)} copy-done((f32[32,64,64]{2,1,0:T(8,128)S(1)}, f32[32,64,64]{2,1,0:T(8,128)}, u32[]{:S(2)}) %copy-start.10) | copy-done | bytes 524312
  26.8 5.2 %lines.1 = (f32[32,64,128]{2,1,0:T(8,128)S(1)}, f32[32,4,128]{2,1,0:T(4,128)}) custom-call(f32[32,64,128]{2,1,0:T(8,128)S(1)} %copy-done.2, f32[32,64,128]{2,1,0:T(8,128)S(1)} %copy-done.4, f32[32,64,64]{2,1,0:T(8,128)S(1)} %copy-done.10, f32[96,128]{1,0:T(8,128)S(1)} %get-tuple-element.13.own_lo, f32[96,128]{1,0:T(8,128)S(1)} %get-tuple-element.14.own_hi, ...), custom_call_target="tpu_custom_call" | custom-call | tf_op jit(solution)/shard_map/lines/pallas_call | solution.py:215
  32.0 1.0 copy-done.6
  32.9 9.9 %all-to-all-start = ((f32[32,4,128]{2,1,0:T(4,128)}), f32[32,4,128]{2,1,0:T(4,128)S(1)}, u32[]{:S(2)}, u32[]{:S(2)}) async-start(f32[32,4,128]{2,1,0:T(4,128)} %get-tuple-element.18), calls=%async_computation | async-start | bytes 131072 | tf_op jit(solution)/shard_map/all_to_all | solution.py:228
  43.0 9.9 %all-to-all-done = f32[32,4,128]{2,1,0:T(4,128)S(1)} async-done(((f32[32,4,128]{2,1,0:T(4,128)}), f32[32,4,128]{2,1,0:T(4,128)S(1)}, u32[]{:S(2)}, u32[]{:S(2)}) %all-to-all-start) | async-done | bytes 65568 | tf_op jit(solution)/shard_map/all_to_all | solution.py:228
  52.8 0.8 reduced.1
  53.6 3.9 %all-to-all-start.1 = ((f32[32,4,128]{2,1,0:T(4,128)}), f32[32,4,128]{2,1,0:T(4,128)S(1)}, u32[]{:S(2)}, u32[]{:S(2)}) async-start(f32[32,4,128]{2,1,0:T(4,128)} %bitcast.2), calls=%async_computation.1 | async-start | bytes 131072 | tf_op jit(solution)/shard_map/all_to_all | solution.py:232
  57.8 4.3 %mul.20 = f32[8,32,4,32,4]{0,4,3,2,1:T(4,128)} broadcast(f32[8,32,4,4]{0,3,2,1:T(4,128)S(1)} %copy.12), dimensions={0,1,2,4} | broadcast | bytes 540672 | tf_op jit(solution)/shard_map/mul | solution.py:249
  62.1 5.9 %copy.13 = f32[8,128,128]{2,1,0:T(8,128)} copy(f32[8,128,128]{0,2,1:T(8,128)} %bitcast.18) | data formatting | bytes 1048576 | tf_op jit(solution)/shard_map/mul | solution.py:249
  68.0 1.7 %mul.22 = f32[32,4,32,4]{3,2,1,0:T(8,128)} broadcast(f32[32,32]{1,0:T(8,128)S(1)} %fusion), dimensions={0,2} | broadcast | bytes 69632 | tf_op jit(solution)/shard_map/mul | solution.py:249
  69.7 3.2 %mul.23 = f32[128,128]{1,0:T(8,128)S(1)} reshape(f32[32,4,32,4]{3,2,1,0:T(8,128)} %mul.22) | data formatting | bytes 131072 | tf_op jit(solution)/shard_map/mul | solution.py:249
  72.9 1.6 %copy-done.5 = f32[32,128,128]{2,1,0:T(8,128)S(1)} copy-done((f32[32,128,128]{2,1,0:T(8,128)S(1)}, f32[32,128,128]{2,1,0:T(8,128)}, u32[]{:S(2)}) %copy-start.5) | copy-done | bytes 2097176
  74.5 6.2 %middle.1 = (f32[32,64,128]{2,1,0:T(8,128)S(1)}, f32[64,128]{1,0:T(8,128)S(1)}) custom-call(f32[32,64,128]{2,1,0:T(8,128)S(1)} %copy-done.7, f32[32,4,128]{2,1,0:T(4,128)S(1)} %all-to-all-done.1.cx_ref, f32[32,4,64]{2,1,0:T(4,128)S(1)} %bitcast.16, f32[32,128,128]{2,1,0:T(8,128)S(1)} %copy-done.5), custom_call_target="tpu_custom_call" | custom-call | tf_op jit(solution)/shard_map/middle/pallas_call | solution.py:234
  80.7 1.0 copy-done.8
  81.7 0.7 broadcast_in_dim.24
  82.4 3.5 %all-to-all-start.2 = ((f32[8,64,128]{2,1,0:T(8,128)}), f32[8,64,128]{2,1,0:T(8,128)S(1)}, u32[]{:S(2)}, u32[]{:S(2)}) async-start(f32[8,64,128]{2,1,0:T(8,128)} %broadcast_in_dim.24), calls=%async_computation.2 | async-start | bytes 524288 | tf_op jit(solution)/shard_map/all_to_all | solution.py:251
  85.9 1.1 %broadcast_multiply_fusion.bd_ref = f32[8,128,128]{2,1,0:T(8,128)S(1)} fusion(f32[8,128,128]{2,1,0:T(8,128)} %copy.13, f32[128,128]{1,0:T(8,128)S(1)} %mul.23), kind=kLoop, calls=%fused_computation.1 | loop fusion | flops 131072 | bytes 1114112 | tf_op jit(solution)/shard_map/mul | solution.py:249
  87.0 5.1 %all-to-all-done.2.g_ref = f32[8,64,128]{2,1,0:T(8,128)S(1)} async-done(((f32[8,64,128]{2,1,0:T(8,128)}), f32[8,64,128]{2,1,0:T(8,128)S(1)}, u32[]{:S(2)}, u32[]{:S(2)}) %all-to-all-start.2) | async-done | bytes 262176 | tf_op jit(solution)/shard_map/all_to_all | solution.py:251
  92.1 1.2 %copy-done.9 = f32[32,64,128]{2,1,0:T(8,128)S(1)} copy-done((f32[32,64,128]{2,1,0:T(8,128)S(1)}, f32[32,64,128]{2,1,0:T(8,128)}, u32[]{:S(2)}) %copy-start.9) | copy-done | bytes 1048600
  93.4 4.2 %last.1 = f32[32,64,128]{2,1,0:T(8,128)} custom-call(f32[32,64,128]{2,1,0:T(8,128)S(1)} %copy-done.9, f32[8,64,128]{2,1,0:T(8,128)S(1)} %all-to-all-done.2.g_ref, f32[8,128,128]{2,1,0:T(8,128)S(1)} %broadcast_multiply_fusion.bd_ref, f32[128,128]{1,0:T(8,128)S(1)} %bitcast.17), custom_call_target="tpu_custom_call" | custom-call | tf_op jit(solution)/shard_map/last/pallas_call | solution.py:252
  (39 shorter events, 2.6 us)
Async XLA Ops:
  0.0 42.9 %copy-start = (f32[32,128,128]{2,1,0:T(8,128)S(1)}, f32[32,128,128]{2,1,0:T(8,128)}, u32[]{:S(2)}) copy-start(f32[32,128,128]{2,1,0:T(8,128)} %param.13) | copy-start | bytes 6291460
  0.0 8.4 %copy-start.14 = (s32[4]{0:T(128)S(1)}, s32[4]{0:T(128)}, u32[]{:S(2)}) copy-start(s32[4]{0:T(128)} %constant.47.clone) | copy-start | bytes 52
  0.0 1.4 %copy-start.1 = (f32[32,64,128]{2,1,0:T(8,128)S(1)}, f32[32,64,128]{2,1,0:T(8,128)}, u32[]{:S(2)}) copy-start(f32[32,64,128]{2,1,0:T(8,128)} %c_ref.3) | copy-start | bytes 3145732
  1.4 1.2 %copy-start.3 = (f32[32,64,128]{2,1,0:T(8,128)S(1)}, f32[32,64,128]{2,1,0:T(8,128)}, u32[]{:S(2)}) copy-start(f32[32,64,128]{2,1,0:T(8,128)} %m_ref.3) | copy-start | bytes 3145732
  2.6 21.7 %copy-start.2 = (f32[32,64,128]{2,1,0:T(8,128)S(1)}, f32[32,64,128]{2,1,0:T(8,128)}, u32[]{:S(2)}) copy-start(f32[32,64,128]{2,1,0:T(8,128)} %c_ref.3) | copy-start | bytes 3145732
  3.2 8.2 %collective-permute-start.1 = (f32[64,128]{1,0:T(8,128)S(1)}, f32[64,128]{1,0:T(8,128)S(1)}, u32[]{:S(2)}, u32[]{:S(2)}) collective-permute-start(f32[64,128]{1,0:T(8,128)S(1)} %get-tuple-element.15.ylo_ref), channel_id=1, source_target_pairs={{0,7},{1,0},{2,1},{3,2},{4,3},{5,4},{6,5},{7,6},{8,15},{9,8},{10,9... | collective-permute-start | bytes 98312 | tf_op jit(solution)/shard_map/ppermute | solution.py:208
  7.8 4.9 %collective-permute-start = (f32[64,128]{1,0:T(8,128)S(1)}, f32[64,128]{1,0:T(8,128)S(1)}, u32[]{:S(2)}, u32[]{:S(2)}) collective-permute-start(f32[64,128]{1,0:T(8,128)S(1)} %get-tuple-element.16.yhi_ref), channel_id=1, source_target_pairs={{0,1},{1,2},{2,3},{3,4},{4,5},{5,6},{6,7},{7,0},{8,9},{9,10},{10,1... | collective-permute-start | bytes 98312 | tf_op jit(solution)/shard_map/ppermute | solution.py:207
  13.3 7.1 %collective-permute-start.3 = (f32[104,128]{1,0:T(8,128)S(1)}, f32[104,128]{1,0:T(8,128)S(1)}, u32[]{:S(2)}, u32[]{:S(2)}) collective-permute-start(f32[104,128]{1,0:T(8,128)S(1)} %concatenate.11), channel_id=1, source_target_pairs={{0,248},{8,0},{16,8},{24,16},{32,24},{40,32},{48,40},{56,48},{64,5... | collective-permute-start | bytes 159752 | tf_op jit(solution)/shard_map/ppermute | solution.py:213
  17.3 7.0 %collective-permute-start.2 = (f32[104,128]{1,0:T(8,128)}, f32[104,128]{1,0:T(8,128)S(1)}, u32[]{:S(2)}, u32[]{:S(2)}) collective-permute-start(f32[104,128]{1,0:T(8,128)} %concatenate.10), channel_id=1, source_target_pairs={{0,8},{8,16},{16,24},{24,32},{32,40},{40,48},{48,56},{56,64},{64,7... | collective-permute-start | bytes 159752 | tf_op jit(solution)/shard_map/ppermute | solution.py:212
  24.3 1.2 %copy-start.4 = (f32[32,64,128]{2,1,0:T(8,128)S(1)}, f32[32,64,128]{2,1,0:T(8,128)}, u32[]{:S(2)}) copy-start(f32[32,64,128]{2,1,0:T(8,128)} %m_ref.3) | copy-start | bytes 3145732
  25.5 1.2 %copy-start.10 = (f32[32,64,64]{2,1,0:T(8,128)S(1)}, f32[32,64,64]{2,1,0:T(8,128)}, u32[]{:S(2)}) copy-start(f32[32,64,64]{2,1,0:T(8,128)} %bx_ref.1) | copy-start | bytes 1572868
  26.8 16.1 %copy-start.13 = (f32[32,4,8,4]{0,3,2,1:T(4,128)S(1)}, f32[32,4,8,4]{0,3,2,1:T(4,128)}, u32[]{:S(2)}) copy-start(f32[32,4,8,4]{0,3,2,1:T(4,128)} %broadcast_select_fusion) | copy-start | bytes 49156
  32.0 1.0 copy-start.6
  32.9 19.9 %all-to-all-start = ((f32[32,4,128]{2,1,0:T(4,128)}), f32[32,4,128]{2,1,0:T(4,128)S(1)}, u32[]{:S(2)}, u32[]{:S(2)}) async-start(f32[32,4,128]{2,1,0:T(4,128)} %get-tuple-element.18), calls=%async_computation | async-start | bytes 131072 | tf_op jit(solution)/shard_map/all_to_all | solution.py:228
  53.6 19.3 %all-to-all-start.1 = ((f32[32,4,128]{2,1,0:T(4,128)}), f32[32,4,128]{2,1,0:T(4,128)S(1)}, u32[]{:S(2)}, u32[]{:S(2)}) async-start(f32[32,4,128]{2,1,0:T(4,128)} %bitcast.2), calls=%async_computation.1 | async-start | bytes 131072 | tf_op jit(solution)/shard_map/all_to_all | solution.py:232
  68.0 4.9 %copy-start.7 = (f32[32,64,128]{2,1,0:T(8,128)S(1)}, f32[32,64,128]{2,1,0:T(8,128)}, u32[]{:S(2)}) copy-start(f32[32,64,128]{2,1,0:T(8,128)} %copy-done.6) | copy-start | bytes 3145732
  68.0 4.9 %copy-start.11 = (f32[32,64,4]{1,2,0:T(4,128)S(1)}, f32[32,64,4]{1,2,0:T(4,128)}, u32[]{:S(2)}) copy-start(f32[32,64,4]{1,2,0:T(4,128)} %param.12) | copy-start | bytes 98308
  72.9 1.6 %copy-start.5 = (f32[32,128,128]{2,1,0:T(8,128)S(1)}, f32[32,128,128]{2,1,0:T(8,128)}, u32[]{:S(2)}) copy-start(f32[32,128,128]{2,1,0:T(8,128)} %by_ref.1) | copy-start | bytes 6291460
  74.5 17.6 %copy-start.12 = (f32[32,128,4]{1,2,0:T(4,128)S(1)}, f32[32,128,4]{1,2,0:T(4,128)}, u32[]{:S(2)}) copy-start(f32[32,128,4]{1,2,0:T(4,128)} %param.15) | copy-start | bytes 196612
  80.7 1.0 copy-start.8
  82.4 9.7 %all-to-all-start.2 = ((f32[8,64,128]{2,1,0:T(8,128)}), f32[8,64,128]{2,1,0:T(8,128)S(1)}, u32[]{:S(2)}, u32[]{:S(2)}) async-start(f32[8,64,128]{2,1,0:T(8,128)} %broadcast_in_dim.24), calls=%async_computation.2 | async-start | bytes 524288 | tf_op jit(solution)/shard_map/all_to_all | solution.py:251
  92.1 1.2 %copy-start.9 = (f32[32,64,128]{2,1,0:T(8,128)S(1)}, f32[32,64,128]{2,1,0:T(8,128)}, u32[]{:S(2)}) copy-start(f32[32,64,128]{2,1,0:T(8,128)} %copy-done.8) | copy-start | bytes 3145732

commit v2 on v1

v2 whole, which is shorter than its diff:
```python
import jax
import jax.numpy as jnp
from jax import lax
from jax.experimental import pallas as pl
from jax.experimental.pallas import tpu as pltpu
from jax.sharding import PartitionSpec as P

NZ, CX, CY = 32, 64, 128
STEP = 4
F32, BF16 = jnp.float32, jnp.bfloat16
CALL = pltpu.CompilerParams(vmem_limit_bytes=12 * 1024 * 1024)


def halves(a):
    hi = a.astype(BF16)
    return hi, (a - hi.astype(F32)).astype(BF16)


def dot3(a, b, dims):
    ah, al = halves(a)
    bh, bl = halves(b)
    one = lambda x, y: lax.dot_general(x, y, (dims, ((), ())), preferred_element_type=F32)
    return one(ah, bh) + (one(ah, bl) + one(al, bh))


def iota(shape, axis):
    return lax.broadcasted_iota(jnp.int32, shape, axis)


def roll(a, shift, axis):
    if isinstance(shift, int) and shift % a.shape[axis] == 0:
        return a
    if isinstance(shift, int):
        shift = shift % a.shape[axis]
    return pltpu.roll(a, shift, axis)


def potential(c, lap):
    return c * c * c - c - lap


def mobile(prefactor, c):
    sq = c * c
    return prefactor * (0.25 + sq) / (1.0 + sq)


def edge_kernel(c_ref, m_ref, xlo_ref, xhi_ref, ct, cb, mt, mb, sems):
    top, bottom = pl.ds(0, 8), pl.ds(CX - 8, 8)
    copies = [
        pltpu.make_async_copy(c_ref.at[:, top, :], ct, sems.at[0]),
        pltpu.make_async_copy(m_ref.at[:, top, :], mt, sems.at[1]),
        pltpu.make_async_copy(c_ref.at[:, bottom, :], cb, sems.at[2]),
        pltpu.make_async_copy(m_ref.at[:, bottom, :], mb, sems.at[3]),
    ]
    for copy in copies:
        copy.start()
    for copy in copies:
        copy.wait()
    xlo_ref[0:32] = ct[:, 0, :]
    xlo_ref[32:64] = ct[:, 1, :]
    xlo_ref[64:96] = mt[:, 0, :]
    xhi_ref[0:32] = cb[:, 7, :]
    xhi_ref[32:64] = cb[:, 6, :]
    xhi_ref[64:96] = mb[:, 7, :]


def pack_kernel(c_ref, m_ref, ylo_ref, yhi_ref):
    lane = iota((CX, CY), 1)
    lo = jnp.zeros((CX, CY), F32)
    hi = jnp.zeros((CX, CY), F32)
    for z in range(NZ):
        c = roll(c_ref[z], 4 * z, 1)
        m = roll(m_ref[z], 4 * z + 2, 1)
        a, b = (4 * z - 2) % CY, 4 * z
        lo = jnp.where((lane >= b) & (lane <= b + 1), c, lo)
        lo = jnp.where(lane == b + 2, m, lo)
        hi = jnp.where((lane >= a) & (lane <= a + 1), c, hi)
        hi = jnp.where(lane == b + 1, m, hi)
    ylo_ref[...] = lo
    yhi_ref[...] = hi


def corner_kernel(lo_ref, hi_ref, xl_ref, xr_ref, slo_ref, shi_ref):
    sub, lane = iota((NZ, CY), 0), iota((NZ, CY), 1)

    def across(column, at):
        return jnp.sum(jnp.where(lane == at, column, 0.0), axis=0, keepdims=True)

    pad = jnp.zeros((6, CY), F32)
    up, down = xl_ref[0:NZ], xr_ref[0:NZ]
    first, last = 4 * sub, (4 * sub - 1) & (CY - 1)
    slo_ref[0:CX] = lo_ref[...]
    slo_ref[CX:72] = jnp.concatenate([across(up[:, :1], first), across(down[:, :1], first), pad])
    shi_ref[0:CX] = hi_ref[...]
    shi_ref[CX:72] = jnp.concatenate([across(up[:, CY - 1:], last), across(down[:, CY - 1:], last), pad])


def piece(src, dst, sems, g):
    at = pl.ds(g * STEP, STEP)
    return pltpu.make_async_copy(src.at[at], dst.at[at], sems.at[g])


def lines_kernel(c_hbm, m_hbm, bx_hbm, own_lo, own_hi, slo_ref, shi_ref, yl_ref, yr_ref,
                 xl_ref, xr_ref, lin_hbm, rim_ref, c_ref, m_ref, bx_ref, lin_ref, ch, fh, mul, mobl, mur, mobr, sems):
    row = iota((CX, CY), 0)
    lane = iota((CX, CY), 1)
    moves = ((c_hbm, c_ref), (m_hbm, m_ref), (bx_hbm, bx_ref), (lin_ref, lin_hbm))
    for g in range(NZ // STEP):
        for k in range(3):
            piece(*moves[k], sems.at[k], g).start()

    def edges():
        lo, hi, left, right = slo_ref[0:CX], shi_ref[0:CX], yl_ref[0:CX], yr_ref[0:CX]

        def around(a, ref):
            up = jnp.where(row == 0, ref[CX:CX + 1], roll(a, 1, 0))
            down = jnp.where(row == CX - 1, ref[CX + 1:CX + 2], roll(a, -1, 0))
            return up + down

        c0, c1, m0 = lo, roll(lo, -1, 1), roll(lo, -2, 1)
        cm1, cm2, mm1 = roll(left, 1, 1), roll(left, 2, 1), roll(left, -1, 1)
        mu0 = potential(c0, cm1 + c1 + around(lo, slo_ref) - 4.0 * c0)
        mum1 = potential(cm1, cm2 + c0 + roll(around(left, yl_ref), 1, 1) - 4.0 * cm1)
        flux_l = 0.5 * (mobile(mm1, cm1) + mobile(m0, c0)) * (mu0 - mum1)
        cn, cn1, mn = hi, roll(hi, 1, 1), roll(hi, -2, 1)
        cp, cp2, mp = roll(right, -1, 1), roll(right, -2, 1), roll(right, -3, 1)
        mun = potential(cn, cn1 + cp + around(hi, shi_ref) - 4.0 * cn)
        mup = potential(cp, cn + cp2 + roll(around(right, yr_ref), -1, 1) - 4.0 * cp)
        flux_r = 0.5 * (mobile(mp, cp) + mobile(mn, cn)) * (mup - mun)
        first = (lane & 3) == 0
        fh[...] = jnp.where(first, flux_l, flux_r)
        ch[...] = jnp.where(first, cm1, cp)

        sub, ln = iota((NZ, CY), 0), iota((NZ, CY), 1)

        def halo_row(x_ref, own, k, mu_out, mob_out):
            a = x_ref[0:32]
            west = jnp.where(ln == ((4 * sub - 1) & (CY - 1)), yl_ref[CX + k:CX + k + 1], 0.0)
            east = jnp.where(ln == 4 * sub, yr_ref[CX + k:CX + k + 1], 0.0)
            lf = jnp.where(ln == 0, jnp.sum(west, axis=1, keepdims=True), roll(a, 1, 1))
            rt = jnp.where(ln == CY - 1, jnp.sum(east, axis=1, keepdims=True), roll(a, -1, 1))
            mu_out[...] = potential(a, x_ref[32:64] + own[0:32] + lf + rt - 4.0 * a)
            mob_out[...] = mobile(x_ref[64:96], a)

        halo_row(xl_ref, own_lo, 0, mul, mobl)
        halo_row(xr_ref, own_hi, 1, mur, mobr)

    edges()

    def step(g, carry):
        for k in range(3):
            piece(*moves[k], sems.at[k], g).wait()
        for i in range(STEP):
            plane(g * STEP + i)
        piece(*moves[3], sems.at[3], g).start()
        return carry

    def plane(z):
        at = pl.ds(z, 1)
        turn = (CY - 4 * z) & (CY - 1)
        c = c_ref[z]
        hz = roll(ch[...], turn, 1)
        fz = roll(fh[...], turn, 1)
        up = jnp.where(row == 0, xl_ref[at], roll(c, 1, 0))
        down = jnp.where(row == CX - 1, xr_ref[at], roll(c, -1, 0))
        lf = jnp.where(lane == 0, hz, roll(c, 1, 1))
        rt = jnp.where(lane == CY - 1, hz, roll(c, -1, 1))
        mu = potential(c, up + down + lf + rt - 4.0 * c)
        mob = mobile(m_ref[z], c)
        mu_d = jnp.where(row == CX - 1, mur[at], roll(mu, -1, 0))
        mob_d = jnp.where(row == CX - 1, mobr[at], roll(mob, -1, 0))
        fx = 0.5 * (mob_d + mob) * (mu_d - mu)
        f0 = 0.5 * (mob[0:1] + mobl[at]) * (mu[0:1] - mul[at])
        fx_up = jnp.where(row == 0, f0, roll(fx, 1, 0))
        fy = 0.5 * (roll(mob, -1, 1) + mob) * (roll(mu, -1, 1) - mu)
        fy = jnp.where(lane == CY - 1, fz, fy)
        fy_lf = jnp.where(lane == 0, fz, roll(fy, 1, 1))
        rhs = c + 0.02 * ((fx - fx_up) + (fy - fy_lf))
        lin = dot3(bx_ref[z], rhs, ((1,), (0,)))
        lin_ref[z] = lin
        rim_ref[z, 0:2] = lin[0:2]
        rim_ref[z, 2:4] = lin[CX - 2:CX]

    lax.fori_loop(0, NZ // STEP, step, 0)
    for g in range(NZ // STEP):
        piece(*moves[3], sems.at[3], g).wait()


def reduced_kernel(r_ref, rim_ref, out_ref):
    r = r_ref[...]
    use = jnp.where((iota((4 * NZ, 4 * NZ), 0) & 3) < 2, roll(r, 2, 0), roll(r, -2, 0))
    out_ref[...] = dot3(use, rim_ref[...], ((1,), (0,)))


def wide_kernel(lin_ref, byr_ref, rim_ref):
    lane = iota((CX, CY), 1)
    acc = jnp.zeros((CX, CY), F32)
    for g in range(NZ // STEP):
        part = lin_ref[STEP * g:STEP * (g + 1)].reshape(STEP * CX, CY)
        out = dot3(part, byr_ref[...], ((1,), (1,)))
        for i in range(STEP):
            acc = jnp.where((lane >> 2) == STEP * g + i, out[CX * i:CX * (i + 1)], acc)
    rim_ref[...] = acc


def diag_kernel(y_ref, hi_ref, lo_ref):
    n = 4 * NZ
    yh, yl = halves(y_ref[...])
    same = (iota((n, n), 0) >> 2) == (iota((n, n), 1) >> 2)
    col, ln = iota((32, n), 0), iota((32, n), 1)
    for q in range(8):
        pick = jnp.where(col == 4 * q + ((ln + 2) & 3), 1.0, 0.0).astype(BF16)
        for a, ref in ((yh, hi_ref), (yl, lo_ref)):
            full = jnp.dot(a, pick, preferred_element_type=F32)
            ref[q] = jnp.where(same, full, 0.0).astype(BF16)


def rims_kernel(wrim_ref, cx_ref, byr_ref, sx_ref, out_ref):
    n = 4 * NZ
    same = (iota((n, n), 0) >> 2) == (iota((n, n), 1) >> 2)
    mixed = jnp.where(same, dot3(cx_ref[...], byr_ref[...], ((1,), (1,))), 0.0)
    v = wrim_ref[...] - dot3(sx_ref[...], mixed, ((0,), (0,)))
    for q in range(8):
        out_ref[q] = v


def spread(packed, g):
    lane = iota((CX, CY), 1)
    return jnp.concatenate([jnp.where((lane >> 2) == STEP * g + i, packed, 0.0) for i in range(STEP)])


def couple_kernel(lin_hbm, by_hbm, cx_ref, sx_ref, u_hbm, lin, by, u, spikes, sems):
    for g in range(NZ // STEP):
        piece(lin_hbm, lin, sems.at[0], g).start()
        piece(by_hbm, by, sems.at[1], g).start()
    spikes[...] = jnp.transpose(sx_ref[...])

    def step(g, carry):
        fix = dot3(spread(spikes[...], g), cx_ref[...], ((1,), (0,)))
        piece(lin_hbm, lin, sems.at[0], g).wait()
        piece(by_hbm, by, sems.at[1], g).wait()
        for i in range(STEP):
            z = STEP * g + i
            v = lin[z] - fix[CX * i:CX * (i + 1)]
            u[z] = dot3(v, by[z], ((1,), (1,)))
        piece(u, u_hbm, sems.at[2], g).start()
        return carry

    lax.fori_loop(0, NZ // STEP, step, 0)
    for g in range(NZ // STEP):
        piece(u, u_hbm, sems.at[2], g).wait()


def last_kernel(u_hbm, g_ref, dh_ref, dl_ref, sy_ref, out_hbm, u, cy, sems):
    nt = lambda a, b: lax.dot_general(a, b, (((1,), (1,)), ((), ())), preferred_element_type=F32)
    for g in range(NZ // STEP):
        piece(u_hbm, u, sems.at[0], g).start()
    total = jnp.zeros((CX, CY), F32)
    for q in range(8):
        gh, gl = halves(g_ref[q])
        total = total + (nt(gh, dh_ref[q]) + (nt(gh, dl_ref[q]) + nt(gl, dh_ref[q])))
    cy[...] = total

    def step(g, carry):
        fix = dot3(spread(cy[...], g), sy_ref[...], ((1,), (0,)))
        piece(u_hbm, u, sems.at[0], g).wait()
        for i in range(STEP):
            z = STEP * g + i
            u[z] = u[z] - fix[CX * i:CX * (i + 1)]
        piece(u, out_hbm, sems.at[1], g).start()
        return carry

    lax.fori_loop(0, NZ // STEP, step, 0)
    for g in range(NZ // STEP):
        piece(u, out_hbm, sems.at[1], g).wait()


def shape(*dims):
    return jax.ShapeDtypeStruct(dims, F32)


def body(conc, mobility, block_x, spike_x, reduced_x, block_y, spike_y, reduced_y):
    nx, ny = lax.axis_size("gx"), lax.axis_size("gy")
    p, q = lax.axis_index("gx"), lax.axis_index("gy")
    ring = lambda n, s: [(i, (i + s) % n) for i in range(n)]
    hbm = lambda a: pltpu.with_memory_space_constraint(a, pltpu.HBM)

    any_space = pl.BlockSpec(memory_space=pl.ANY)
    slab = pltpu.VMEM((NZ, 8, CY), F32)
    xlo, xhi = pl.pallas_call(
        edge_kernel,
        in_specs=[any_space, any_space],
        out_shape=(shape(96, CY), shape(96, CY)),
        scratch_shapes=[slab] * 4 + [pltpu.SemaphoreType.DMA((4,))],
        compiler_params=CALL, name="edge",
    )(hbm(conc), hbm(mobility))
    xl = lax.ppermute(xhi, "gx", ring(nx, 1))
    xr = lax.ppermute(xlo, "gx", ring(nx, -1))
    ylo, yhi = pl.pallas_call(
        pack_kernel, out_shape=(shape(CX, CY), shape(CX, CY)), compiler_params=CALL, name="pack"
    )(conc, mobility)
    slo, shi = pl.pallas_call(
        corner_kernel, out_shape=(shape(72, CY), shape(72, CY)), compiler_params=CALL, name="corner"
    )(ylo, yhi, xl, xr)
    yl = lax.ppermute(shi, "gy", ring(ny, 1))
    yr = lax.ppermute(slo, "gy", ring(ny, -1))

    full = lambda *dims: pltpu.VMEM(dims, F32)
    groups = NZ // STEP
    big = pltpu.HBM((NZ, CX, CY), F32)
    lin, rims = pl.pallas_call(
        lines_kernel,
        in_specs=[any_space] * 3 + [pl.BlockSpec()] * 8,
        out_specs=(any_space, pl.BlockSpec()),
        out_shape=(big, shape(NZ, 4, CY)),
        scratch_shapes=[full(NZ, CX, CY), full(NZ, CX, CY), full(NZ, CX, CX), full(NZ, CX, CY)]
        + [full(CX, CY)] * 2 + [full(NZ, CY)] * 4 + [pltpu.SemaphoreType.DMA((4, groups))],
        compiler_params=CALL, name="lines",
    )(hbm(conc), hbm(mobility), hbm(block_x), xlo, xhi, slo, shi, yl, yr, xl, xr)

    lin, rims, block_y, reduced_y = lax.optimization_barrier((lin, rims, block_y, reduced_y))
    sx = jnp.transpose(spike_x, (0, 2, 1)).reshape(4 * NZ, CX)
    sy = jnp.transpose(spike_y, (0, 2, 1)).reshape(4 * NZ, CY)
    byr = jnp.concatenate([block_y[:, CY - 2:], block_y[:, :2]], axis=1).reshape(4 * NZ, CY)
    wrim = pl.pallas_call(wide_kernel, out_shape=shape(CX, CY), compiler_params=CALL, name="wide")(lin, byr)
    below = lax.dynamic_slice_in_dim(reduced_y, (4 * q - 2) % (4 * ny), 2, 1)
    above = lax.dynamic_slice_in_dim(reduced_y, (4 * q + 4) % (4 * ny), 2, 1)
    used = jnp.concatenate([below, above], axis=1).reshape(4 * NZ, 4 * ny)
    dh, dl = pl.pallas_call(
        diag_kernel,
        out_shape=(jax.ShapeDtypeStruct((ny, CY, CY), BF16),) * 2,
        compiler_params=CALL, name="diag",
    )(used)

    mine = lax.dynamic_index_in_dim(reduced_x, p, 0, keepdims=False)
    rims = lax.all_to_all(rims, "gx", 0, 0, tiled=True)
    rims, wrim, dh, dl, mine = lax.optimization_barrier((rims, wrim, dh, dl, mine))
    solved = pl.pallas_call(
        reduced_kernel, out_shape=shape(4 * NZ, CY), compiler_params=CALL, name="reduced"
    )(mine, rims.reshape(4 * NZ, CY))
    cx = lax.all_to_all(solved.reshape(NZ, 4, CY), "gx", 0, 0, tiled=True).reshape(4 * NZ, CY)

    yrim = pl.pallas_call(rims_kernel, out_shape=shape(ny, CX, CY), compiler_params=CALL, name="rims")(
        wrim, cx, byr, sx
    )
    yall = lax.all_to_all(yrim, "gy", 0, 0, tiled=True)
    u = pl.pallas_call(
        couple_kernel,
        in_specs=[any_space, any_space, pl.BlockSpec(), pl.BlockSpec()],
        out_specs=any_space,
        out_shape=big,
        scratch_shapes=[full(NZ, CX, CY), full(NZ, CY, CY), full(NZ, CX, CY), full(CX, CY),
                        pltpu.SemaphoreType.DMA((3, groups))],
        compiler_params=CALL, name="couple",
    )(hbm(lin), hbm(block_y), cx, sx)
    return pl.pallas_call(
        last_kernel,
        in_specs=[any_space] + [pl.BlockSpec()] * 4,
        out_specs=any_space,
        out_shape=big,
        scratch_shapes=[full(NZ, CX, CY), full(CX, CY), pltpu.SemaphoreType.DMA((2, groups))],
        compiler_params=CALL, name="last",
    )(hbm(u), yall, dh, dl, sy)


def solution(mesh):
    in_specs = (
        P(None, "gx", "gy"),
        P(None, "gx", "gy"),
        P(None, "gx", None),
        P(None, "gx", None),
        P(),
        P(None, "gy", None),
        P(None, "gy", None),
        P(),
    )
    out_specs = P(None, "gx", "gy")
    return jax.shard_map(body, mesh=mesh, in_specs=in_specs, out_specs=out_specs, check_vma=False)
```

time: 99.5 us -> 76.6 us (0.77); the launches traced: 97.6 us -> 76.2 us
  local copies, waits for them, and re-layouts: 32.5 us -> 3.32 us
  blocking collectives: 0 us -> 13.8 us
  starting transfers between devices: 26.5 us -> 21.9 us
  Pallas kernels: 17 us -> 21.2 us
  waiting for transfers between devices: 19.6 us -> 15.7 us
  other arithmetic: 1.85 us -> 0.07 us
    mul x4 -> x0, local copies, waits for them, and re-layouts: 15.1 us -> none  [body(): diag = (blocks * same).reshape(ny, 4 * NZ, 4 * NZ)]
    all_to_all x0 -> x1, blocking collectives: none -> 13.8 us  [body(): lax.all_to_all(solved.reshape(NZ, 4, CY), 'gx', 0, 0, tiled=True)]
    unnamed x30 -> x12, local copies, waits for them, and re-layouts: 9.83 us -> 1.24 us
    ppermute x4, waiting for transfers between devices: 4.6 us -> 9.98 us  [the longest x1 4.07 us: body(): xl = lax.ppermute(xhi, 'gx', ring(nx, 1))]
    all_to_all x2 -> x1, waiting for transfers between devices: 5.13 us -> 0.01 us  [body(): yall = lax.all_to_all(yrim, 'gy', 0, 0, tiled=True)]
    pallas_call x4 -> x9, Pallas kernels: 16.2 us -> 21 us  [the longest x1 6.78 us: body(): pl.pallas_call(lines_kernel, in_specs=[any_space] * 3 + [pl.BlockSpec()]...]
    all_to_all x1, waiting for transfers between devices: 9.85 us -> 5.68 us  [body(): rims = lax.all_to_all(rims, 'gx', 0, 0, tiled=True)]
    all_to_all x2 -> x1, starting transfers between devices: 7.41 us -> 3.41 us  [body(): yall = lax.all_to_all(yrim, 'gy', 0, 0, tiled=True)]
  transfers between devices with their start and end apart: 7 -> 6, of which waited for: 4 -> 5; matrix products, arithmetic and copies ran while one was open for 24% -> 3% of each run, Pallas kernels for 0% -> 11%
where the time goes in v2:
time: 76.6 us; the launch traced here: 76.2 us
  starting transfers between devices  21.9 us (29%)
  Pallas kernels  21.2 us (28%)
  waiting for transfers between devices  15.7 us (20%)
  blocking collectives  13.8 us (18%)
  local copies, waits for them, and re-layouts  3.32 us (4%)
    all_to_all x1, blocking collectives, body(): lax.all_to_all(solved.reshape(NZ, 4, CY), 'gx', 0, 0, tiled=True)  13.8 us
    all_to_all x1, starting transfers between devices, body(): rims = lax.all_to_all(rims, 'gx', 0, 0, tiled=True)  11.3 us
    pallas_call x1, Pallas kernels, body(): pl.pallas_call(lines_kernel, in_specs=[any_space] * 3 + [pl.BlockSpec()]...  6.78 us
    pallas_call x1, Pallas kernels, body(): pl.pallas_call(couple_kernel, in_specs=[any_space, any_space, pl.BlockSpe...  6.67 us
    all_to_all x1, waiting for transfers between devices, body(): rims = lax.all_to_all(rims, 'gx', 0, 0, tiled=True)  5.68 us
    ppermute x1, waiting for transfers between devices, body(): xl = lax.ppermute(xhi, 'gx', ring(nx, 1))  4.07 us
    ppermute x1, waiting for transfers between devices, body(): yl = lax.ppermute(shi, 'gy', ring(ny, 1))  3.86 us
    pallas_call x1, Pallas kernels, body(): pl.pallas_call(last_kernel, in_specs=[any_space] + [pl.BlockSpec()] * 4,...  3.61 us
  transfers between devices with their start and end apart: 6, of which 5 were waited for; matrix products, arithmetic and copies ran while one was open for 3% of the time, Pallas kernels for 11%

profile of v2, /device:TPU:1, one launch (start us, length us, event | category | flops | bytes accessed | tf_op | source)
XLA Modules:
  0.0 76.2 jit_solution(13320353293253999131)
XLA Ops:
  0.0 0.0 copy-start
  0.0 1.3 %edge.1 = (f32[96,128]{1,0:T(8,128)S(1)}, f32[96,128]{1,0:T(8,128)S(1)}) custom-call(f32[32,64,128]{2,1,0:T(8,128)} %c_hbm.1, f32[32,64,128]{2,1,0:T(8,128)} %m_hbm.1), custom_call_target="tpu_custom_call" | custom-call | tf_op jit(solution)/shard_map/edge/pallas_call | solution.py:290
  1.4 3.3 %collective-permute-start.1 = (f32[96,128]{1,0:T(8,128)S(1)}, f32[96,128]{1,0:T(8,128)S(1)}, u32[]{:S(2)}, u32[]{:S(2)}) collective-permute-start(f32[96,128]{1,0:T(8,128)S(1)} %get-tuple-element.24.own_lo), channel_id=1, source_target_pairs={{0,248},{8,0},{16,8},{24,16},{32,24},{40,32},{48,40},{56,48},{64,5... | collective-permute-start | bytes 147464 | tf_op jit(solution)/shard_map/ppermute | solution.py:298
  4.7 1.0 %collective-permute-start = (f32[96,128]{1,0:T(8,128)S(1)}, f32[96,128]{1,0:T(8,128)S(1)}, u32[]{:S(2)}, u32[]{:S(2)}) collective-permute-start(f32[96,128]{1,0:T(8,128)S(1)} %get-tuple-element.25.own_hi), channel_id=1, source_target_pairs={{0,8},{8,16},{16,24},{24,32},{32,40},{40,48},{48,56},{56,64},{64,7... | collective-permute-start | bytes 147464 | tf_op jit(solution)/shard_map/ppermute | solution.py:297
  5.7 0.0 copy-done.2
  5.7 0.0 copy-done.1
  5.7 0.6 pack.1
  6.3 1.1 %collective-permute-done.1.xr_ref = f32[96,128]{1,0:T(8,128)S(1)} collective-permute-done((f32[96,128]{1,0:T(8,128)S(1)}, f32[96,128]{1,0:T(8,128)S(1)}, u32[]{:S(2)}, u32[]{:S(2)}) %collective-permute-start.1) | collective-permute-done | bytes 49184 | tf_op jit(solution)/shard_map/ppermute | solution.py:298
  7.3 4.1 %collective-permute-done.xl_ref = f32[96,128]{1,0:T(8,128)S(1)} collective-permute-done((f32[96,128]{1,0:T(8,128)S(1)}, f32[96,128]{1,0:T(8,128)S(1)}, u32[]{:S(2)}, u32[]{:S(2)}) %collective-permute-start) | collective-permute-done | bytes 49184 | tf_op jit(solution)/shard_map/ppermute | solution.py:297
  11.4 0.1 corner.1
  11.5 2.8 %collective-permute-start.3 = (f32[72,128]{1,0:T(8,128)S(1)}, f32[72,128]{1,0:T(8,128)S(1)}, u32[]{:S(2)}, u32[]{:S(2)}) collective-permute-start(f32[72,128]{1,0:T(8,128)S(1)} %get-tuple-element.28.slo_ref), channel_id=1, source_target_pairs={{0,7},{1,0},{2,1},{3,2},{4,3},{5,4},{6,5},{7,6},{8,15},{9,8},{10,9... | collective-permute-start | bytes 110600 | tf_op jit(solution)/shard_map/ppermute | solution.py:306
  14.4 0.0 collective-permute-start.2
  14.4 0.0 copy-start.4
  14.4 1.0 %collective-permute-done.3.yr_ref = f32[72,128]{1,0:T(8,128)S(1)} collective-permute-done((f32[72,128]{1,0:T(8,128)S(1)}, f32[72,128]{1,0:T(8,128)S(1)}, u32[]{:S(2)}, u32[]{:S(2)}) %collective-permute-start.3) | collective-permute-done | bytes 36896 | tf_op jit(solution)/shard_map/ppermute | solution.py:306
  15.4 3.9 %collective-permute-done.2.yl_ref = f32[72,128]{1,0:T(8,128)S(1)} collective-permute-done((f32[72,128]{1,0:T(8,128)S(1)}, f32[72,128]{1,0:T(8,128)S(1)}, u32[]{:S(2)}, u32[]{:S(2)}) %collective-permute-start.2) | collective-permute-done | bytes 36896 | tf_op jit(solution)/shard_map/ppermute | solution.py:305
  19.3 6.8 %lines.1 = (f32[32,64,128]{2,1,0:T(8,128)}, f32[32,4,128]{2,1,0:T(4,128)}) custom-call(f32[32,64,128]{2,1,0:T(8,128)} %c_hbm.1, f32[32,64,128]{2,1,0:T(8,128)} %m_hbm.1, f32[32,64,64]{2,1,0:T(8,128)} %bx_hbm.1, f32[96,128]{1,0:T(8,128)S(1)} %get-tuple-element.24.own_lo, f32[96,128]{1,0:T(8,128)S(1)} %get-tuple-element.25.own_hi, ...), custom_call_target="tpu_custom_call" | custom-call | tf_op jit(solution)/shard_map/lines/pallas_call | solution.py:311
  26.1 11.3 %all-to-all-start = ((f32[32,4,128]{2,1,0:T(4,128)}), f32[32,4,128]{2,1,0:T(4,128)S(1)}, u32[]{:S(2)}, u32[]{:S(2)}) async-start(f32[32,4,128]{2,1,0:T(4,128)} %get-tuple-element.34), calls=%async_computation | async-start | bytes 131072 | tf_op jit(solution)/shard_map/all_to_all | solution.py:336
  37.4 1.0 %fusion = (f32[32,2,128]{2,1,0:T(2,128)S(1)}, f32[32,2,128]{2,1,0:T(2,128)S(1)}) fusion(f32[32,128,128]{2,1,0:T(8,128)} %by_hbm), kind=kLoop, calls=%fused_computation.5 | loop fusion | bytes 131072 | tf_op jit(solution)/shard_map/slice | solution.py:324
  38.4 1.1 %constant_dynamic-slice_fusion.1 = (f32[32,2,32]{2,1,0:T(2,128)S(1)}, f32[32,2,32]{2,1,0:T(2,128)S(1)}) fusion(f32[32,32,32]{2,1,0:T(8,128)} %param.15, s32[]{:T(128)S(6)} %select_n.22, s32[]{:T(128)S(6)} %select_n.24), kind=kLoop, calls=%fused_computation.4 | loop fusion | bytes 32776 | tf_op jit(solution)/shard_map/dynamic_slice | solution.py:326
  39.5 0.3 diag.1
  39.9 0.0 copy-start.3
  39.9 1.2 %copy-done.3 = f32[32,64,128]{2,1,0:T(8,128)S(1)} copy-done((f32[32,64,128]{2,1,0:T(8,128)S(1)}, f32[32,64,128]{2,1,0:T(8,128)}, u32[]{:S(2)}) %copy-start.3) | copy-done | bytes 1048600
  41.1 0.6 wide.1.wrim_ref
  41.7 5.7 %all-to-all-done = f32[32,4,128]{2,1,0:T(4,128)S(1)} async-done(((f32[32,4,128]{2,1,0:T(4,128)}), f32[32,4,128]{2,1,0:T(4,128)S(1)}, u32[]{:S(2)}, u32[]{:S(2)}) %all-to-all-start) | async-done | bytes 65568 | tf_op jit(solution)/shard_map/all_to_all | solution.py:336
  47.4 0.2 reduced.1
  47.5 13.8 %all_to_all.15 = f32[32,4,128]{2,1,0:T(4,128)S(1)} all-to-all(f32[32,4,128]{2,1,0:T(4,128)S(1)} %bitcast.20), channel_id=1, replica_groups=mesh['gx'=32,'gy'=8] {'gx'}, dimensions={0} | all-to-all | bytes 131072 | tf_op jit(solution)/shard_map/all_to_all | solution.py:341
  61.4 1.1 %rims.1 = f32[8,64,128]{2,1,0:T(8,128)} custom-call(f32[64,128]{1,0:T(8,128)S(1)} %wide.1.wrim_ref, f32[128,128]{1,0:T(8,128)S(1)} %bitcast.13, f32[128,128]{1,0:T(8,128)S(1)} %bitcast.16, f32[128,64]{1,0:T(8,128)S(1)} %bitcast.17), custom_call_target="tpu_custom_call" | custom-call | tf_op jit(solution)/shard_map/rims/pallas_call | solution.py:343
  62.5 3.4 %all-to-all-start.2 = ((f32[8,64,128]{2,1,0:T(8,128)}), f32[8,64,128]{2,1,0:T(8,128)S(1)}, u32[]{:S(2)}, u32[]{:S(2)}) async-start(f32[8,64,128]{2,1,0:T(8,128)} %rims.1), calls=%async_computation.2 | async-start | bytes 524288 | tf_op jit(solution)/shard_map/all_to_all | solution.py:346
  65.9 0.0 copy-start.5
  65.9 6.7 %couple.1.u_hbm = f32[32,64,128]{2,1,0:T(8,128)} custom-call(f32[32,64,128]{2,1,0:T(8,128)} %get-tuple-element.32.lin_ref.lin_hbm, f32[32,128,128]{2,1,0:T(8,128)} %by_hbm, f32[128,128]{1,0:T(8,128)S(1)} %bitcast.14, f32[128,64]{1,0:T(8,128)S(1)} %bitcast.18), custom_call_target="tpu_custom_call" | custom-call | tf_op jit(solution)/shard_map/couple/pallas_call | solution.py:347
  72.6 0.0 all-to-all-done.2.g_ref
  72.6 3.6 %last.1 = f32[32,64,128]{2,1,0:T(8,128)} custom-call(f32[32,64,128]{2,1,0:T(8,128)} %couple.1.u_hbm, f32[8,64,128]{2,1,0:T(8,128)S(1)} %all-to-all-done.2.g_ref, bf16[8,128,128]{2,1,0:T(8,128)(2,1)S(1)} %get-tuple-element.41.dh_ref, bf16[8,128,128]{2,1,0:T(8,128)(2,1)S(1)} %get-tuple-element.42.dl_ref, f32[128,128]{1,0:T(8,128)S(1)} %bitcast.22), custom_call_target="tpu_custom_call" | custom-call | tf_op jit(solution)/shard_map/last/pallas_call | solution.py:356
  (8 shorter events, 0.1 us)
Async XLA Ops:
  0.0 14.4 %copy-start = (f32[32,128,128]{2,1,0:T(8,128)S(1)}, f32[32,128,128]{2,1,0:T(8,128)}, u32[]{:S(2)}) copy-start(f32[32,128,128]{2,1,0:T(8,128)} %param.12) | copy-start | bytes 6291460
  0.0 5.7 %copy-start.2 = (f32[32,64,128]{2,1,0:T(8,128)S(1)}, f32[32,64,128]{2,1,0:T(8,128)}, u32[]{:S(2)}) copy-start(f32[32,64,128]{2,1,0:T(8,128)} %m_hbm.1) | copy-start | bytes 3145732
  0.0 5.7 %copy-start.1 = (f32[32,64,128]{2,1,0:T(8,128)S(1)}, f32[32,64,128]{2,1,0:T(8,128)}, u32[]{:S(2)}) copy-start(f32[32,64,128]{2,1,0:T(8,128)} %c_hbm.1) | copy-start | bytes 3145732
  1.4 6.0 %collective-permute-start.1 = (f32[96,128]{1,0:T(8,128)S(1)}, f32[96,128]{1,0:T(8,128)S(1)}, u32[]{:S(2)}, u32[]{:S(2)}) collective-permute-start(f32[96,128]{1,0:T(8,128)S(1)} %get-tuple-element.24.own_lo), channel_id=1, source_target_pairs={{0,248},{8,0},{16,8},{24,16},{32,24},{40,32},{48,40},{56,48},{64,5... | collective-permute-start | bytes 147464 | tf_op jit(solution)/shard_map/ppermute | solution.py:298
  4.7 6.8 %collective-permute-start = (f32[96,128]{1,0:T(8,128)S(1)}, f32[96,128]{1,0:T(8,128)S(1)}, u32[]{:S(2)}, u32[]{:S(2)}) collective-permute-start(f32[96,128]{1,0:T(8,128)S(1)} %get-tuple-element.25.own_hi), channel_id=1, source_target_pairs={{0,8},{8,16},{16,24},{24,32},{32,40},{40,48},{48,56},{56,64},{64,7... | collective-permute-start | bytes 147464 | tf_op jit(solution)/shard_map/ppermute | solution.py:297
  11.5 3.9 %collective-permute-start.3 = (f32[72,128]{1,0:T(8,128)S(1)}, f32[72,128]{1,0:T(8,128)S(1)}, u32[]{:S(2)}, u32[]{:S(2)}) collective-permute-start(f32[72,128]{1,0:T(8,128)S(1)} %get-tuple-element.28.slo_ref), channel_id=1, source_target_pairs={{0,7},{1,0},{2,1},{3,2},{4,3},{5,4},{6,5},{7,6},{8,15},{9,8},{10,9... | collective-permute-start | bytes 110600 | tf_op jit(solution)/shard_map/ppermute | solution.py:306
  14.4 4.9 %collective-permute-start.2 = (f32[72,128]{1,0:T(8,128)S(1)}, f32[72,128]{1,0:T(8,128)S(1)}, u32[]{:S(2)}, u32[]{:S(2)}) collective-permute-start(f32[72,128]{1,0:T(8,128)S(1)} %get-tuple-element.29.shi_ref), channel_id=1, source_target_pairs={{0,1},{1,2},{2,3},{3,4},{4,5},{5,6},{6,7},{7,0},{8,9},{9,10},{10,1... | collective-permute-start | bytes 110600 | tf_op jit(solution)/shard_map/ppermute | solution.py:305
  14.4 46.9 %copy-start.4 = (f32[32,64,4]{1,2,0:T(4,128)S(1)}, f32[32,64,4]{1,2,0:T(4,128)}, u32[]{:S(2)}) copy-start(f32[32,64,4]{1,2,0:T(4,128)} %param.11) | copy-start | bytes 98308
  26.1 21.3 %all-to-all-start = ((f32[32,4,128]{2,1,0:T(4,128)}), f32[32,4,128]{2,1,0:T(4,128)S(1)}, u32[]{:S(2)}, u32[]{:S(2)}) async-start(f32[32,4,128]{2,1,0:T(4,128)} %get-tuple-element.34), calls=%async_computation | async-start | bytes 131072 | tf_op jit(solution)/shard_map/all_to_all | solution.py:336
  39.9 1.2 %copy-start.3 = (f32[32,64,128]{2,1,0:T(8,128)S(1)}, f32[32,64,128]{2,1,0:T(8,128)}, u32[]{:S(2)}) copy-start(f32[32,64,128]{2,1,0:T(8,128)} %get-tuple-element.32.lin_ref.lin_hbm) | copy-start | bytes 3145732
  62.5 10.1 %all-to-all-start.2 = ((f32[8,64,128]{2,1,0:T(8,128)}), f32[8,64,128]{2,1,0:T(8,128)S(1)}, u32[]{:S(2)}, u32[]{:S(2)}) async-start(f32[8,64,128]{2,1,0:T(8,128)} %rims.1), calls=%async_computation.2 | async-start | bytes 524288 | tf_op jit(solution)/shard_map/all_to_all | solution.py:346
  65.9 6.7 %copy-start.5 = (f32[32,128,4]{1,2,0:T(4,128)S(1)}, f32[32,128,4]{1,2,0:T(4,128)}, u32[]{:S(2)}) copy-start(f32[32,128,4]{1,2,0:T(4,128)} %param.14) | copy-start | bytes 196612

commit v3 on v2

--- a/solution.py
+++ b/solution.py
@@ -44,7 +44,11 @@
     return prefactor * (0.25 + sq) / (1.0 + sq)
 
 
-def edge_kernel(c_ref, m_ref, xlo_ref, xhi_ref, ct, cb, mt, mb, sems):
+def odd_at(axis):
+    return (lax.axis_index(axis) & 1) == 1
+
+
+def edge_kernel(c_ref, m_ref, first_ref, second_ref, ct, cb, mt, mb, sems):
     top, bottom = pl.ds(0, 8), pl.ds(CX - 8, 8)
     copies = [
         pltpu.make_async_copy(c_ref.at[:, top, :], ct, sems.at[0]),
@@ -56,15 +60,14 @@
         copy.start()
     for copy in copies:
         copy.wait()
-    xlo_ref[0:32] = ct[:, 0, :]
-    xlo_ref[32:64] = ct[:, 1, :]
-    xlo_ref[64:96] = mt[:, 0, :]
-    xhi_ref[0:32] = cb[:, 7, :]
-    xhi_ref[32:64] = cb[:, 6, :]
-    xhi_ref[64:96] = mb[:, 7, :]
-
-
-def pack_kernel(c_ref, m_ref, ylo_ref, yhi_ref):
+    odd = odd_at("gx")
+    rows = ((ct[:, 0, :], cb[:, 7, :]), (ct[:, 1, :], cb[:, 6, :]), (mt[:, 0, :], mb[:, 7, :]))
+    for k, (lo, hi) in enumerate(rows):
+        first_ref[NZ * k:NZ * (k + 1)] = jnp.where(odd, lo, hi)
+        second_ref[NZ * k:NZ * (k + 1)] = jnp.where(odd, hi, lo)
+
+
+def pack_kernel(c_ref, m_ref, first_ref, second_ref):
     lane = iota((CX, CY), 1)
     lo = jnp.zeros((CX, CY), F32)
     hi = jnp.zeros((CX, CY), F32)
@@ -76,23 +79,27 @@
         lo = jnp.where(lane == b + 2, m, lo)
         hi = jnp.where((lane >= a) & (lane <= a + 1), c, hi)
         hi = jnp.where(lane == b + 1, m, hi)
-    ylo_ref[...] = lo
-    yhi_ref[...] = hi
-
-
-def corner_kernel(lo_ref, hi_ref, xl_ref, xr_ref, slo_ref, shi_ref):
+    odd = odd_at("gy")
+    first_ref[...] = jnp.where(odd, lo, hi)
+    second_ref[...] = jnp.where(odd, hi, lo)
+
+
+def corner_kernel(side0_ref, side1_ref, got0_ref, got1_ref, first_ref, second_ref):
     sub, lane = iota((NZ, CY), 0), iota((NZ, CY), 1)
-
-    def across(column, at):
-        return jnp.sum(jnp.where(lane == at, column, 0.0), axis=0, keepdims=True)
-
+    odd_x, odd_y = odd_at("gx"), odd_at("gy")
+    got0, got1 = got0_ref[0:NZ], got1_ref[0:NZ]
+    up, down = jnp.where(odd_x, got0, got1), jnp.where(odd_x, got1, got0)
     pad = jnp.zeros((6, CY), F32)
-    up, down = xl_ref[0:NZ], xr_ref[0:NZ]
-    first, last = 4 * sub, (4 * sub - 1) & (CY - 1)
-    slo_ref[0:CX] = lo_ref[...]
-    slo_ref[CX:72] = jnp.concatenate([across(up[:, :1], first), across(down[:, :1], first), pad])
-    shi_ref[0:CX] = hi_ref[...]
-    shi_ref[CX:72] = jnp.concatenate([across(up[:, CY - 1:], last), across(down[:, CY - 1:], last), pad])
+
+    def rows(k, at):
+        pick = lambda a: jnp.sum(jnp.where(lane == at, a[:, k:k + 1], 0.0), axis=0, keepdims=True)
+        return jnp.concatenate([pick(up), pick(down), pad])
+
+    lo, hi = rows(0, 4 * sub), rows(CY - 1, (4 * sub - 1) & (CY - 1))
+    first_ref[0:CX] = side0_ref[...]
+    second_ref[0:CX] = side1_ref[...]
+    first_ref[CX:72] = jnp.where(odd_y, lo, hi)
+    second_ref[CX:72] = jnp.where(odd_y, hi, lo)
 
 
 def piece(src, dst, sems, g):
@@ -100,16 +107,26 @@
     return pltpu.make_async_copy(src.at[at], dst.at[at], sems.at[g])
 
 
-def lines_kernel(c_hbm, m_hbm, bx_hbm, own_lo, own_hi, slo_ref, shi_ref, yl_ref, yr_ref,
-                 xl_ref, xr_ref, lin_hbm, rim_ref, c_ref, m_ref, bx_ref, lin_ref, ch, fh, mul, mobl, mur, mobr, sems):
+def lines_kernel(c_hbm, m_hbm, bx_hbm, own0_ref, own1_ref, send0_ref, send1_ref, side0_ref, side1_ref, got0_ref,
+                 got1_ref, lin_hbm, rim_ref, c_ref, m_ref, bx_ref, lin_ref, ch, fh, mul, mobl, mur, mobr, slo_ref,
+                 shi_ref, yl_ref, yr_ref, xl_ref, xr_ref, sems):
     row = iota((CX, CY), 0)
     lane = iota((CX, CY), 1)
-    moves = ((c_hbm, c_ref), (m_hbm, m_ref), (bx_hbm, bx_ref), (lin_ref, lin_hbm))
-    for g in range(NZ // STEP):
-        for k in range(3):
-            piece(*moves[k], sems.at[k], g).start()
+    loads = ((c_hbm, c_ref), (m_hbm, m_ref), (bx_hbm, bx_ref))
+    for g in range(NZ // STEP):
+        for k, (src, dst) in enumerate(loads):
+            piece(src, dst, sems.at[k], g).start()
+    odd_x, odd_y = odd_at("gx"), odd_at("gy")
 
     def edges():
+        slo_ref[...] = jnp.where(odd_y, send0_ref[...], send1_ref[...])
+        shi_ref[...] = jnp.where(odd_y, send1_ref[...], send0_ref[...])
+        yl_ref[...] = jnp.where(odd_y, side0_ref[...], side1_ref[...])
+        yr_ref[...] = jnp.where(odd_y, side1_ref[...], side0_ref[...])
+        xl_ref[...] = jnp.where(odd_x, got0_ref[...], got1_ref[...])
+        xr_ref[...] = jnp.where(odd_x, got1_ref[...], got0_ref[...])
+        own_lo = jnp.where(odd_x, own0_ref[0:NZ], own1_ref[0:NZ])
+        own_hi = jnp.where(odd_x, own1_ref[0:NZ], own0_ref[0:NZ])
         lo, hi, left, right = slo_ref[0:CX], shi_ref[0:CX], yl_ref[0:CX], yr_ref[0:CX]
 
         def around(a, ref):
@@ -139,7 +156,7 @@
             east = jnp.where(ln == 4 * sub, yr_ref[CX + k:CX + k + 1], 0.0)
             lf = jnp.where(ln == 0, jnp.sum(west, axis=1, keepdims=True), roll(a, 1, 1))
             rt = jnp.where(ln == CY - 1, jnp.sum(east, axis=1, keepdims=True), roll(a, -1, 1))
-            mu_out[...] = potential(a, x_ref[32:64] + own[0:32] + lf + rt - 4.0 * a)
+            mu_out[...] = potential(a, x_ref[32:64] + own + lf + rt - 4.0 * a)
             mob_out[...] = mobile(x_ref[64:96], a)
 
         halo_row(xl_ref, own_lo, 0, mul, mobl)
@@ -148,11 +165,11 @@
     edges()
 
     def step(g, carry):
-        for k in range(3):
-            piece(*moves[k], sems.at[k], g).wait()
+        for k, (src, dst) in enumerate(loads):
+            piece(src, dst, sems.at[k], g).wait()
         for i in range(STEP):
             plane(g * STEP + i)
-        piece(*moves[3], sems.at[3], g).start()
+        piece(lin_ref, lin_hbm, sems.at[3], g).start()
         return carry
 
     def plane(z):
@@ -183,7 +200,7 @@
 
     lax.fori_loop(0, NZ // STEP, step, 0)
     for g in range(NZ // STEP):
-        piece(*moves[3], sems.at[3], g).wait()
+        piece(lin_ref, lin_hbm, sems.at[3], g).wait()
 
 
 def reduced_kernel(r_ref, rim_ref, out_ref):
@@ -192,11 +209,24 @@
     out_ref[...] = dot3(use, rim_ref[...], ((1,), (0,)))
 
 
-def wide_kernel(lin_ref, byr_ref, rim_ref):
+def wide_kernel(lin_hbm, by_hbm, rim_ref, byr_ref, lin, low, high, sems):
+    ends = [
+        pltpu.make_async_copy(by_hbm.at[:, pl.ds(0, 8), :], low, sems.at[NZ // STEP]),
+        pltpu.make_async_copy(by_hbm.at[:, pl.ds(CY - 8, 8), :], high, sems.at[NZ // STEP + 1]),
+    ]
+    for copy in ends:
+        copy.start()
+    for g in range(NZ // STEP):
+        piece(lin_hbm, lin, sems, g).start()
+    for copy in ends:
+        copy.wait()
+    for k in range(4):
+        byr_ref[pl.ds(k, NZ, stride=4), :] = high[:, 6 + k, :] if k < 2 else low[:, k - 2, :]
     lane = iota((CX, CY), 1)
     acc = jnp.zeros((CX, CY), F32)
     for g in range(NZ // STEP):
-        part = lin_ref[STEP * g:STEP * (g + 1)].reshape(STEP * CX, CY)
+        piece(lin_hbm, lin, sems, g).wait()
+        part = lin[STEP * g:STEP * (g + 1)].reshape(STEP * CX, CY)
         out = dot3(part, byr_ref[...], ((1,), (1,)))
         for i in range(STEP):
             acc = jnp.where((lane >> 2) == STEP * g + i, out[CX * i:CX * (i + 1)], acc)
@@ -205,14 +235,18 @@
 
 def diag_kernel(y_ref, hi_ref, lo_ref):
     n = 4 * NZ
-    yh, yl = halves(y_ref[...])
+    r, col = iota((n, 32 * NZ), 0), iota((n, 32 * NZ), 1)
+    k, q = r & 3, lax.axis_index("gy")
+    used = (r >> 2) * 32 + ((4 * q + k + jnp.where(k < 2, -2, 2)) & 31)
+    take = jnp.where(col == used, 1.0, 0.0).astype(BF16)
     same = (iota((n, n), 0) >> 2) == (iota((n, n), 1) >> 2)
     col, ln = iota((32, n), 0), iota((32, n), 1)
-    for q in range(8):
-        pick = jnp.where(col == 4 * q + ((ln + 2) & 3), 1.0, 0.0).astype(BF16)
-        for a, ref in ((yh, hi_ref), (yl, lo_ref)):
-            full = jnp.dot(a, pick, preferred_element_type=F32)
-            ref[q] = jnp.where(same, full, 0.0).astype(BF16)
+    for half, ref in zip(halves(y_ref[...]), (hi_ref, lo_ref)):
+        mine = jnp.dot(take, half, preferred_element_type=F32).astype(BF16)
+        for p in range(8):
+            pick = jnp.where(col == 4 * p + ((ln + 2) & 3), 1.0, 0.0).astype(BF16)
+            full = jnp.dot(mine, pick, preferred_element_type=F32)
+            ref[:, n * p:n * (p + 1)] = jnp.where(same, full, 0.0).astype(BF16)
 
 
 def rims_kernel(wrim_ref, cx_ref, byr_ref, sx_ref, out_ref):
@@ -255,11 +289,8 @@
     nt = lambda a, b: lax.dot_general(a, b, (((1,), (1,)), ((), ())), preferred_element_type=F32)
     for g in range(NZ // STEP):
         piece(u_hbm, u, sems.at[0], g).start()
-    total = jnp.zeros((CX, CY), F32)
-    for q in range(8):
-        gh, gl = halves(g_ref[q])
-        total = total + (nt(gh, dh_ref[q]) + (nt(gh, dl_ref[q]) + nt(gl, dh_ref[q])))
-    cy[...] = total
+    gh, gl = halves(jnp.concatenate([g_ref[q] for q in range(8)], axis=1))
+    cy[...] = nt(gh, dh_ref[...]) + (nt(gh, dl_ref[...]) + nt(gl, dh_ref[...]))
 
     def step(g, carry):
         fix = dot3(spread(cy[...], g), sy_ref[...], ((1,), (0,)))
@@ -281,56 +312,63 @@
 
 def body(conc, mobility, block_x, spike_x, reduced_x, block_y, spike_y, reduced_y):
     nx, ny = lax.axis_size("gx"), lax.axis_size("gy")
-    p, q = lax.axis_index("gx"), lax.axis_index("gy")
-    ring = lambda n, s: [(i, (i + s) % n) for i in range(n)]
+    p = lax.axis_index("gx")
     hbm = lambda a: pltpu.with_memory_space_constraint(a, pltpu.HBM)
-
     any_space = pl.BlockSpec(memory_space=pl.ANY)
-    slab = pltpu.VMEM((NZ, 8, CY), F32)
-    xlo, xhi = pl.pallas_call(
+    here = pl.BlockSpec()
+    full = lambda *dims: pltpu.VMEM(dims, F32)
+    groups = NZ // STEP
+    big, big_hbm = shape(NZ, CX, CY), pltpu.HBM((NZ, CX, CY), F32)
+
+    def pairs(n, start):
+        ends = [(i % n, (i + 1) % n) for i in range(start, start + n, 2)]
+        return ends + [(b, a) for a, b in ends]
+
+    def swap(first, second, axis, n):
+        return lax.ppermute(first, axis, pairs(n, 0)), lax.ppermute(second, axis, pairs(n, 1))
+
+    own0, own1 = pl.pallas_call(
         edge_kernel,
         in_specs=[any_space, any_space],
-        out_shape=(shape(96, CY), shape(96, CY)),
-        scratch_shapes=[slab] * 4 + [pltpu.SemaphoreType.DMA((4,))],
+        out_shape=(shape(3 * NZ, CY), shape(3 * NZ, CY)),
+        scratch_shapes=[full(NZ, 8, CY)] * 4 + [pltpu.SemaphoreType.DMA((4,))],
         compiler_params=CALL, name="edge",
     )(hbm(conc), hbm(mobility))
-    xl = lax.ppermute(xhi, "gx", ring(nx, 1))
-    xr = lax.ppermute(xlo, "gx", ring(nx, -1))
-    ylo, yhi = pl.pallas_call(
-        pack_kernel, out_shape=(shape(CX, CY), shape(CX, CY)), compiler_params=CALL, name="pack"
+    got0, got1 = swap(own0, own1, "gx", nx)
+    side = pl.pallas_call(
+        pack_kernel, out_shape=(shape(CX, CY),) * 2, compiler_params=CALL, name="pack"
     )(conc, mobility)
-    slo, shi = pl.pallas_call(
-        corner_kernel, out_shape=(shape(72, CY), shape(72, CY)), compiler_params=CALL, name="corner"
-    )(ylo, yhi, xl, xr)
-    yl = lax.ppermute(shi, "gy", ring(ny, 1))
-    yr = lax.ppermute(slo, "gy", ring(ny, -1))
-
-    full = lambda *dims: pltpu.VMEM(dims, F32)
-    groups = NZ // STEP
-    big = pltpu.HBM((NZ, CX, CY), F32)
+    send0, send1 = pl.pallas_call(
+        corner_kernel, out_shape=(shape(72, CY),) * 2, compiler_params=CALL, name="corner"
+    )(*side, got0, got1)
+    side0, side1 = swap(send0, send1, "gy", ny)
+
     lin, rims = pl.pallas_call(
         lines_kernel,
-        in_specs=[any_space] * 3 + [pl.BlockSpec()] * 8,
-        out_specs=(any_space, pl.BlockSpec()),
-        out_shape=(big, shape(NZ, 4, CY)),
+        in_specs=[any_space] * 3 + [here] * 8,
+        out_specs=(any_space, here),
+        out_shape=(big_hbm, shape(NZ, 4, CY)),
         scratch_shapes=[full(NZ, CX, CY), full(NZ, CX, CY), full(NZ, CX, CX), full(NZ, CX, CY)]
-        + [full(CX, CY)] * 2 + [full(NZ, CY)] * 4 + [pltpu.SemaphoreType.DMA((4, groups))],
+        + [full(CX, CY)] * 2 + [full(NZ, CY)] * 4 + [full(72, CY)] * 4 + [full(3 * NZ, CY)] * 2
+        + [pltpu.SemaphoreType.DMA((4, groups))],
         compiler_params=CALL, name="lines",
-    )(hbm(conc), hbm(mobility), hbm(block_x), xlo, xhi, slo, shi, yl, yr, xl, xr)
+    )(hbm(conc), hbm(mobility), hbm(block_x), own0, own1, send0, send1, side0, side1, got0, got1)
 
     lin, rims, block_y, reduced_y = lax.optimization_barrier((lin, rims, block_y, reduced_y))
     sx = jnp.transpose(spike_x, (0, 2, 1)).reshape(4 * NZ, CX)
     sy = jnp.transpose(spike_y, (0, 2, 1)).reshape(4 * NZ, CY)
-    byr = jnp.concatenate([block_y[:, CY - 2:], block_y[:, :2]], axis=1).reshape(4 * NZ, CY)
-    wrim = pl.pallas_call(wide_kernel, out_shape=shape(CX, CY), compiler_params=CALL, name="wide")(lin, byr)
-    below = lax.dynamic_slice_in_dim(reduced_y, (4 * q - 2) % (4 * ny), 2, 1)
-    above = lax.dynamic_slice_in_dim(reduced_y, (4 * q + 4) % (4 * ny), 2, 1)
-    used = jnp.concatenate([below, above], axis=1).reshape(4 * NZ, 4 * ny)
+    wrim, byr = pl.pallas_call(
+        wide_kernel,
+        in_specs=[any_space] * 2,
+        out_shape=(shape(CX, CY), shape(4 * NZ, CY)),
+        scratch_shapes=[full(NZ, CX, CY)] + [full(NZ, 8, CY)] * 2 + [pltpu.SemaphoreType.DMA((groups + 2,))],
+        compiler_params=CALL, name="wide",
+    )(hbm(lin), hbm(block_y))
     dh, dl = pl.pallas_call(
         diag_kernel,
-        out_shape=(jax.ShapeDtypeStruct((ny, CY, CY), BF16),) * 2,
+        out_shape=(jax.ShapeDtypeStruct((CY, ny * CY), BF16),) * 2,
         compiler_params=CALL, name="diag",
-    )(used)
+    )(reduced_y.reshape(NZ * 4 * ny, 4 * ny))
 
     mine = lax.dynamic_index_in_dim(reduced_x, p, 0, keepdims=False)
     rims = lax.all_to_all(rims, "gx", 0, 0, tiled=True)
@@ -346,18 +384,18 @@
     yall = lax.all_to_all(yrim, "gy", 0, 0, tiled=True)
     u = pl.pallas_call(
         couple_kernel,
-        in_specs=[any_space, any_space, pl.BlockSpec(), pl.BlockSpec()],
+        in_specs=[any_space, any_space, here, here],
         out_specs=any_space,
-        out_shape=big,
+        out_shape=big_hbm,
         scratch_shapes=[full(NZ, CX, CY), full(NZ, CY, CY), full(NZ, CX, CY), full(CX, CY),
                         pltpu.SemaphoreType.DMA((3, groups))],
         compiler_params=CALL, name="couple",
     )(hbm(lin), hbm(block_y), cx, sx)
     return pl.pallas_call(
         last_kernel,
-        in_specs=[any_space] + [pl.BlockSpec()] * 4,
+        in_specs=[any_space] + [here] * 4,
         out_specs=any_space,
-        out_shape=big,
+        out_shape=big_hbm,
         scratch_shapes=[full(NZ, CX, CY), full(CX, CY), pltpu.SemaphoreType.DMA((2, groups))],
         compiler_params=CALL, name="last",
     )(hbm(u), yall, dh, dl, sy)

time: 76.6 us -> 72.5 us (0.946)
  waiting for transfers between devices: 15.7 us -> 11.9 us
  local copies, waits for them, and re-layouts: 3.32 us -> 0.04 us
  Pallas kernels: 21.2 us -> 23.9 us
    ppermute x4, waiting for transfers between devices: 9.98 us -> 6 us  [the longest x2 5.53 us: swap(): lax.ppermute(second, axis, pairs(n, 1))]
    pallas_call x7, Pallas kernels: 18.6 us -> 21.3 us  [the longest x1 6.71 us: body(): pl.pallas_call(lines_kernel, in_specs=[any_space] * 3 + [here] * 8, out_s...]
    unnamed x12, local copies, waits for them, and re-layouts: 1.24 us -> 0.03 us
    all_to_all x1, starting transfers between devices: 11.3 us -> 12.4 us  [body(): rims = lax.all_to_all(rims, 'gx', 0, 0, tiled=True)]
    dynamic_slice x1 -> x0, local copies, waits for them, and re-layouts: 1.07 us -> none  [body(): below = lax.dynamic_slice_in_dim(reduced_y, (4 * q - 2) % (4 * ny), 2, 1)]
    slice x1 -> x0, local copies, waits for them, and re-layouts: 1 us -> none  [body(): block_y[:, CY - 2:]]
  transfers between devices with their start and end apart: 6 -> 6, of which waited for: 5 -> 4; matrix products, arithmetic and copies ran while one was open for 3% -> 0% of each run, Pallas kernels for 11% -> 15%
where the time goes in v3:
time: 72.5 us; the launch traced here: 72.2 us
  Pallas kernels  23.9 us (33%)
  starting transfers between devices  22.6 us (31%)
  blocking collectives  13.5 us (19%)
  waiting for transfers between devices  11.9 us (16%)
    all_to_all x1, blocking collectives, body(): lax.all_to_all(solved.reshape(NZ, 4, CY), 'gx', 0, 0, tiled=True)  13.5 us
    all_to_all x1, starting transfers between devices, body(): rims = lax.all_to_all(rims, 'gx', 0, 0, tiled=True)  12.4 us
    pallas_call x1, Pallas kernels, body(): pl.pallas_call(lines_kernel, in_specs=[any_space] * 3 + [here] * 8, out_s...  6.71 us
    pallas_call x1, Pallas kernels, body(): pl.pallas_call(couple_kernel, in_specs=[any_space, any_space, here, here]...  6.66 us
    all_to_all x1, waiting for transfers between devices, body(): rims = lax.all_to_all(rims, 'gx', 0, 0, tiled=True)  5.95 us
    ppermute x2, waiting for transfers between devices, swap(): lax.ppermute(second, axis, pairs(n, 1))  5.53 us
    all_to_all x1, starting transfers between devices, body(): yall = lax.all_to_all(yrim, 'gy', 0, 0, tiled=True)  3.42 us
    pallas_call x1, Pallas kernels, body(): pl.pallas_call(last_kernel, in_specs=[any_space] + [here] * 4, out_specs=...  3.42 us
  transfers between devices with their start and end apart: 6, of which 4 were waited for; matrix products, arithmetic and copies ran while one was open for 0% of the time, Pallas kernels for 15%

profile of v3, /device:TPU:1, one launch (start us, length us, event | category | flops | bytes accessed | tf_op | source)
XLA Modules:
  0.0 72.2 jit_solution(5506535824316373814)
XLA Ops:
  0.0 0.0 copy-start
  0.0 1.4 %edge.1 = (f32[96,128]{1,0:T(8,128)S(1)}, f32[96,128]{1,0:T(8,128)S(1)}) custom-call(f32[32,64,128]{2,1,0:T(8,128)} %c_hbm.1, f32[32,64,128]{2,1,0:T(8,128)} %m_hbm.1), custom_call_target="tpu_custom_call" | custom-call | tf_op jit(solution)/shard_map/edge/pallas_call | solution.py:330
  1.4 3.3 %collective-permute-start = (f32[96,128]{1,0:T(8,128)S(1)}, f32[96,128]{1,0:T(8,128)S(1)}, u32[]{:S(2)}, u32[]{:S(2)}) collective-permute-start(f32[96,128]{1,0:T(8,128)S(1)} %get-tuple-element.26.own0_ref), channel_id=1, source_target_pairs={{0,8},{16,24},{32,40},{48,56},{64,72},{80,88},{96,104},{112,120},{... | collective-permute-start | bytes 147464 | tf_op jit(solution)/shard_map/ppermute | solution.py:328
  4.7 1.0 %collective-permute-start.1 = (f32[96,128]{1,0:T(8,128)S(1)}, f32[96,128]{1,0:T(8,128)S(1)}, u32[]{:S(2)}, u32[]{:S(2)}) collective-permute-start(f32[96,128]{1,0:T(8,128)S(1)} %get-tuple-element.27.own1_ref), channel_id=1, source_target_pairs={{8,16},{24,32},{40,48},{56,64},{72,80},{88,96},{104,112},{120,128}... | collective-permute-start | bytes 147464 | tf_op jit(solution)/shard_map/ppermute | solution.py:328
  5.7 0.0 copy-done.2
  5.7 0.0 copy-done.1
  5.7 0.6 pack.1
  6.3 0.0 copy-start.3
  6.4 0.0 collective-permute-done.got0_ref
  6.4 3.4 %collective-permute-done.1.got1_ref = f32[96,128]{1,0:T(8,128)S(1)} collective-permute-done((f32[96,128]{1,0:T(8,128)S(1)}, f32[96,128]{1,0:T(8,128)S(1)}, u32[]{:S(2)}, u32[]{:S(2)}) %collective-permute-start.1) | collective-permute-done | bytes 49184 | tf_op jit(solution)/shard_map/ppermute | solution.py:328
  9.7 0.1 corner.1
  9.8 0.1 collective-permute-start.2
  9.9 2.4 %collective-permute-start.3 = (f32[72,128]{1,0:T(8,128)S(1)}, f32[72,128]{1,0:T(8,128)S(1)}, u32[]{:S(2)}, u32[]{:S(2)}) collective-permute-start(f32[72,128]{1,0:T(8,128)S(1)} %get-tuple-element.31.send1_ref), channel_id=1, source_target_pairs={{1,2},{3,4},{5,6},{7,0},{2,1},{4,3},{6,5},{0,7},{9,10},{11,12},{13... | collective-permute-start | bytes 110600 | tf_op jit(solution)/shard_map/ppermute | solution.py:328
  12.3 0.5 collective-permute-done.2.side0_ref
  12.8 2.2 %collective-permute-done.3.side1_ref = f32[72,128]{1,0:T(8,128)S(1)} collective-permute-done((f32[72,128]{1,0:T(8,128)S(1)}, f32[72,128]{1,0:T(8,128)S(1)}, u32[]{:S(2)}, u32[]{:S(2)}) %collective-permute-start.3) | collective-permute-done | bytes 36896 | tf_op jit(solution)/shard_map/ppermute | solution.py:328
  15.0 6.7 %lines.1 = (f32[32,64,128]{2,1,0:T(8,128)}, f32[32,4,128]{2,1,0:T(4,128)}) custom-call(f32[32,64,128]{2,1,0:T(8,128)} %c_hbm.1, f32[32,64,128]{2,1,0:T(8,128)} %m_hbm.1, f32[32,64,64]{2,1,0:T(8,128)} %bx_hbm.1, f32[96,128]{1,0:T(8,128)S(1)} %get-tuple-element.26.own0_ref, f32[96,128]{1,0:T(8,128)S(1)} %get-tuple-element.27.own1_ref, ...), custom_call_target="tpu_custom_call" | custom-call | tf_op jit(solution)/shard_map/lines/pallas_call | solution.py:346
  21.7 12.4 %all-to-all-start = ((f32[32,4,128]{2,1,0:T(4,128)}), f32[32,4,128]{2,1,0:T(4,128)S(1)}, u32[]{:S(2)}, u32[]{:S(2)}) async-start(f32[32,4,128]{2,1,0:T(4,128)} %get-tuple-element.36), calls=%async_computation | async-start | bytes 131072 | tf_op jit(solution)/shard_map/all_to_all | solution.py:374
  34.1 0.0 copy-start.4
  34.1 0.0 copy-done
  34.1 0.0 copy-done.3
  34.2 0.7 diag.1
  34.8 3.1 %wide.1 = (f32[64,128]{1,0:T(8,128)S(1)}, f32[128,128]{1,0:T(8,128)S(1)}) custom-call(f32[32,64,128]{2,1,0:T(8,128)} %get-tuple-element.34.lin_hbm, f32[32,128,128]{2,1,0:T(8,128)} %by_hbm.1), custom_call_target="tpu_custom_call" | custom-call | tf_op jit(solution)/shard_map/wide/pallas_call | solution.py:360
  38.0 5.9 %all-to-all-done = f32[32,4,128]{2,1,0:T(4,128)S(1)} async-done(((f32[32,4,128]{2,1,0:T(4,128)}), f32[32,4,128]{2,1,0:T(4,128)S(1)}, u32[]{:S(2)}, u32[]{:S(2)}) %all-to-all-start) | async-done | bytes 65568 | tf_op jit(solution)/shard_map/all_to_all | solution.py:374
  43.9 0.2 reduced.1
  44.1 13.5 %all_to_all.15 = f32[32,4,128]{2,1,0:T(4,128)S(1)} all-to-all(f32[32,4,128]{2,1,0:T(4,128)S(1)} %bitcast.18), channel_id=1, replica_groups=mesh['gx'=32,'gy'=8] {'gx'}, dimensions={0} | all-to-all | bytes 131072 | tf_op jit(solution)/shard_map/all_to_all | solution.py:379
  57.6 0.0 copy-done.4
  57.6 1.1 %rims.1 = f32[8,64,128]{2,1,0:T(8,128)} custom-call(f32[64,128]{1,0:T(8,128)S(1)} %get-tuple-element.43.wrim_ref, f32[128,128]{1,0:T(8,128)S(1)} %bitcast.12, f32[128,128]{1,0:T(8,128)S(1)} %get-tuple-element.44.byr_ref, f32[128,64]{1,0:T(8,128)S(1)} %bitcast.15), custom_call_target="tpu_custom_call" | custom-call | tf_op jit(solution)/shard_map/rims/pallas_call | solution.py:381
  58.7 3.4 %all-to-all-start.2 = ((f32[8,64,128]{2,1,0:T(8,128)}), f32[8,64,128]{2,1,0:T(8,128)S(1)}, u32[]{:S(2)}, u32[]{:S(2)}) async-start(f32[8,64,128]{2,1,0:T(8,128)} %rims.1), calls=%async_computation.2 | async-start | bytes 524288 | tf_op jit(solution)/shard_map/all_to_all | solution.py:384
  62.1 0.0 copy-start.5
  62.1 6.7 %couple.1.u_hbm = f32[32,64,128]{2,1,0:T(8,128)} custom-call(f32[32,64,128]{2,1,0:T(8,128)} %get-tuple-element.34.lin_hbm, f32[32,128,128]{2,1,0:T(8,128)} %by_hbm.1, f32[128,128]{1,0:T(8,128)S(1)} %bitcast.13, f32[128,64]{1,0:T(8,128)S(1)} %bitcast.16), custom_call_target="tpu_custom_call" | custom-call | tf_op jit(solution)/shard_map/couple/pallas_call | solution.py:385
  68.8 0.0 all-to-all-done.2.g_ref
  68.8 3.4 %last.1 = f32[32,64,128]{2,1,0:T(8,128)} custom-call(f32[32,64,128]{2,1,0:T(8,128)} %couple.1.u_hbm, f32[8,64,128]{2,1,0:T(8,128)S(1)} %all-to-all-done.2.g_ref, bf16[128,1024]{1,0:T(8,128)(2,1)S(1)} %get-tuple-element.45.dh_ref, bf16[128,1024]{1,0:T(8,128)(2,1)S(1)} %get-tuple-element.46.dl_ref, f32[128,128]{1,0:T(8,128)S(1)} %bitcast.19), custom_call_target="tpu_custom_call" | custom-call | tf_op jit(solution)/shard_map/last/pallas_call | solution.py:394
  (4 shorter events, 0.0 us)
Async XLA Ops:
  0.0 34.1 %copy-start = (f32[32,128,128]{2,1,0:T(8,128)S(1)}, f32[32,128,128]{2,1,0:T(8,128)}, u32[]{:S(2)}) copy-start(f32[32,128,128]{2,1,0:T(8,128)} %param.12) | copy-start | bytes 6291460
  0.0 5.7 %copy-start.2 = (f32[32,64,128]{2,1,0:T(8,128)S(1)}, f32[32,64,128]{2,1,0:T(8,128)}, u32[]{:S(2)}) copy-start(f32[32,64,128]{2,1,0:T(8,128)} %m_hbm.1) | copy-start | bytes 3145732
  0.0 5.7 %copy-start.1 = (f32[32,64,128]{2,1,0:T(8,128)S(1)}, f32[32,64,128]{2,1,0:T(8,128)}, u32[]{:S(2)}) copy-start(f32[32,64,128]{2,1,0:T(8,128)} %c_hbm.1) | copy-start | bytes 3145732
  1.4 5.0 %collective-permute-start = (f32[96,128]{1,0:T(8,128)S(1)}, f32[96,128]{1,0:T(8,128)S(1)}, u32[]{:S(2)}, u32[]{:S(2)}) collective-permute-start(f32[96,128]{1,0:T(8,128)S(1)} %get-tuple-element.26.own0_ref), channel_id=1, source_target_pairs={{0,8},{16,24},{32,40},{48,56},{64,72},{80,88},{96,104},{112,120},{... | collective-permute-start | bytes 147464 | tf_op jit(solution)/shard_map/ppermute | solution.py:328
  4.7 5.0 %collective-permute-start.1 = (f32[96,128]{1,0:T(8,128)S(1)}, f32[96,128]{1,0:T(8,128)S(1)}, u32[]{:S(2)}, u32[]{:S(2)}) collective-permute-start(f32[96,128]{1,0:T(8,128)S(1)} %get-tuple-element.27.own1_ref), channel_id=1, source_target_pairs={{8,16},{24,32},{40,48},{56,64},{72,80},{88,96},{104,112},{120,128}... | collective-permute-start | bytes 147464 | tf_op jit(solution)/shard_map/ppermute | solution.py:328
  6.3 27.8 %copy-start.3 = (f32[32,32,32]{2,1,0:T(8,128)S(1)}, f32[32,32,32]{2,1,0:T(8,128)}, u32[]{:S(2)}) copy-start(f32[32,32,32]{2,1,0:T(8,128)} %param.15) | copy-start | bytes 393220
  9.8 3.0 %collective-permute-start.2 = (f32[72,128]{1,0:T(8,128)S(1)}, f32[72,128]{1,0:T(8,128)S(1)}, u32[]{:S(2)}, u32[]{:S(2)}) collective-permute-start(f32[72,128]{1,0:T(8,128)S(1)} %get-tuple-element.30.send0_ref), channel_id=1, source_target_pairs={{0,1},{2,3},{4,5},{6,7},{1,0},{3,2},{5,4},{7,6},{8,9},{10,11},{12,... | collective-permute-start | bytes 110600 | tf_op jit(solution)/shard_map/ppermute | solution.py:328
  9.9 5.0 %collective-permute-start.3 = (f32[72,128]{1,0:T(8,128)S(1)}, f32[72,128]{1,0:T(8,128)S(1)}, u32[]{:S(2)}, u32[]{:S(2)}) collective-permute-start(f32[72,128]{1,0:T(8,128)S(1)} %get-tuple-element.31.send1_ref), channel_id=1, source_target_pairs={{1,2},{3,4},{5,6},{7,0},{2,1},{4,3},{6,5},{0,7},{9,10},{11,12},{13... | collective-permute-start | bytes 110600 | tf_op jit(solution)/shard_map/ppermute | solution.py:328
  21.7 22.3 %all-to-all-start = ((f32[32,4,128]{2,1,0:T(4,128)}), f32[32,4,128]{2,1,0:T(4,128)S(1)}, u32[]{:S(2)}, u32[]{:S(2)}) async-start(f32[32,4,128]{2,1,0:T(4,128)} %get-tuple-element.36), calls=%async_computation | async-start | bytes 131072 | tf_op jit(solution)/shard_map/all_to_all | solution.py:374
  34.1 23.5 %copy-start.4 = (f32[32,64,4]{1,2,0:T(4,128)S(1)}, f32[32,64,4]{1,2,0:T(4,128)}, u32[]{:S(2)}) copy-start(f32[32,64,4]{1,2,0:T(4,128)} %param.11) | copy-start | bytes 98308
  58.7 10.1 %all-to-all-start.2 = ((f32[8,64,128]{2,1,0:T(8,128)}), f32[8,64,128]{2,1,0:T(8,128)S(1)}, u32[]{:S(2)}, u32[]{:S(2)}) async-start(f32[8,64,128]{2,1,0:T(8,128)} %rims.1), calls=%async_computation.2 | async-start | bytes 524288 | tf_op jit(solution)/shard_map/all_to_all | solution.py:384
  62.1 6.7 %copy-start.5 = (f32[32,128,4]{1,2,0:T(4,128)S(1)}, f32[32,128,4]{1,2,0:T(4,128)}, u32[]{:S(2)}) copy-start(f32[32,128,4]{1,2,0:T(4,128)} %param.14) | copy-start | bytes 196612

commit v4 on v3

--- a/solution.py
+++ b/solution.py
@@ -6,7 +6,7 @@
 from jax.sharding import PartitionSpec as P
 
 NZ, CX, CY = 32, 64, 128
-STEP = 4
+STEP = 8
 F32, BF16 = jnp.float32, jnp.bfloat16
 CALL = pltpu.CompilerParams(vmem_limit_bytes=12 * 1024 * 1024)
 
@@ -67,8 +67,8 @@
         second_ref[NZ * k:NZ * (k + 1)] = jnp.where(odd, hi, lo)
 
 
-def pack_kernel(c_ref, m_ref, first_ref, second_ref):
-    lane = iota((CX, CY), 1)
+def pack_kernel(c_ref, m_ref, first_ref, second_ref, mu_hbm, mob_hbm, mu_ref, mob_ref, sems):
+    row, lane = iota((CX, CY), 0), iota((CX, CY), 1)
     lo = jnp.zeros((CX, CY), F32)
     hi = jnp.zeros((CX, CY), F32)
     for z in range(NZ):
@@ -83,6 +83,25 @@
     first_ref[...] = jnp.where(odd, lo, hi)
     second_ref[...] = jnp.where(odd, hi, lo)
 
+    def step(g, carry):
+        for i in range(STEP):
+            z = g * STEP + i
+            c = c_ref[z]
+            up = jnp.where(row == 0, 0.0, roll(c, 1, 0))
+            down = jnp.where(row == CX - 1, 0.0, roll(c, -1, 0))
+            lf = jnp.where(lane == 0, 0.0, roll(c, 1, 1))
+            rt = jnp.where(lane == CY - 1, 0.0, roll(c, -1, 1))
+            mu_ref[z] = potential(c, up + down + lf + rt - 4.0 * c)
+            mob_ref[z] = mobile(m_ref[z], c)
+        piece(mu_ref, mu_hbm, sems.at[0], g).start()
+        piece(mob_ref, mob_hbm, sems.at[1], g).start()
+        return carry
+
+    lax.fori_loop(0, NZ // STEP, step, 0)
+    for g in range(NZ // STEP):
+        piece(mu_ref, mu_hbm, sems.at[0], g).wait()
+        piece(mob_ref, mob_hbm, sems.at[1], g).wait()
+
 
 def corner_kernel(side0_ref, side1_ref, got0_ref, got1_ref, first_ref, second_ref):
     sub, lane = iota((NZ, CY), 0), iota((NZ, CY), 1)
@@ -107,12 +126,12 @@
     return pltpu.make_async_copy(src.at[at], dst.at[at], sems.at[g])
 
 
-def lines_kernel(c_hbm, m_hbm, bx_hbm, own0_ref, own1_ref, send0_ref, send1_ref, side0_ref, side1_ref, got0_ref,
-                 got1_ref, lin_hbm, rim_ref, c_ref, m_ref, bx_ref, lin_ref, ch, fh, mul, mobl, mur, mobr, slo_ref,
+def lines_kernel(c_hbm, mu_hbm, mob_hbm, bx_hbm, own0_ref, own1_ref, send0_ref, send1_ref, side0_ref, side1_ref, got0_ref,
+                 got1_ref, lin_hbm, rim_ref, c_ref, mu_ref, mob_ref, bx_ref, lin_ref, ch, fh, mul, mobl, mur, mobr, slo_ref,
                  shi_ref, yl_ref, yr_ref, xl_ref, xr_ref, sems):
-    row = iota((CX, CY), 0)
+    row, row8 = iota((CX, CY), 0), iota((8, CY), 0)
     lane = iota((CX, CY), 1)
-    loads = ((c_hbm, c_ref), (m_hbm, m_ref), (bx_hbm, bx_ref))
+    loads = ((c_hbm, c_ref), (mu_hbm, mu_ref), (mob_hbm, mob_ref), (bx_hbm, bx_ref))
     for g in range(NZ // STEP):
         for k, (src, dst) in enumerate(loads):
             piece(src, dst, sems.at[k], g).start()
@@ -138,12 +157,12 @@
         cm1, cm2, mm1 = roll(left, 1, 1), roll(left, 2, 1), roll(left, -1, 1)
         mu0 = potential(c0, cm1 + c1 + around(lo, slo_ref) - 4.0 * c0)
         mum1 = potential(cm1, cm2 + c0 + roll(around(left, yl_ref), 1, 1) - 4.0 * cm1)
-        flux_l = 0.5 * (mobile(mm1, cm1) + mobile(m0, c0)) * (mu0 - mum1)
+        flux_l = (mobile(mm1, cm1) + mobile(m0, c0)) * (mu0 - mum1)
         cn, cn1, mn = hi, roll(hi, 1, 1), roll(hi, -2, 1)
         cp, cp2, mp = roll(right, -1, 1), roll(right, -2, 1), roll(right, -3, 1)
         mun = potential(cn, cn1 + cp + around(hi, shi_ref) - 4.0 * cn)
         mup = potential(cp, cn + cp2 + roll(around(right, yr_ref), -1, 1) - 4.0 * cp)
-        flux_r = 0.5 * (mobile(mp, cp) + mobile(mn, cn)) * (mup - mun)
+        flux_r = (mobile(mp, cp) + mobile(mn, cn)) * (mup - mun)
         first = (lane & 3) == 0
         fh[...] = jnp.where(first, flux_l, flux_r)
         ch[...] = jnp.where(first, cm1, cp)
@@ -169,30 +188,30 @@
             piece(src, dst, sems.at[k], g).wait()
         for i in range(STEP):
             plane(g * STEP + i)
-        piece(lin_ref, lin_hbm, sems.at[3], g).start()
+        piece(lin_ref, lin_hbm, sems.at[4], g).start()
         return carry
 
     def plane(z):
         at = pl.ds(z, 1)
         turn = (CY - 4 * z) & (CY - 1)
-        c = c_ref[z]
+        c, mob = c_ref[z], mob_ref[z]
         hz = roll(ch[...], turn, 1)
         fz = roll(fh[...], turn, 1)
-        up = jnp.where(row == 0, xl_ref[at], roll(c, 1, 0))
-        down = jnp.where(row == CX - 1, xr_ref[at], roll(c, -1, 0))
-        lf = jnp.where(lane == 0, hz, roll(c, 1, 1))
-        rt = jnp.where(lane == CY - 1, hz, roll(c, -1, 1))
-        mu = potential(c, up + down + lf + rt - 4.0 * c)
-        mob = mobile(m_ref[z], c)
+        mu = mu_ref[z] - jnp.where((lane == 0) | (lane == CY - 1), hz, 0.0)
+        mu = jnp.concatenate([
+            mu[0:8] - jnp.where(row8 == 0, xl_ref[at], 0.0),
+            mu[8:CX - 8],
+            mu[CX - 8:CX] - jnp.where(row8 == 7, xr_ref[at], 0.0),
+        ])
         mu_d = jnp.where(row == CX - 1, mur[at], roll(mu, -1, 0))
         mob_d = jnp.where(row == CX - 1, mobr[at], roll(mob, -1, 0))
-        fx = 0.5 * (mob_d + mob) * (mu_d - mu)
-        f0 = 0.5 * (mob[0:1] + mobl[at]) * (mu[0:1] - mul[at])
+        fx = (mob_d + mob) * (mu_d - mu)
+        f0 = (mob[0:1] + mobl[at]) * (mu[0:1] - mul[at])
         fx_up = jnp.where(row == 0, f0, roll(fx, 1, 0))
-        fy = 0.5 * (roll(mob, -1, 1) + mob) * (roll(mu, -1, 1) - mu)
+        fy = (roll(mob, -1, 1) + mob) * (roll(mu, -1, 1) - mu)
         fy = jnp.where(lane == CY - 1, fz, fy)
         fy_lf = jnp.where(lane == 0, fz, roll(fy, 1, 1))
-        rhs = c + 0.02 * ((fx - fx_up) + (fy - fy_lf))
+        rhs = c + 0.01 * ((fx - fx_up) + (fy - fy_lf))
         lin = dot3(bx_ref[z], rhs, ((1,), (0,)))
         lin_ref[z] = lin
         rim_ref[z, 0:2] = lin[0:2]
@@ -200,7 +219,7 @@
 
     lax.fori_loop(0, NZ // STEP, step, 0)
     for g in range(NZ // STEP):
-        piece(lin_ref, lin_hbm, sems.at[3], g).wait()
+        piece(lin_ref, lin_hbm, sems.at[4], g).wait()
 
 
 def reduced_kernel(r_ref, rim_ref, out_ref):
@@ -269,18 +288,21 @@
         piece(by_hbm, by, sems.at[1], g).start()
     spikes[...] = jnp.transpose(sx_ref[...])
 
-    def step(g, carry):
-        fix = dot3(spread(spikes[...], g), cx_ref[...], ((1,), (0,)))
-        piece(lin_hbm, lin, sems.at[0], g).wait()
-        piece(by_hbm, by, sems.at[1], g).wait()
-        for i in range(STEP):
-            z = STEP * g + i
-            v = lin[z] - fix[CX * i:CX * (i + 1)]
-            u[z] = dot3(v, by[z], ((1,), (1,)))
-        piece(u, u_hbm, sems.at[2], g).start()
+    def step(h, carry):
+        for g in (2 * h, 2 * h + 1):
+            fix = dot3(spread(spikes[...], g), cx_ref[...], ((1,), (0,)))
+            piece(lin_hbm, lin, sems.at[0], g).wait()
+            piece(by_hbm, by, sems.at[1], g).wait()
+            for i in range(STEP):
+                z = STEP * g + i
+                vs = jnp.concatenate(halves(lin[z] - fix[CX * i:CX * (i + 1)]))
+                bs = jnp.concatenate(halves(by[z]))
+                all_ = lax.dot_general(vs, bs, (((1,), (1,)), ((), ())), preferred_element_type=F32)
+                u[z] = all_[:CX, :CY] + (all_[:CX, CY:] + all_[CX:, :CY])
+            piece(u, u_hbm, sems.at[2], g).start()
         return carry
 
-    lax.fori_loop(0, NZ // STEP, step, 0)
+    lax.fori_loop(0, NZ // STEP // 2, step, 0)
     for g in range(NZ // STEP):
         piece(u, u_hbm, sems.at[2], g).wait()
 
@@ -335,8 +357,13 @@
         compiler_params=CALL, name="edge",
     )(hbm(conc), hbm(mobility))
     got0, got1 = swap(own0, own1, "gx", nx)
-    side = pl.pallas_call(
-        pack_kernel, out_shape=(shape(CX, CY),) * 2, compiler_params=CALL, name="pack"
+    *side, mu, mob = pl.pallas_call(
+        pack_kernel,
+        in_specs=[here, here],
+        out_specs=(here, here, any_space, any_space),
+        out_shape=(shape(CX, CY), shape(CX, CY), big_hbm, big_hbm),
+        scratch_shapes=[full(NZ, CX, CY)] * 2 + [pltpu.SemaphoreType.DMA((2, groups))],
+        compiler_params=CALL, name="pack",
     )(conc, mobility)
     send0, send1 = pl.pallas_call(
         corner_kernel, out_shape=(shape(72, CY),) * 2, compiler_params=CALL, name="corner"
@@ -345,14 +372,14 @@
 
     lin, rims = pl.pallas_call(
         lines_kernel,
-        in_specs=[any_space] * 3 + [here] * 8,
+        in_specs=[any_space] * 4 + [here] * 8,
         out_specs=(any_space, here),
         out_shape=(big_hbm, shape(NZ, 4, CY)),
-        scratch_shapes=[full(NZ, CX, CY), full(NZ, CX, CY), full(NZ, CX, CX), full(NZ, CX, CY)]
+        scratch_shapes=[full(NZ, CX, CY)] * 3 + [full(NZ, CX, CX), full(NZ, CX, CY)]
         + [full(CX, CY)] * 2 + [full(NZ, CY)] * 4 + [full(72, CY)] * 4 + [full(3 * NZ, CY)] * 2
-        + [pltpu.SemaphoreType.DMA((4, groups))],
+        + [pltpu.SemaphoreType.DMA((5, groups))],
         compiler_params=CALL, name="lines",
-    )(hbm(conc), hbm(mobility), hbm(block_x), own0, own1, send0, send1, side0, side1, got0, got1)
+    )(hbm(conc), hbm(mu), hbm(mob), hbm(block_x), own0, own1, send0, send1, side0, side1, got0, got1)
 
     lin, rims, block_y, reduced_y = lax.optimization_barrier((lin, rims, block_y, reduced_y))
     sx = jnp.transpose(spike_x, (0, 2, 1)).reshape(4 * NZ, CX)
@@ -372,7 +399,7 @@
 
     mine = lax.dynamic_index_in_dim(reduced_x, p, 0, keepdims=False)
     rims = lax.all_to_all(rims, "gx", 0, 0, tiled=True)
-    rims, wrim, dh, dl, mine = lax.optimization_barrier((rims, wrim, dh, dl, mine))
+    rims, wrim, mine = lax.optimization_barrier((rims, wrim, mine))
     solved = pl.pallas_call(
         reduced_kernel, out_shape=shape(4 * NZ, CY), compiler_params=CALL, name="reduced"
     )(mine, rims.reshape(4 * NZ, CY))

time: 72.5 us -> 69.8 us (0.963)
  Pallas kernels: 23.9 us -> 20.6 us
  waiting for transfers between devices: 11.9 us -> 13 us
    pallas_call x1, Pallas kernels: 6.66 us -> 3.93 us  [body(): pl.pallas_call(couple_kernel, in_specs=[any_space, any_space, here, here]...]
    ppermute x2, waiting for transfers between devices: 5.53 us -> 3.83 us  [swap(): lax.ppermute(second, axis, pairs(n, 1))]
    all_to_all x1, waiting for transfers between devices: 0.01 us -> 1.56 us  [body(): yall = lax.all_to_all(yrim, 'gy', 0, 0, tiled=True)]
    all_to_all x1, waiting for transfers between devices: 5.95 us -> 7.17 us  [body(): rims = lax.all_to_all(rims, 'gx', 0, 0, tiled=True)]
  transfers between devices with their start and end apart: 6 -> 6, of which waited for: 4 -> 5; matrix products, arithmetic and copies ran while one was open for 0% -> 0% of each run, Pallas kernels for 15% -> 14%
where the time goes in v4:
time: 69.8 us; the launch traced here: 69.5 us
  starting transfers between devices  22.8 us (33%)
  Pallas kernels  20.6 us (30%)
  waiting for transfers between devices  13 us (19%)
  blocking collectives  12.9 us (18%)
    all_to_all x1, blocking collectives, body(): lax.all_to_all(solved.reshape(NZ, 4, CY), 'gx', 0, 0, tiled=True)  12.9 us
    all_to_all x1, starting transfers between devices, body(): rims = lax.all_to_all(rims, 'gx', 0, 0, tiled=True)  12.6 us
    all_to_all x1, waiting for transfers between devices, body(): rims = lax.all_to_all(rims, 'gx', 0, 0, tiled=True)  7.17 us
    pallas_call x1, Pallas kernels, body(): pl.pallas_call(lines_kernel, in_specs=[any_space] * 4 + [here] * 8, out_s...  5.52 us
    pallas_call x1, Pallas kernels, body(): pl.pallas_call(couple_kernel, in_specs=[any_space, any_space, here, here]...  3.93 us
    ppermute x2, waiting for transfers between devices, swap(): lax.ppermute(second, axis, pairs(n, 1))  3.83 us
    all_to_all x1, starting transfers between devices, body(): yall = lax.all_to_all(yrim, 'gy', 0, 0, tiled=True)  3.42 us
    ppermute x2, starting transfers between devices, swap(): lax.ppermute(first, axis, pairs(n, 0))  3.41 us
  transfers between devices with their start and end apart: 6, of which 5 were waited for; matrix products, arithmetic and copies ran while one was open for 0% of the time, Pallas kernels for 14%

profile of v4, /device:TPU:1, one launch (start us, length us, event | category | flops | bytes accessed | tf_op | source)
XLA Modules:
  0.0 69.5 jit_solution(6550540615213022198)
XLA Ops:
  0.0 0.0 copy-start
  0.0 1.4 %edge.1 = (f32[96,128]{1,0:T(8,128)S(1)}, f32[96,128]{1,0:T(8,128)S(1)}) custom-call(f32[32,64,128]{2,1,0:T(8,128)} %c_hbm.1, f32[32,64,128]{2,1,0:T(8,128)} %m_ref.3), custom_call_target="tpu_custom_call" | custom-call | tf_op jit(solution)/shard_map/edge/pallas_call | solution.py:352
  1.4 3.3 %collective-permute-start = (f32[96,128]{1,0:T(8,128)S(1)}, f32[96,128]{1,0:T(8,128)S(1)}, u32[]{:S(2)}, u32[]{:S(2)}) collective-permute-start(f32[96,128]{1,0:T(8,128)S(1)} %get-tuple-element.28.own0_ref), channel_id=1, source_target_pairs={{0,8},{16,24},{32,40},{48,56},{64,72},{80,88},{96,104},{112,120},{... | collective-permute-start | bytes 147464 | tf_op jit(solution)/shard_map/ppermute | solution.py:350
  4.7 1.0 %collective-permute-start.1 = (f32[96,128]{1,0:T(8,128)S(1)}, f32[96,128]{1,0:T(8,128)S(1)}, u32[]{:S(2)}, u32[]{:S(2)}) collective-permute-start(f32[96,128]{1,0:T(8,128)S(1)} %get-tuple-element.29.own1_ref), channel_id=1, source_target_pairs={{8,16},{24,32},{40,48},{56,64},{72,80},{88,96},{104,112},{120,128}... | collective-permute-start | bytes 147464 | tf_op jit(solution)/shard_map/ppermute | solution.py:350
  5.7 0.0 copy-done.1
  5.7 0.0 copy-done.2
  5.7 2.3 %pack.1 = (f32[64,128]{1,0:T(8,128)S(1)}, f32[64,128]{1,0:T(8,128)S(1)}, f32[32,64,128]{2,1,0:T(8,128)}, f32[32,64,128]{2,1,0:T(8,128)}) custom-call(f32[32,64,128]{2,1,0:T(8,128)S(1)} %copy-done.1, f32[32,64,128]{2,1,0:T(8,128)S(1)} %copy-done.2), custom_call_target="tpu_custom_call" | custom-call | tf_op jit(solution)/shard_map/pack/pallas_call | solution.py:360
  8.1 0.0 collective-permute-done.got0_ref
  8.1 1.7 %collective-permute-done.1.got1_ref = f32[96,128]{1,0:T(8,128)S(1)} collective-permute-done((f32[96,128]{1,0:T(8,128)S(1)}, f32[96,128]{1,0:T(8,128)S(1)}, u32[]{:S(2)}, u32[]{:S(2)}) %collective-permute-start.1) | collective-permute-done | bytes 49184 | tf_op jit(solution)/shard_map/ppermute | solution.py:350
  9.7 0.1 corner.1
  9.8 0.1 collective-permute-start.2
  9.9 2.4 %collective-permute-start.3 = (f32[72,128]{1,0:T(8,128)S(1)}, f32[72,128]{1,0:T(8,128)S(1)}, u32[]{:S(2)}, u32[]{:S(2)}) collective-permute-start(f32[72,128]{1,0:T(8,128)S(1)} %get-tuple-element.33.send1_ref), channel_id=1, source_target_pairs={{1,2},{3,4},{5,6},{7,0},{2,1},{4,3},{6,5},{0,7},{9,10},{11,12},{13... | collective-permute-start | bytes 110600 | tf_op jit(solution)/shard_map/ppermute | solution.py:350
  12.3 0.5 collective-permute-done.2.side0_ref
  12.8 2.2 %collective-permute-done.3.side1_ref = f32[72,128]{1,0:T(8,128)S(1)} collective-permute-done((f32[72,128]{1,0:T(8,128)S(1)}, f32[72,128]{1,0:T(8,128)S(1)}, u32[]{:S(2)}, u32[]{:S(2)}) %collective-permute-start.3) | collective-permute-done | bytes 36896 | tf_op jit(solution)/shard_map/ppermute | solution.py:350
  15.0 5.5 %lines.1 = (f32[32,64,128]{2,1,0:T(8,128)}, f32[32,4,128]{2,1,0:T(4,128)}) custom-call(f32[32,64,128]{2,1,0:T(8,128)} %c_hbm.1, f32[32,64,128]{2,1,0:T(8,128)} %get-tuple-element.26.mu_hbm, f32[32,64,128]{2,1,0:T(8,128)} %get-tuple-element.27.mob_hbm, f32[32,64,64]{2,1,0:T(8,128)} %bx_hbm.1, f32[96,128]{1,0:T(8,128)S(1)} %get-tuple-element.28.own0_ref, ...), custom_call_target="tpu_custom_call" | custom-call | tf_op jit(solution)/shard_map/lines/pallas_call | solution.py:373
  20.5 0.0 copy-start.4
  20.5 12.6 %all-to-all-start = ((f32[32,4,128]{2,1,0:T(4,128)}), f32[32,4,128]{2,1,0:T(4,128)S(1)}, u32[]{:S(2)}, u32[]{:S(2)}) async-start(f32[32,4,128]{2,1,0:T(4,128)} %get-tuple-element.38), calls=%async_computation | async-start | bytes 131072 | tf_op jit(solution)/shard_map/all_to_all | solution.py:401
  33.1 0.0 copy-done
  33.1 0.0 copy-start.3
  33.1 2.6 %wide.1 = (f32[64,128]{1,0:T(8,128)S(1)}, f32[128,128]{1,0:T(8,128)S(1)}) custom-call(f32[32,64,128]{2,1,0:T(8,128)} %get-tuple-element.36.lin_hbm, f32[32,128,128]{2,1,0:T(8,128)} %by_hbm.1), custom_call_target="tpu_custom_call" | custom-call | tf_op jit(solution)/shard_map/wide/pallas_call | solution.py:387
  35.7 7.2 %all-to-all-done = f32[32,4,128]{2,1,0:T(4,128)S(1)} async-done(((f32[32,4,128]{2,1,0:T(4,128)}), f32[32,4,128]{2,1,0:T(4,128)S(1)}, u32[]{:S(2)}, u32[]{:S(2)}) %all-to-all-start) | async-done | bytes 65568 | tf_op jit(solution)/shard_map/all_to_all | solution.py:401
  42.9 0.2 reduced.1
  43.1 12.9 %all_to_all.15 = f32[32,4,128]{2,1,0:T(4,128)S(1)} all-to-all(f32[32,4,128]{2,1,0:T(4,128)S(1)} %bitcast.18), channel_id=1, replica_groups=mesh['gx'=32,'gy'=8] {'gx'}, dimensions={0} | all-to-all | bytes 131072 | tf_op jit(solution)/shard_map/all_to_all | solution.py:406
  56.0 1.1 %rims.1 = f32[8,64,128]{2,1,0:T(8,128)} custom-call(f32[64,128]{1,0:T(8,128)S(1)} %get-tuple-element.42.wrim_ref, f32[128,128]{1,0:T(8,128)S(1)} %bitcast.12, f32[128,128]{1,0:T(8,128)S(1)} %get-tuple-element.43.byr_ref, f32[128,64]{1,0:T(8,128)S(1)} %bitcast.15), custom_call_target="tpu_custom_call" | custom-call | tf_op jit(solution)/shard_map/rims/pallas_call | solution.py:408
  57.1 3.4 %all-to-all-start.2 = ((f32[8,64,128]{2,1,0:T(8,128)}), f32[8,64,128]{2,1,0:T(8,128)S(1)}, u32[]{:S(2)}, u32[]{:S(2)}) async-start(f32[8,64,128]{2,1,0:T(8,128)} %rims.1), calls=%async_computation.2 | async-start | bytes 524288 | tf_op jit(solution)/shard_map/all_to_all | solution.py:411
  60.5 0.0 copy-done.3
  60.5 0.7 diag.1
  61.2 0.0 copy-start.5
  61.2 3.9 %couple.1.u_hbm = f32[32,64,128]{2,1,0:T(8,128)} custom-call(f32[32,64,128]{2,1,0:T(8,128)} %get-tuple-element.36.lin_hbm, f32[32,128,128]{2,1,0:T(8,128)} %by_hbm.1, f32[128,128]{1,0:T(8,128)S(1)} %bitcast.13, f32[128,64]{1,0:T(8,128)S(1)} %bitcast.16), custom_call_target="tpu_custom_call" | custom-call | tf_op jit(solution)/shard_map/couple/pallas_call | solution.py:412
  65.1 1.6 %all-to-all-done.2.g_ref = f32[8,64,128]{2,1,0:T(8,128)S(1)} async-done(((f32[8,64,128]{2,1,0:T(8,128)}), f32[8,64,128]{2,1,0:T(8,128)S(1)}, u32[]{:S(2)}, u32[]{:S(2)}) %all-to-all-start.2) | async-done | bytes 262176 | tf_op jit(solution)/shard_map/all_to_all | solution.py:411
  66.7 0.0 copy-done.5
  66.7 2.8 %last.1 = f32[32,64,128]{2,1,0:T(8,128)} custom-call(f32[32,64,128]{2,1,0:T(8,128)} %couple.1.u_hbm, f32[8,64,128]{2,1,0:T(8,128)S(1)} %all-to-all-done.2.g_ref, bf16[128,1024]{1,0:T(8,128)(2,1)S(1)} %get-tuple-element.45.dh_ref, bf16[128,1024]{1,0:T(8,128)(2,1)S(1)} %get-tuple-element.46.dl_ref, f32[128,128]{1,0:T(8,128)S(1)} %bitcast.19), custom_call_target="tpu_custom_call" | custom-call | tf_op jit(solution)/shard_map/last/pallas_call | solution.py:421
  (4 shorter events, 0.0 us)
Async XLA Ops:
  0.0 33.1 %copy-start = (f32[32,128,128]{2,1,0:T(8,128)S(1)}, f32[32,128,128]{2,1,0:T(8,128)}, u32[]{:S(2)}) copy-start(f32[32,128,128]{2,1,0:T(8,128)} %param.12) | copy-start | bytes 6291460
  0.0 5.7 %copy-start.1 = (f32[32,64,128]{2,1,0:T(8,128)S(1)}, f32[32,64,128]{2,1,0:T(8,128)}, u32[]{:S(2)}) copy-start(f32[32,64,128]{2,1,0:T(8,128)} %c_hbm.1) | copy-start | bytes 3145732
  0.0 5.7 %copy-start.2 = (f32[32,64,128]{2,1,0:T(8,128)S(1)}, f32[32,64,128]{2,1,0:T(8,128)}, u32[]{:S(2)}) copy-start(f32[32,64,128]{2,1,0:T(8,128)} %m_ref.3) | copy-start | bytes 3145732
  1.4 6.7 %collective-permute-start = (f32[96,128]{1,0:T(8,128)S(1)}, f32[96,128]{1,0:T(8,128)S(1)}, u32[]{:S(2)}, u32[]{:S(2)}) collective-permute-start(f32[96,128]{1,0:T(8,128)S(1)} %get-tuple-element.28.own0_ref), channel_id=1, source_target_pairs={{0,8},{16,24},{32,40},{48,56},{64,72},{80,88},{96,104},{112,120},{... | collective-permute-start | bytes 147464 | tf_op jit(solution)/shard_map/ppermute | solution.py:350
  4.7 5.0 %collective-permute-start.1 = (f32[96,128]{1,0:T(8,128)S(1)}, f32[96,128]{1,0:T(8,128)S(1)}, u32[]{:S(2)}, u32[]{:S(2)}) collective-permute-start(f32[96,128]{1,0:T(8,128)S(1)} %get-tuple-element.29.own1_ref), channel_id=1, source_target_pairs={{8,16},{24,32},{40,48},{56,64},{72,80},{88,96},{104,112},{120,128}... | collective-permute-start | bytes 147464 | tf_op jit(solution)/shard_map/ppermute | solution.py:350
  9.8 2.9 %collective-permute-start.2 = (f32[72,128]{1,0:T(8,128)S(1)}, f32[72,128]{1,0:T(8,128)S(1)}, u32[]{:S(2)}, u32[]{:S(2)}) collective-permute-start(f32[72,128]{1,0:T(8,128)S(1)} %get-tuple-element.32.send0_ref), channel_id=1, source_target_pairs={{0,1},{2,3},{4,5},{6,7},{1,0},{3,2},{5,4},{7,6},{8,9},{10,11},{12,... | collective-permute-start | bytes 110600 | tf_op jit(solution)/shard_map/ppermute | solution.py:350
  9.9 5.0 %collective-permute-start.3 = (f32[72,128]{1,0:T(8,128)S(1)}, f32[72,128]{1,0:T(8,128)S(1)}, u32[]{:S(2)}, u32[]{:S(2)}) collective-permute-start(f32[72,128]{1,0:T(8,128)S(1)} %get-tuple-element.33.send1_ref), channel_id=1, source_target_pairs={{1,2},{3,4},{5,6},{7,0},{2,1},{4,3},{6,5},{0,7},{9,10},{11,12},{13... | collective-permute-start | bytes 110600 | tf_op jit(solution)/shard_map/ppermute | solution.py:350
  20.5 35.5 %copy-start.4 = (f32[32,64,4]{1,2,0:T(4,128)S(1)}, f32[32,64,4]{1,2,0:T(4,128)}, u32[]{:S(2)}) copy-start(f32[32,64,4]{1,2,0:T(4,128)} %param.11) | copy-start | bytes 98308
  20.5 22.4 %all-to-all-start = ((f32[32,4,128]{2,1,0:T(4,128)}), f32[32,4,128]{2,1,0:T(4,128)S(1)}, u32[]{:S(2)}, u32[]{:S(2)}) async-start(f32[32,4,128]{2,1,0:T(4,128)} %get-tuple-element.38), calls=%async_computation | async-start | bytes 131072 | tf_op jit(solution)/shard_map/all_to_all | solution.py:401
  33.1 27.4 %copy-start.3 = (f32[32,32,32]{2,1,0:T(8,128)S(1)}, f32[32,32,32]{2,1,0:T(8,128)}, u32[]{:S(2)}) copy-start(f32[32,32,32]{2,1,0:T(8,128)} %param.15) | copy-start | bytes 393220
  57.1 9.6 %all-to-all-start.2 = ((f32[8,64,128]{2,1,0:T(8,128)}), f32[8,64,128]{2,1,0:T(8,128)S(1)}, u32[]{:S(2)}, u32[]{:S(2)}) async-start(f32[8,64,128]{2,1,0:T(8,128)} %rims.1), calls=%async_computation.2 | async-start | bytes 524288 | tf_op jit(solution)/shard_map/all_to_all | solution.py:411
  61.2 5.5 %copy-start.5 = (f32[32,128,4]{1,2,0:T(4,128)S(1)}, f32[32,128,4]{1,2,0:T(4,128)}, u32[]{:S(2)}) copy-start(f32[32,128,4]{1,2,0:T(4,128)} %param.14) | copy-start | bytes 196612

commit v5 on v4

--- a/solution.py
+++ b/solution.py
@@ -6,7 +6,7 @@
 from jax.sharding import PartitionSpec as P
 
 NZ, CX, CY = 32, 64, 128
-STEP = 8
+STEP, HALF = 8, 4
 F32, BF16 = jnp.float32, jnp.bfloat16
 CALL = pltpu.CompilerParams(vmem_limit_bytes=12 * 1024 * 1024)
 
@@ -67,7 +67,7 @@
         second_ref[NZ * k:NZ * (k + 1)] = jnp.where(odd, hi, lo)
 
 
-def pack_kernel(c_ref, m_ref, first_ref, second_ref, mu_hbm, mob_hbm, mu_ref, mob_ref, sems):
+def pack_kernel(c_ref, m_ref, first_ref, second_ref, mu_ref, mobx_ref, moby_ref):
     row, lane = iota((CX, CY), 0), iota((CX, CY), 1)
     lo = jnp.zeros((CX, CY), F32)
     hi = jnp.zeros((CX, CY), F32)
@@ -92,15 +92,12 @@
             lf = jnp.where(lane == 0, 0.0, roll(c, 1, 1))
             rt = jnp.where(lane == CY - 1, 0.0, roll(c, -1, 1))
             mu_ref[z] = potential(c, up + down + lf + rt - 4.0 * c)
-            mob_ref[z] = mobile(m_ref[z], c)
-        piece(mu_ref, mu_hbm, sems.at[0], g).start()
-        piece(mob_ref, mob_hbm, sems.at[1], g).start()
+            mob = mobile(m_ref[z], c)
+            mobx_ref[z] = mob + roll(mob, -1, 0)
+            moby_ref[z] = mob + roll(mob, -1, 1)
         return carry
 
     lax.fori_loop(0, NZ // STEP, step, 0)
-    for g in range(NZ // STEP):
-        piece(mu_ref, mu_hbm, sems.at[0], g).wait()
-        piece(mob_ref, mob_hbm, sems.at[1], g).wait()
 
 
 def corner_kernel(side0_ref, side1_ref, got0_ref, got1_ref, first_ref, second_ref):
@@ -121,20 +118,16 @@
     second_ref[CX:72] = jnp.where(odd_y, hi, lo)
 
 
-def piece(src, dst, sems, g):
-    at = pl.ds(g * STEP, STEP)
+def piece(src, dst, sems, g, size=STEP):
+    at = pl.ds(g * size, size)
     return pltpu.make_async_copy(src.at[at], dst.at[at], sems.at[g])
 
 
-def lines_kernel(c_hbm, mu_hbm, mob_hbm, bx_hbm, own0_ref, own1_ref, send0_ref, send1_ref, side0_ref, side1_ref, got0_ref,
-                 got1_ref, lin_hbm, rim_ref, c_ref, mu_ref, mob_ref, bx_ref, lin_ref, ch, fh, mul, mobl, mur, mobr, slo_ref,
+def lines_kernel(c_ref, mu_ref, mobx_ref, moby_ref, bx_ref, own0_ref, own1_ref, send0_ref, send1_ref, side0_ref, side1_ref, got0_ref,
+                 got1_ref, lin_hbm, rim_ref, lin_ref, ch, fh, mul, mobl, mur, mobr, slo_ref,
                  shi_ref, yl_ref, yr_ref, xl_ref, xr_ref, sems):
     row, row8 = iota((CX, CY), 0), iota((8, CY), 0)
     lane = iota((CX, CY), 1)
-    loads = ((c_hbm, c_ref), (mu_hbm, mu_ref), (mob_hbm, mob_ref), (bx_hbm, bx_ref))
-    for g in range(NZ // STEP):
-        for k, (src, dst) in enumerate(loads):
-            piece(src, dst, sems.at[k], g).start()
     odd_x, odd_y = odd_at("gx"), odd_at("gy")
 
     def edges():
@@ -144,8 +137,8 @@
         yr_ref[...] = jnp.where(odd_y, side1_ref[...], side0_ref[...])
         xl_ref[...] = jnp.where(odd_x, got0_ref[...], got1_ref[...])
         xr_ref[...] = jnp.where(odd_x, got1_ref[...], got0_ref[...])
-        own_lo = jnp.where(odd_x, own0_ref[0:NZ], own1_ref[0:NZ])
-        own_hi = jnp.where(odd_x, own1_ref[0:NZ], own0_ref[0:NZ])
+        own_lo = jnp.where(odd_x, own0_ref[...], own1_ref[...])
+        own_hi = jnp.where(odd_x, own1_ref[...], own0_ref[...])
         lo, hi, left, right = slo_ref[0:CX], shi_ref[0:CX], yl_ref[0:CX], yr_ref[0:CX]
 
         def around(a, ref):
@@ -175,8 +168,8 @@
             east = jnp.where(ln == 4 * sub, yr_ref[CX + k:CX + k + 1], 0.0)
             lf = jnp.where(ln == 0, jnp.sum(west, axis=1, keepdims=True), roll(a, 1, 1))
             rt = jnp.where(ln == CY - 1, jnp.sum(east, axis=1, keepdims=True), roll(a, -1, 1))
-            mu_out[...] = potential(a, x_ref[32:64] + own + lf + rt - 4.0 * a)
-            mob_out[...] = mobile(x_ref[64:96], a)
+            mu_out[...] = potential(a, x_ref[32:64] + own[0:32] + lf + rt - 4.0 * a)
+            mob_out[...] = mobile(x_ref[64:96], a) + mobile(own[64:96], own[0:32])
 
         halo_row(xl_ref, own_lo, 0, mul, mobl)
         halo_row(xr_ref, own_hi, 1, mur, mobr)
@@ -184,17 +177,16 @@
     edges()
 
     def step(g, carry):
-        for k, (src, dst) in enumerate(loads):
-            piece(src, dst, sems.at[k], g).wait()
         for i in range(STEP):
             plane(g * STEP + i)
-        piece(lin_ref, lin_hbm, sems.at[4], g).start()
+            if i % HALF == HALF - 1:
+                piece(lin_ref, lin_hbm, sems, 2 * g + i // HALF, HALF).start()
         return carry
 
     def plane(z):
         at = pl.ds(z, 1)
         turn = (CY - 4 * z) & (CY - 1)
-        c, mob = c_ref[z], mob_ref[z]
+        c, mobx = c_ref[z], mobx_ref[z]
         hz = roll(ch[...], turn, 1)
         fz = roll(fh[...], turn, 1)
         mu = mu_ref[z] - jnp.where((lane == 0) | (lane == CY - 1), hz, 0.0)
@@ -204,11 +196,11 @@
             mu[CX - 8:CX] - jnp.where(row8 == 7, xr_ref[at], 0.0),
         ])
         mu_d = jnp.where(row == CX - 1, mur[at], roll(mu, -1, 0))
-        mob_d = jnp.where(row == CX - 1, mobr[at], roll(mob, -1, 0))
-        fx = (mob_d + mob) * (mu_d - mu)
-        f0 = (mob[0:1] + mobl[at]) * (mu[0:1] - mul[at])
+        mobx = jnp.concatenate([mobx[:CX - 8], jnp.where(row8 == 7, mobr[at], mobx[CX - 8:])])
+        fx = mobx * (mu_d - mu)
+        f0 = mobl[at] * (mu[0:1] - mul[at])
         fx_up = jnp.where(row == 0, f0, roll(fx, 1, 0))
-        fy = (roll(mob, -1, 1) + mob) * (roll(mu, -1, 1) - mu)
+        fy = moby_ref[z] * (roll(mu, -1, 1) - mu)
         fy = jnp.where(lane == CY - 1, fz, fy)
         fy_lf = jnp.where(lane == 0, fz, roll(fy, 1, 1))
         rhs = c + 0.01 * ((fx - fx_up) + (fy - fy_lf))
@@ -218,8 +210,8 @@
         rim_ref[z, 2:4] = lin[CX - 2:CX]
 
     lax.fori_loop(0, NZ // STEP, step, 0)
-    for g in range(NZ // STEP):
-        piece(lin_ref, lin_hbm, sems.at[4], g).wait()
+    for g in range(NZ // HALF):
+        piece(lin_ref, lin_hbm, sems, g, HALF).wait()
 
 
 def reduced_kernel(r_ref, rim_ref, out_ref):
@@ -357,12 +349,9 @@
         compiler_params=CALL, name="edge",
     )(hbm(conc), hbm(mobility))
     got0, got1 = swap(own0, own1, "gx", nx)
-    *side, mu, mob = pl.pallas_call(
+    *side, mu, mobx, moby = pl.pallas_call(
         pack_kernel,
-        in_specs=[here, here],
-        out_specs=(here, here, any_space, any_space),
-        out_shape=(shape(CX, CY), shape(CX, CY), big_hbm, big_hbm),
-        scratch_shapes=[full(NZ, CX, CY)] * 2 + [pltpu.SemaphoreType.DMA((2, groups))],
+        out_shape=(shape(CX, CY),) * 2 + (shape(NZ, CX, CY),) * 3,
         compiler_params=CALL, name="pack",
     )(conc, mobility)
     send0, send1 = pl.pallas_call(
@@ -372,14 +361,13 @@
 
     lin, rims = pl.pallas_call(
         lines_kernel,
-        in_specs=[any_space] * 4 + [here] * 8,
-        out_specs=(any_space, here),
+                out_specs=(any_space, here),
         out_shape=(big_hbm, shape(NZ, 4, CY)),
-        scratch_shapes=[full(NZ, CX, CY)] * 3 + [full(NZ, CX, CX), full(NZ, CX, CY)]
+        scratch_shapes=[full(NZ, CX, CY)]
         + [full(CX, CY)] * 2 + [full(NZ, CY)] * 4 + [full(72, CY)] * 4 + [full(3 * NZ, CY)] * 2
-        + [pltpu.SemaphoreType.DMA((5, groups))],
+        + [pltpu.SemaphoreType.DMA((2 * groups,))],
         compiler_params=CALL, name="lines",
-    )(hbm(conc), hbm(mu), hbm(mob), hbm(block_x), own0, own1, send0, send1, side0, side1, got0, got1)
+    )(conc, mu, mobx, moby, block_x, own0, own1, send0, send1, side0, side1, got0, got1)
 
     lin, rims, block_y, reduced_y = lax.optimization_barrier((lin, rims, block_y, reduced_y))
     sx = jnp.transpose(spike_x, (0, 2, 1)).reshape(4 * NZ, CX)

time: 69.8 us -> 68.4 us (0.980)
  Pallas kernels: 20.6 us -> 18.5 us
  waiting for transfers between devices: 13 us -> 13.7 us
    pallas_call x2, Pallas kernels: 7.84 us -> 5.77 us  [the longest x1 4.05 us: body(): pl.pallas_call(lines_kernel, out_specs=(any_space, here), out_shape=(big_...]
  transfers between devices with their start and end apart: 6 -> 6, of which waited for: 5 -> 5; matrix products, arithmetic and copies ran while one was open for 0% -> 0% of each run, Pallas kernels for 14% -> 13%
where the time goes in v5:
time: 68.4 us; the launch traced here: 68 us
  starting transfers between devices  22.8 us (33%)
  Pallas kernels  18.5 us (27%)
  waiting for transfers between devices  13.7 us (20%)
  blocking collectives  12.9 us (19%)
    all_to_all x1, blocking collectives, body(): lax.all_to_all(solved.reshape(NZ, 4, CY), 'gx', 0, 0, tiled=True)  12.9 us
    all_to_all x1, starting transfers between devices, body(): rims = lax.all_to_all(rims, 'gx', 0, 0, tiled=True)  12.6 us
    all_to_all x1, waiting for transfers between devices, body(): rims = lax.all_to_all(rims, 'gx', 0, 0, tiled=True)  7.17 us
    ppermute x2, waiting for transfers between devices, swap(): lax.ppermute(second, axis, pairs(n, 1))  4.43 us
    pallas_call x1, Pallas kernels, body(): pl.pallas_call(lines_kernel, out_specs=(any_space, here), out_shape=(big_...  4.05 us
    pallas_call x1, Pallas kernels, body(): pl.pallas_call(couple_kernel, in_specs=[any_space, any_space, here, here]...  3.91 us
    all_to_all x1, starting transfers between devices, body(): yall = lax.all_to_all(yrim, 'gy', 0, 0, tiled=True)  3.42 us
    ppermute x2, starting transfers between devices, swap(): lax.ppermute(first, axis, pairs(n, 0))  3.41 us
  transfers between devices with their start and end apart: 6, of which 5 were waited for; matrix products, arithmetic and copies ran while one was open for 0% of the time, Pallas kernels for 13%

profile of v5, /device:TPU:1, one launch (start us, length us, event | category | flops | bytes accessed | tf_op | source)
XLA Modules:
  0.0 68.0 jit_solution(9840103215884906190)
XLA Ops:
  0.0 0.0 copy-start
  0.0 0.0 copy-start.3
  0.0 1.4 %edge.1 = (f32[96,128]{1,0:T(8,128)S(1)}, f32[96,128]{1,0:T(8,128)S(1)}) custom-call(f32[32,64,128]{2,1,0:T(8,128)} %c_ref.5, f32[32,64,128]{2,1,0:T(8,128)} %m_ref.3), custom_call_target="tpu_custom_call" | custom-call | tf_op jit(solution)/shard_map/edge/pallas_call | solution.py:344
  1.4 3.3 %collective-permute-start = (f32[96,128]{1,0:T(8,128)S(1)}, f32[96,128]{1,0:T(8,128)S(1)}, u32[]{:S(2)}, u32[]{:S(2)}) collective-permute-start(f32[96,128]{1,0:T(8,128)S(1)} %get-tuple-element.30.own0_ref), channel_id=1, source_target_pairs={{0,8},{16,24},{32,40},{48,56},{64,72},{80,88},{96,104},{112,120},{... | collective-permute-start | bytes 147464 | tf_op jit(solution)/shard_map/ppermute | solution.py:342
  4.7 1.0 %collective-permute-start.1 = (f32[96,128]{1,0:T(8,128)S(1)}, f32[96,128]{1,0:T(8,128)S(1)}, u32[]{:S(2)}, u32[]{:S(2)}) collective-permute-start(f32[96,128]{1,0:T(8,128)S(1)} %get-tuple-element.31.own1_ref), channel_id=1, source_target_pairs={{8,16},{24,32},{40,48},{56,64},{72,80},{88,96},{104,112},{120,128}... | collective-permute-start | bytes 147464 | tf_op jit(solution)/shard_map/ppermute | solution.py:342
  5.7 0.0 copy-done.1
  5.7 0.0 copy-done.2
  5.7 1.7 %pack.1 = (f32[64,128]{1,0:T(8,128)S(1)}, f32[64,128]{1,0:T(8,128)S(1)}, f32[32,64,128]{2,1,0:T(8,128)S(1)}, f32[32,64,128]{2,1,0:T(8,128)S(1)}, f32[32,64,128]{2,1,0:T(8,128)S(1)}) custom-call(f32[32,64,128]{2,1,0:T(8,128)S(1)} %copy-done.1, f32[32,64,128]{2,1,0:T(8,128)S(1)} %copy-done.2), custom_call_target="tpu_custom_call" | custom-call | tf_op jit(solution)/shard_map/pack/pallas_call | solution.py:352
  7.5 0.0 collective-permute-done.got0_ref
  7.5 2.3 %collective-permute-done.1.got1_ref = f32[96,128]{1,0:T(8,128)S(1)} collective-permute-done((f32[96,128]{1,0:T(8,128)S(1)}, f32[96,128]{1,0:T(8,128)S(1)}, u32[]{:S(2)}, u32[]{:S(2)}) %collective-permute-start.1) | collective-permute-done | bytes 49184 | tf_op jit(solution)/shard_map/ppermute | solution.py:342
  9.7 0.1 corner.1
  9.9 0.1 collective-permute-start.2
  10.0 2.4 %collective-permute-start.3 = (f32[72,128]{1,0:T(8,128)S(1)}, f32[72,128]{1,0:T(8,128)S(1)}, u32[]{:S(2)}, u32[]{:S(2)}) collective-permute-start(f32[72,128]{1,0:T(8,128)S(1)} %get-tuple-element.35.send1_ref), channel_id=1, source_target_pairs={{1,2},{3,4},{5,6},{7,0},{2,1},{4,3},{6,5},{0,7},{9,10},{11,12},{13... | collective-permute-start | bytes 110600 | tf_op jit(solution)/shard_map/ppermute | solution.py:342
  12.3 0.5 collective-permute-done.2.side0_ref
  12.8 2.2 %collective-permute-done.3.side1_ref = f32[72,128]{1,0:T(8,128)S(1)} collective-permute-done((f32[72,128]{1,0:T(8,128)S(1)}, f32[72,128]{1,0:T(8,128)S(1)}, u32[]{:S(2)}, u32[]{:S(2)}) %collective-permute-start.3) | collective-permute-done | bytes 36896 | tf_op jit(solution)/shard_map/ppermute | solution.py:342
  15.0 4.0 %lines.1 = (f32[32,64,128]{2,1,0:T(8,128)}, f32[32,4,128]{2,1,0:T(4,128)}) custom-call(f32[32,64,128]{2,1,0:T(8,128)S(1)} %copy-done.1, f32[32,64,128]{2,1,0:T(8,128)S(1)} %get-tuple-element.27.mu_ref, f32[32,64,128]{2,1,0:T(8,128)S(1)} %get-tuple-element.28.mobx_ref, f32[32,64,128]{2,1,0:T(8,128)S(1)} %get-tuple-element.29.moby_ref, ...), custom_call_target="tpu_custom_call" | custom-call | tf_op jit(solution)/shard_map/lines/pallas_call | solution.py:362
  19.0 0.0 copy-start.5
  19.0 12.6 %all-to-all-start = ((f32[32,4,128]{2,1,0:T(4,128)}), f32[32,4,128]{2,1,0:T(4,128)S(1)}, u32[]{:S(2)}, u32[]{:S(2)}) async-start(f32[32,4,128]{2,1,0:T(4,128)} %get-tuple-element.40), calls=%async_computation | async-start | bytes 131072 | tf_op jit(solution)/shard_map/all_to_all | solution.py:389
  31.6 0.0 copy-start.4
  31.6 2.6 %wide.1 = (f32[64,128]{1,0:T(8,128)S(1)}, f32[128,128]{1,0:T(8,128)S(1)}) custom-call(f32[32,64,128]{2,1,0:T(8,128)} %get-tuple-element.38.lin_hbm, f32[32,128,128]{2,1,0:T(8,128)} %by_hbm.1), custom_call_target="tpu_custom_call" | custom-call | tf_op jit(solution)/shard_map/wide/pallas_call | solution.py:375
  34.2 7.2 %all-to-all-done = f32[32,4,128]{2,1,0:T(4,128)S(1)} async-done(((f32[32,4,128]{2,1,0:T(4,128)}), f32[32,4,128]{2,1,0:T(4,128)S(1)}, u32[]{:S(2)}, u32[]{:S(2)}) %all-to-all-start) | async-done | bytes 65568 | tf_op jit(solution)/shard_map/all_to_all | solution.py:389
  41.4 0.2 reduced.1
  41.6 12.9 %all_to_all.15 = f32[32,4,128]{2,1,0:T(4,128)S(1)} all-to-all(f32[32,4,128]{2,1,0:T(4,128)S(1)} %bitcast.18), channel_id=1, replica_groups=mesh['gx'=32,'gy'=8] {'gx'}, dimensions={0} | all-to-all | bytes 131072 | tf_op jit(solution)/shard_map/all_to_all | solution.py:394
  54.5 0.0 copy-done.5
  54.5 1.1 %rims.1 = f32[8,64,128]{2,1,0:T(8,128)} custom-call(f32[64,128]{1,0:T(8,128)S(1)} %get-tuple-element.44.wrim_ref, f32[128,128]{1,0:T(8,128)S(1)} %bitcast.12, f32[128,128]{1,0:T(8,128)S(1)} %get-tuple-element.45.byr_ref, f32[128,64]{1,0:T(8,128)S(1)} %bitcast.15), custom_call_target="tpu_custom_call" | custom-call | tf_op jit(solution)/shard_map/rims/pallas_call | solution.py:396
  55.6 3.4 %all-to-all-start.2 = ((f32[8,64,128]{2,1,0:T(8,128)}), f32[8,64,128]{2,1,0:T(8,128)S(1)}, u32[]{:S(2)}, u32[]{:S(2)}) async-start(f32[8,64,128]{2,1,0:T(8,128)} %rims.1), calls=%async_computation.2 | async-start | bytes 524288 | tf_op jit(solution)/shard_map/all_to_all | solution.py:399
  59.1 0.7 diag.1
  59.7 0.0 copy-start.6
  59.8 3.9 %couple.1.u_hbm = f32[32,64,128]{2,1,0:T(8,128)} custom-call(f32[32,64,128]{2,1,0:T(8,128)} %get-tuple-element.38.lin_hbm, f32[32,128,128]{2,1,0:T(8,128)} %by_hbm.1, f32[128,128]{1,0:T(8,128)S(1)} %bitcast.13, f32[128,64]{1,0:T(8,128)S(1)} %bitcast.16), custom_call_target="tpu_custom_call" | custom-call | tf_op jit(solution)/shard_map/couple/pallas_call | solution.py:400
  63.7 1.6 %all-to-all-done.2.g_ref = f32[8,64,128]{2,1,0:T(8,128)S(1)} async-done(((f32[8,64,128]{2,1,0:T(8,128)}), f32[8,64,128]{2,1,0:T(8,128)S(1)}, u32[]{:S(2)}, u32[]{:S(2)}) %all-to-all-start.2) | async-done | bytes 262176 | tf_op jit(solution)/shard_map/all_to_all | solution.py:399
  65.3 0.0 copy-done.6
  65.3 2.8 %last.1 = f32[32,64,128]{2,1,0:T(8,128)} custom-call(f32[32,64,128]{2,1,0:T(8,128)} %couple.1.u_hbm, f32[8,64,128]{2,1,0:T(8,128)S(1)} %all-to-all-done.2.g_ref, bf16[128,1024]{1,0:T(8,128)(2,1)S(1)} %get-tuple-element.47.dh_ref, bf16[128,1024]{1,0:T(8,128)(2,1)S(1)} %get-tuple-element.48.dl_ref, f32[128,128]{1,0:T(8,128)S(1)} %bitcast.19), custom_call_target="tpu_custom_call" | custom-call | tf_op jit(solution)/shard_map/last/pallas_call | solution.py:409
  (6 shorter events, 0.0 us)
Async XLA Ops:
  0.0 31.6 %copy-start = (f32[32,128,128]{2,1,0:T(8,128)S(1)}, f32[32,128,128]{2,1,0:T(8,128)}, u32[]{:S(2)}) copy-start(f32[32,128,128]{2,1,0:T(8,128)} %param.12) | copy-start | bytes 6291460
  0.0 5.7 %copy-start.1 = (f32[32,64,128]{2,1,0:T(8,128)S(1)}, f32[32,64,128]{2,1,0:T(8,128)}, u32[]{:S(2)}) copy-start(f32[32,64,128]{2,1,0:T(8,128)} %c_ref.5) | copy-start | bytes 3145732
  0.0 5.7 %copy-start.2 = (f32[32,64,128]{2,1,0:T(8,128)S(1)}, f32[32,64,128]{2,1,0:T(8,128)}, u32[]{:S(2)}) copy-start(f32[32,64,128]{2,1,0:T(8,128)} %m_ref.3) | copy-start | bytes 3145732
  0.0 14.9 %copy-start.3 = (f32[32,64,64]{2,1,0:T(8,128)S(1)}, f32[32,64,64]{2,1,0:T(8,128)}, u32[]{:S(2)}) copy-start(f32[32,64,64]{2,1,0:T(8,128)} %bx_ref.1) | copy-start | bytes 1572868
  1.4 6.1 %collective-permute-start = (f32[96,128]{1,0:T(8,128)S(1)}, f32[96,128]{1,0:T(8,128)S(1)}, u32[]{:S(2)}, u32[]{:S(2)}) collective-permute-start(f32[96,128]{1,0:T(8,128)S(1)} %get-tuple-element.30.own0_ref), channel_id=1, source_target_pairs={{0,8},{16,24},{32,40},{48,56},{64,72},{80,88},{96,104},{112,120},{... | collective-permute-start | bytes 147464 | tf_op jit(solution)/shard_map/ppermute | solution.py:342
  4.7 5.0 %collective-permute-start.1 = (f32[96,128]{1,0:T(8,128)S(1)}, f32[96,128]{1,0:T(8,128)S(1)}, u32[]{:S(2)}, u32[]{:S(2)}) collective-permute-start(f32[96,128]{1,0:T(8,128)S(1)} %get-tuple-element.31.own1_ref), channel_id=1, source_target_pairs={{8,16},{24,32},{40,48},{56,64},{72,80},{88,96},{104,112},{120,128}... | collective-permute-start | bytes 147464 | tf_op jit(solution)/shard_map/ppermute | solution.py:342
  9.9 3.0 %collective-permute-start.2 = (f32[72,128]{1,0:T(8,128)S(1)}, f32[72,128]{1,0:T(8,128)S(1)}, u32[]{:S(2)}, u32[]{:S(2)}) collective-permute-start(f32[72,128]{1,0:T(8,128)S(1)} %get-tuple-element.34.send0_ref), channel_id=1, source_target_pairs={{0,1},{2,3},{4,5},{6,7},{1,0},{3,2},{5,4},{7,6},{8,9},{10,11},{12,... | collective-permute-start | bytes 110600 | tf_op jit(solution)/shard_map/ppermute | solution.py:342
  10.0 5.0 %collective-permute-start.3 = (f32[72,128]{1,0:T(8,128)S(1)}, f32[72,128]{1,0:T(8,128)S(1)}, u32[]{:S(2)}, u32[]{:S(2)}) collective-permute-start(f32[72,128]{1,0:T(8,128)S(1)} %get-tuple-element.35.send1_ref), channel_id=1, source_target_pairs={{1,2},{3,4},{5,6},{7,0},{2,1},{4,3},{6,5},{0,7},{9,10},{11,12},{13... | collective-permute-start | bytes 110600 | tf_op jit(solution)/shard_map/ppermute | solution.py:342
  19.0 35.5 %copy-start.5 = (f32[32,64,4]{1,2,0:T(4,128)S(1)}, f32[32,64,4]{1,2,0:T(4,128)}, u32[]{:S(2)}) copy-start(f32[32,64,4]{1,2,0:T(4,128)} %param.11) | copy-start | bytes 98308
  19.0 22.4 %all-to-all-start = ((f32[32,4,128]{2,1,0:T(4,128)}), f32[32,4,128]{2,1,0:T(4,128)S(1)}, u32[]{:S(2)}, u32[]{:S(2)}) async-start(f32[32,4,128]{2,1,0:T(4,128)} %get-tuple-element.40), calls=%async_computation | async-start | bytes 131072 | tf_op jit(solution)/shard_map/all_to_all | solution.py:389
  31.6 27.4 %copy-start.4 = (f32[32,32,32]{2,1,0:T(8,128)S(1)}, f32[32,32,32]{2,1,0:T(8,128)}, u32[]{:S(2)}) copy-start(f32[32,32,32]{2,1,0:T(8,128)} %param.15) | copy-start | bytes 393220
  55.6 9.6 %all-to-all-start.2 = ((f32[8,64,128]{2,1,0:T(8,128)}), f32[8,64,128]{2,1,0:T(8,128)S(1)}, u32[]{:S(2)}, u32[]{:S(2)}) async-start(f32[8,64,128]{2,1,0:T(8,128)} %rims.1), calls=%async_computation.2 | async-start | bytes 524288 | tf_op jit(solution)/shard_map/all_to_all | solution.py:399
  59.7 5.5 %copy-start.6 = (f32[32,128,4]{1,2,0:T(4,128)S(1)}, f32[32,128,4]{1,2,0:T(4,128)}, u32[]{:S(2)}) copy-start(f32[32,128,4]{1,2,0:T(4,128)} %param.14) | copy-start | bytes 196612

commit v6 on v5

--- a/solution.py
+++ b/solution.py
@@ -124,7 +124,7 @@
 
 
 def lines_kernel(c_ref, mu_ref, mobx_ref, moby_ref, bx_ref, own0_ref, own1_ref, send0_ref, send1_ref, side0_ref, side1_ref, got0_ref,
-                 got1_ref, lin_hbm, rim_ref, lin_ref, ch, fh, mul, mobl, mur, mobr, slo_ref,
+                 got1_ref, lin_hbm, rim_hbm, lin_ref, rim_ref, ch, fh, mul, mobl, mur, mobr, slo_ref,
                  shi_ref, yl_ref, yr_ref, xl_ref, xr_ref, sems):
     row, row8 = iota((CX, CY), 0), iota((8, CY), 0)
     lane = iota((CX, CY), 1)
@@ -180,7 +180,8 @@
         for i in range(STEP):
             plane(g * STEP + i)
             if i % HALF == HALF - 1:
-                piece(lin_ref, lin_hbm, sems, 2 * g + i // HALF, HALF).start()
+                piece(lin_ref, lin_hbm, sems.at[0], 2 * g + i // HALF, HALF).start()
+                piece(rim_ref, rim_hbm, sems.at[1], 2 * g + i // HALF, HALF).start()
         return carry
 
     def plane(z):
@@ -211,7 +212,8 @@
 
     lax.fori_loop(0, NZ // STEP, step, 0)
     for g in range(NZ // HALF):
-        piece(lin_ref, lin_hbm, sems, g, HALF).wait()
+        piece(lin_ref, lin_hbm, sems.at[0], g, HALF).wait()
+        piece(rim_ref, rim_hbm, sems.at[1], g, HALF).wait()
 
 
 def reduced_kernel(r_ref, rim_ref, out_ref):
@@ -361,11 +363,11 @@
 
     lin, rims = pl.pallas_call(
         lines_kernel,
-                out_specs=(any_space, here),
-        out_shape=(big_hbm, shape(NZ, 4, CY)),
-        scratch_shapes=[full(NZ, CX, CY)]
+                out_specs=(any_space, any_space),
+        out_shape=(big_hbm, pltpu.HBM((NZ, 4, CY), F32)),
+        scratch_shapes=[full(NZ, CX, CY), full(NZ, 4, CY)]
         + [full(CX, CY)] * 2 + [full(NZ, CY)] * 4 + [full(72, CY)] * 4 + [full(3 * NZ, CY)] * 2
-        + [pltpu.SemaphoreType.DMA((2 * groups,))],
+        + [pltpu.SemaphoreType.DMA((2, 2 * groups))],
         compiler_params=CALL, name="lines",
     )(conc, mu, mobx, moby, block_x, own0, own1, send0, send1, side0, side1, got0, got1)
 

time: 68.4 us -> 67.8 us (level)
  no operation moved by 1% of the time
where the time goes in v6:
time: 67.8 us; the launch traced here: 67.5 us
  starting transfers between devices  22.8 us (34%)
  Pallas kernels  17.9 us (26%)
  waiting for transfers between devices  13.6 us (20%)
  blocking collectives  12.9 us (19%)
    all_to_all x1, blocking collectives, body(): lax.all_to_all(solved.reshape(NZ, 4, CY), 'gx', 0, 0, tiled=True)  12.9 us
    all_to_all x1, starting transfers between devices, body(): rims = lax.all_to_all(rims, 'gx', 0, 0, tiled=True)  12.6 us
    all_to_all x1, waiting for transfers between devices, body(): rims = lax.all_to_all(rims, 'gx', 0, 0, tiled=True)  7.17 us
    ppermute x2, waiting for transfers between devices, swap(): lax.ppermute(second, axis, pairs(n, 1))  4.43 us
    pallas_call x1, Pallas kernels, body(): pl.pallas_call(couple_kernel, in_specs=[any_space, any_space, here, here]...  3.91 us
    pallas_call x1, Pallas kernels, body(): pl.pallas_call(lines_kernel, out_specs=(any_space, any_space), out_shape=...  3.49 us
    all_to_all x1, starting transfers between devices, body(): yall = lax.all_to_all(yrim, 'gy', 0, 0, tiled=True)  3.42 us
    ppermute x2, starting transfers between devices, swap(): lax.ppermute(first, axis, pairs(n, 0))  3.41 us
  transfers between devices with their start and end apart: 6, of which 5 were waited for; matrix products, arithmetic and copies ran while one was open for 0% of the time, Pallas kernels for 13%

profile of v6, /device:TPU:1, one launch (start us, length us, event | category | flops | bytes accessed | tf_op | source)
XLA Modules:
  0.0 67.5 jit_solution(18168450853717196908)
XLA Ops:
  0.0 0.0 copy-start
  0.0 0.0 copy-start.3
  0.0 1.4 %edge.1 = (f32[96,128]{1,0:T(8,128)S(1)}, f32[96,128]{1,0:T(8,128)S(1)}) custom-call(f32[32,64,128]{2,1,0:T(8,128)} %c_ref.5, f32[32,64,128]{2,1,0:T(8,128)} %m_ref.3), custom_call_target="tpu_custom_call" | custom-call | tf_op jit(solution)/shard_map/edge/pallas_call | solution.py:346
  1.4 3.3 %collective-permute-start = (f32[96,128]{1,0:T(8,128)S(1)}, f32[96,128]{1,0:T(8,128)S(1)}, u32[]{:S(2)}, u32[]{:S(2)}) collective-permute-start(f32[96,128]{1,0:T(8,128)S(1)} %get-tuple-element.30.own0_ref), channel_id=1, source_target_pairs={{0,8},{16,24},{32,40},{48,56},{64,72},{80,88},{96,104},{112,120},{... | collective-permute-start | bytes 147464 | tf_op jit(solution)/shard_map/ppermute | solution.py:344
  4.7 1.0 %collective-permute-start.1 = (f32[96,128]{1,0:T(8,128)S(1)}, f32[96,128]{1,0:T(8,128)S(1)}, u32[]{:S(2)}, u32[]{:S(2)}) collective-permute-start(f32[96,128]{1,0:T(8,128)S(1)} %get-tuple-element.31.own1_ref), channel_id=1, source_target_pairs={{8,16},{24,32},{40,48},{56,64},{72,80},{88,96},{104,112},{120,128}... | collective-permute-start | bytes 147464 | tf_op jit(solution)/shard_map/ppermute | solution.py:344
  5.7 0.0 copy-done.1
  5.7 0.0 copy-done.2
  5.7 1.7 %pack.1 = (f32[64,128]{1,0:T(8,128)S(1)}, f32[64,128]{1,0:T(8,128)S(1)}, f32[32,64,128]{2,1,0:T(8,128)S(1)}, f32[32,64,128]{2,1,0:T(8,128)S(1)}, f32[32,64,128]{2,1,0:T(8,128)S(1)}) custom-call(f32[32,64,128]{2,1,0:T(8,128)S(1)} %copy-done.1, f32[32,64,128]{2,1,0:T(8,128)S(1)} %copy-done.2), custom_call_target="tpu_custom_call" | custom-call | tf_op jit(solution)/shard_map/pack/pallas_call | solution.py:354
  7.5 0.0 collective-permute-done.got0_ref
  7.5 2.3 %collective-permute-done.1.got1_ref = f32[96,128]{1,0:T(8,128)S(1)} collective-permute-done((f32[96,128]{1,0:T(8,128)S(1)}, f32[96,128]{1,0:T(8,128)S(1)}, u32[]{:S(2)}, u32[]{:S(2)}) %collective-permute-start.1) | collective-permute-done | bytes 49184 | tf_op jit(solution)/shard_map/ppermute | solution.py:344
  9.7 0.1 corner.1
  9.9 0.1 collective-permute-start.2
  10.0 2.4 %collective-permute-start.3 = (f32[72,128]{1,0:T(8,128)S(1)}, f32[72,128]{1,0:T(8,128)S(1)}, u32[]{:S(2)}, u32[]{:S(2)}) collective-permute-start(f32[72,128]{1,0:T(8,128)S(1)} %get-tuple-element.35.send1_ref), channel_id=1, source_target_pairs={{1,2},{3,4},{5,6},{7,0},{2,1},{4,3},{6,5},{0,7},{9,10},{11,12},{13... | collective-permute-start | bytes 110600 | tf_op jit(solution)/shard_map/ppermute | solution.py:344
  12.3 0.5 collective-permute-done.2.side0_ref
  12.8 2.2 %collective-permute-done.3.side1_ref = f32[72,128]{1,0:T(8,128)S(1)} collective-permute-done((f32[72,128]{1,0:T(8,128)S(1)}, f32[72,128]{1,0:T(8,128)S(1)}, u32[]{:S(2)}, u32[]{:S(2)}) %collective-permute-start.3) | collective-permute-done | bytes 36896 | tf_op jit(solution)/shard_map/ppermute | solution.py:344
  15.0 0.0 copy-done.3
  15.0 3.5 %lines.1 = (f32[32,64,128]{2,1,0:T(8,128)}, f32[32,4,128]{2,1,0:T(4,128)}) custom-call(f32[32,64,128]{2,1,0:T(8,128)S(1)} %copy-done.1, f32[32,64,128]{2,1,0:T(8,128)S(1)} %get-tuple-element.27.mu_ref, f32[32,64,128]{2,1,0:T(8,128)S(1)} %get-tuple-element.28.mobx_ref, f32[32,64,128]{2,1,0:T(8,128)S(1)} %get-tuple-element.29.moby_ref, ...), custom_call_target="tpu_custom_call" | custom-call | tf_op jit(solution)/shard_map/lines/pallas_call | solution.py:364
  18.5 0.0 copy-start.5
  18.5 12.6 %all-to-all-start = ((f32[32,4,128]{2,1,0:T(4,128)}), f32[32,4,128]{2,1,0:T(4,128)S(1)}, u32[]{:S(2)}, u32[]{:S(2)}) async-start(f32[32,4,128]{2,1,0:T(4,128)} %get-tuple-element.40), calls=%async_computation | async-start | bytes 131072 | tf_op jit(solution)/shard_map/all_to_all | solution.py:391
  31.1 0.0 copy-start.4
  31.1 2.6 %wide.1 = (f32[64,128]{1,0:T(8,128)S(1)}, f32[128,128]{1,0:T(8,128)S(1)}) custom-call(f32[32,64,128]{2,1,0:T(8,128)} %get-tuple-element.38.lin_hbm, f32[32,128,128]{2,1,0:T(8,128)} %by_hbm.1), custom_call_target="tpu_custom_call" | custom-call | tf_op jit(solution)/shard_map/wide/pallas_call | solution.py:377
  33.7 7.2 %all-to-all-done = f32[32,4,128]{2,1,0:T(4,128)S(1)} async-done(((f32[32,4,128]{2,1,0:T(4,128)}), f32[32,4,128]{2,1,0:T(4,128)S(1)}, u32[]{:S(2)}, u32[]{:S(2)}) %all-to-all-start) | async-done | bytes 65568 | tf_op jit(solution)/shard_map/all_to_all | solution.py:391
  40.9 0.2 reduced.1
  41.0 12.9 %all_to_all.15 = f32[32,4,128]{2,1,0:T(4,128)S(1)} all-to-all(f32[32,4,128]{2,1,0:T(4,128)S(1)} %bitcast.18), channel_id=1, replica_groups=mesh['gx'=32,'gy'=8] {'gx'}, dimensions={0} | all-to-all | bytes 131072 | tf_op jit(solution)/shard_map/all_to_all | solution.py:396
  54.0 1.1 %rims.1 = f32[8,64,128]{2,1,0:T(8,128)} custom-call(f32[64,128]{1,0:T(8,128)S(1)} %get-tuple-element.44.wrim_ref, f32[128,128]{1,0:T(8,128)S(1)} %bitcast.12, f32[128,128]{1,0:T(8,128)S(1)} %get-tuple-element.45.byr_ref, f32[128,64]{1,0:T(8,128)S(1)} %bitcast.15), custom_call_target="tpu_custom_call" | custom-call | tf_op jit(solution)/shard_map/rims/pallas_call | solution.py:398
  55.1 3.4 %all-to-all-start.2 = ((f32[8,64,128]{2,1,0:T(8,128)}), f32[8,64,128]{2,1,0:T(8,128)S(1)}, u32[]{:S(2)}, u32[]{:S(2)}) async-start(f32[8,64,128]{2,1,0:T(8,128)} %rims.1), calls=%async_computation.2 | async-start | bytes 524288 | tf_op jit(solution)/shard_map/all_to_all | solution.py:401
  58.5 0.0 copy-done.4
  58.5 0.7 %diag.1 = (bf16[128,1024]{1,0:T(8,128)(2,1)S(1)}, bf16[128,1024]{1,0:T(8,128)(2,1)S(1)}) custom-call(f32[1024,32]{1,0:T(8,128)S(1)} %bitcast.14), custom_call_target="tpu_custom_call" | custom-call | tf_op jit(solution)/shard_map/diag/pallas_call | solution.py:384
  59.2 0.0 copy-start.6
  59.2 3.9 %couple.1.u_hbm = f32[32,64,128]{2,1,0:T(8,128)} custom-call(f32[32,64,128]{2,1,0:T(8,128)} %get-tuple-element.38.lin_hbm, f32[32,128,128]{2,1,0:T(8,128)} %by_hbm.1, f32[128,128]{1,0:T(8,128)S(1)} %bitcast.13, f32[128,64]{1,0:T(8,128)S(1)} %bitcast.16), custom_call_target="tpu_custom_call" | custom-call | tf_op jit(solution)/shard_map/couple/pallas_call | solution.py:402
  63.1 1.6 %all-to-all-done.2.g_ref = f32[8,64,128]{2,1,0:T(8,128)S(1)} async-done(((f32[8,64,128]{2,1,0:T(8,128)}), f32[8,64,128]{2,1,0:T(8,128)S(1)}, u32[]{:S(2)}, u32[]{:S(2)}) %all-to-all-start.2) | async-done | bytes 262176 | tf_op jit(solution)/shard_map/all_to_all | solution.py:401
  64.7 2.8 %last.1 = f32[32,64,128]{2,1,0:T(8,128)} custom-call(f32[32,64,128]{2,1,0:T(8,128)} %couple.1.u_hbm, f32[8,64,128]{2,1,0:T(8,128)S(1)} %all-to-all-done.2.g_ref, bf16[128,1024]{1,0:T(8,128)(2,1)S(1)} %get-tuple-element.47.dh_ref, bf16[128,1024]{1,0:T(8,128)(2,1)S(1)} %get-tuple-element.48.dl_ref, f32[128,128]{1,0:T(8,128)S(1)} %bitcast.19), custom_call_target="tpu_custom_call" | custom-call | tf_op jit(solution)/shard_map/last/pallas_call | solution.py:411
  (6 shorter events, 0.0 us)
Async XLA Ops:
  0.0 31.0 %copy-start = (f32[32,128,128]{2,1,0:T(8,128)S(1)}, f32[32,128,128]{2,1,0:T(8,128)}, u32[]{:S(2)}) copy-start(f32[32,128,128]{2,1,0:T(8,128)} %param.12) | copy-start | bytes 6291460
  0.0 5.7 %copy-start.1 = (f32[32,64,128]{2,1,0:T(8,128)S(1)}, f32[32,64,128]{2,1,0:T(8,128)}, u32[]{:S(2)}) copy-start(f32[32,64,128]{2,1,0:T(8,128)} %c_ref.5) | copy-start | bytes 3145732
  0.0 5.7 %copy-start.2 = (f32[32,64,128]{2,1,0:T(8,128)S(1)}, f32[32,64,128]{2,1,0:T(8,128)}, u32[]{:S(2)}) copy-start(f32[32,64,128]{2,1,0:T(8,128)} %m_ref.3) | copy-start | bytes 3145732
  0.0 14.9 %copy-start.3 = (f32[32,64,64]{2,1,0:T(8,128)S(1)}, f32[32,64,64]{2,1,0:T(8,128)}, u32[]{:S(2)}) copy-start(f32[32,64,64]{2,1,0:T(8,128)} %bx_ref.1) | copy-start | bytes 1572868
  1.4 6.1 %collective-permute-start = (f32[96,128]{1,0:T(8,128)S(1)}, f32[96,128]{1,0:T(8,128)S(1)}, u32[]{:S(2)}, u32[]{:S(2)}) collective-permute-start(f32[96,128]{1,0:T(8,128)S(1)} %get-tuple-element.30.own0_ref), channel_id=1, source_target_pairs={{0,8},{16,24},{32,40},{48,56},{64,72},{80,88},{96,104},{112,120},{... | collective-permute-start | bytes 147464 | tf_op jit(solution)/shard_map/ppermute | solution.py:344
  4.7 5.0 %collective-permute-start.1 = (f32[96,128]{1,0:T(8,128)S(1)}, f32[96,128]{1,0:T(8,128)S(1)}, u32[]{:S(2)}, u32[]{:S(2)}) collective-permute-start(f32[96,128]{1,0:T(8,128)S(1)} %get-tuple-element.31.own1_ref), channel_id=1, source_target_pairs={{8,16},{24,32},{40,48},{56,64},{72,80},{88,96},{104,112},{120,128}... | collective-permute-start | bytes 147464 | tf_op jit(solution)/shard_map/ppermute | solution.py:344
  9.9 3.0 %collective-permute-start.2 = (f32[72,128]{1,0:T(8,128)S(1)}, f32[72,128]{1,0:T(8,128)S(1)}, u32[]{:S(2)}, u32[]{:S(2)}) collective-permute-start(f32[72,128]{1,0:T(8,128)S(1)} %get-tuple-element.34.send0_ref), channel_id=1, source_target_pairs={{0,1},{2,3},{4,5},{6,7},{1,0},{3,2},{5,4},{7,6},{8,9},{10,11},{12,... | collective-permute-start | bytes 110600 | tf_op jit(solution)/shard_map/ppermute | solution.py:344
  10.0 5.0 %collective-permute-start.3 = (f32[72,128]{1,0:T(8,128)S(1)}, f32[72,128]{1,0:T(8,128)S(1)}, u32[]{:S(2)}, u32[]{:S(2)}) collective-permute-start(f32[72,128]{1,0:T(8,128)S(1)} %get-tuple-element.35.send1_ref), channel_id=1, source_target_pairs={{1,2},{3,4},{5,6},{7,0},{2,1},{4,3},{6,5},{0,7},{9,10},{11,12},{13... | collective-permute-start | bytes 110600 | tf_op jit(solution)/shard_map/ppermute | solution.py:344
  18.5 35.5 %copy-start.5 = (f32[32,64,4]{1,2,0:T(4,128)S(1)}, f32[32,64,4]{1,2,0:T(4,128)}, u32[]{:S(2)}) copy-start(f32[32,64,4]{1,2,0:T(4,128)} %param.11) | copy-start | bytes 98308
  18.5 22.4 %all-to-all-start = ((f32[32,4,128]{2,1,0:T(4,128)}), f32[32,4,128]{2,1,0:T(4,128)S(1)}, u32[]{:S(2)}, u32[]{:S(2)}) async-start(f32[32,4,128]{2,1,0:T(4,128)} %get-tuple-element.40), calls=%async_computation | async-start | bytes 131072 | tf_op jit(solution)/shard_map/all_to_all | solution.py:391
  31.1 27.4 %copy-start.4 = (f32[32,32,32]{2,1,0:T(8,128)S(1)}, f32[32,32,32]{2,1,0:T(8,128)}, u32[]{:S(2)}) copy-start(f32[32,32,32]{2,1,0:T(8,128)} %param.15) | copy-start | bytes 393220
  55.1 9.6 %all-to-all-start.2 = ((f32[8,64,128]{2,1,0:T(8,128)}), f32[8,64,128]{2,1,0:T(8,128)S(1)}, u32[]{:S(2)}, u32[]{:S(2)}) async-start(f32[8,64,128]{2,1,0:T(8,128)} %rims.1), calls=%async_computation.2 | async-start | bytes 524288 | tf_op jit(solution)/shard_map/all_to_all | solution.py:401
  59.2 5.5 %copy-start.6 = (f32[32,128,4]{1,2,0:T(4,128)S(1)}, f32[32,128,4]{1,2,0:T(4,128)}, u32[]{:S(2)}) copy-start(f32[32,128,4]{1,2,0:T(4,128)} %param.14) | copy-start | bytes 196612

commit v7 on v6

--- a/solution.py
+++ b/solution.py
@@ -6,7 +6,7 @@
 from jax.sharding import PartitionSpec as P
 
 NZ, CX, CY = 32, 64, 128
-STEP, HALF = 8, 4
+STEP, HALF = 8, 2
 F32, BF16 = jnp.float32, jnp.bfloat16
 CALL = pltpu.CompilerParams(vmem_limit_bytes=12 * 1024 * 1024)
 
@@ -180,8 +180,8 @@
         for i in range(STEP):
             plane(g * STEP + i)
             if i % HALF == HALF - 1:
-                piece(lin_ref, lin_hbm, sems.at[0], 2 * g + i // HALF, HALF).start()
-                piece(rim_ref, rim_hbm, sems.at[1], 2 * g + i // HALF, HALF).start()
+                piece(lin_ref, lin_hbm, sems.at[0], (STEP // HALF) * g + i // HALF, HALF).start()
+                piece(rim_ref, rim_hbm, sems.at[1], (STEP // HALF) * g + i // HALF, HALF).start()
         return carry
 
     def plane(z):
@@ -367,7 +367,7 @@
         out_shape=(big_hbm, pltpu.HBM((NZ, 4, CY), F32)),
         scratch_shapes=[full(NZ, CX, CY), full(NZ, 4, CY)]
         + [full(CX, CY)] * 2 + [full(NZ, CY)] * 4 + [full(72, CY)] * 4 + [full(3 * NZ, CY)] * 2
-        + [pltpu.SemaphoreType.DMA((2, 2 * groups))],
+        + [pltpu.SemaphoreType.DMA((2, NZ // HALF))],
         compiler_params=CALL, name="lines",
     )(conc, mu, mobx, moby, block_x, own0, own1, send0, send1, side0, side1, got0, got1)
 

time: 67.8 us -> 67.9 us (level)
  no operation moved by 1% of the time
where the time goes in v7:
time: 67.9 us; the launch traced here: 67.6 us
  starting transfers between devices  22.8 us (34%)
  Pallas kernels  18 us (27%)
  waiting for transfers between devices  13.6 us (20%)
  blocking collectives  12.9 us (19%)
    all_to_all x1, blocking collectives, body(): lax.all_to_all(solved.reshape(NZ, 4, CY), 'gx', 0, 0, tiled=True)  12.9 us
    all_to_all x1, starting transfers between devices, body(): rims = lax.all_to_all(rims, 'gx', 0, 0, tiled=True)  12.6 us
    all_to_all x1, waiting for transfers between devices, body(): rims = lax.all_to_all(rims, 'gx', 0, 0, tiled=True)  7.17 us
    ppermute x2, waiting for transfers between devices, swap(): lax.ppermute(second, axis, pairs(n, 1))  4.43 us
    pallas_call x1, Pallas kernels, body(): pl.pallas_call(couple_kernel, in_specs=[any_space, any_space, here, here]...  3.91 us
    pallas_call x1, Pallas kernels, body(): pl.pallas_call(lines_kernel, out_specs=(any_space, any_space), out_shape=...  3.6 us
    all_to_all x1, starting transfers between devices, body(): yall = lax.all_to_all(yrim, 'gy', 0, 0, tiled=True)  3.42 us
    ppermute x2, starting transfers between devices, swap(): lax.ppermute(first, axis, pairs(n, 0))  3.41 us
  transfers between devices with their start and end apart: 6, of which 5 were waited for; matrix products, arithmetic and copies ran while one was open for 0% of the time, Pallas kernels for 13%

profile of v7, /device:TPU:1, one launch (start us, length us, event | category | flops | bytes accessed | tf_op | source)
XLA Modules:
  0.0 67.6 jit_solution(12214302261211846602)
XLA Ops:
  0.0 0.0 copy-start
  0.0 0.0 copy-start.3
  0.0 1.4 %edge.1 = (f32[96,128]{1,0:T(8,128)S(1)}, f32[96,128]{1,0:T(8,128)S(1)}) custom-call(f32[32,64,128]{2,1,0:T(8,128)} %c_ref.5, f32[32,64,128]{2,1,0:T(8,128)} %m_ref.3), custom_call_target="tpu_custom_call" | custom-call | tf_op jit(solution)/shard_map/edge/pallas_call | solution.py:346
  1.4 3.3 %collective-permute-start = (f32[96,128]{1,0:T(8,128)S(1)}, f32[96,128]{1,0:T(8,128)S(1)}, u32[]{:S(2)}, u32[]{:S(2)}) collective-permute-start(f32[96,128]{1,0:T(8,128)S(1)} %get-tuple-element.30.own0_ref), channel_id=1, source_target_pairs={{0,8},{16,24},{32,40},{48,56},{64,72},{80,88},{96,104},{112,120},{... | collective-permute-start | bytes 147464 | tf_op jit(solution)/shard_map/ppermute | solution.py:344
  4.7 1.0 %collective-permute-start.1 = (f32[96,128]{1,0:T(8,128)S(1)}, f32[96,128]{1,0:T(8,128)S(1)}, u32[]{:S(2)}, u32[]{:S(2)}) collective-permute-start(f32[96,128]{1,0:T(8,128)S(1)} %get-tuple-element.31.own1_ref), channel_id=1, source_target_pairs={{8,16},{24,32},{40,48},{56,64},{72,80},{88,96},{104,112},{120,128}... | collective-permute-start | bytes 147464 | tf_op jit(solution)/shard_map/ppermute | solution.py:344
  5.7 0.0 copy-done.1
  5.7 0.0 copy-done.2
  5.7 1.7 %pack.1 = (f32[64,128]{1,0:T(8,128)S(1)}, f32[64,128]{1,0:T(8,128)S(1)}, f32[32,64,128]{2,1,0:T(8,128)S(1)}, f32[32,64,128]{2,1,0:T(8,128)S(1)}, f32[32,64,128]{2,1,0:T(8,128)S(1)}) custom-call(f32[32,64,128]{2,1,0:T(8,128)S(1)} %copy-done.1, f32[32,64,128]{2,1,0:T(8,128)S(1)} %copy-done.2), custom_call_target="tpu_custom_call" | custom-call | tf_op jit(solution)/shard_map/pack/pallas_call | solution.py:354
  7.5 0.0 collective-permute-done.got0_ref
  7.5 2.3 %collective-permute-done.1.got1_ref = f32[96,128]{1,0:T(8,128)S(1)} collective-permute-done((f32[96,128]{1,0:T(8,128)S(1)}, f32[96,128]{1,0:T(8,128)S(1)}, u32[]{:S(2)}, u32[]{:S(2)}) %collective-permute-start.1) | collective-permute-done | bytes 49184 | tf_op jit(solution)/shard_map/ppermute | solution.py:344
  9.7 0.1 corner.1
  9.9 0.1 collective-permute-start.2
  10.0 2.4 %collective-permute-start.3 = (f32[72,128]{1,0:T(8,128)S(1)}, f32[72,128]{1,0:T(8,128)S(1)}, u32[]{:S(2)}, u32[]{:S(2)}) collective-permute-start(f32[72,128]{1,0:T(8,128)S(1)} %get-tuple-element.35.send1_ref), channel_id=1, source_target_pairs={{1,2},{3,4},{5,6},{7,0},{2,1},{4,3},{6,5},{0,7},{9,10},{11,12},{13... | collective-permute-start | bytes 110600 | tf_op jit(solution)/shard_map/ppermute | solution.py:344
  12.3 0.5 collective-permute-done.2.side0_ref
  12.8 2.2 %collective-permute-done.3.side1_ref = f32[72,128]{1,0:T(8,128)S(1)} collective-permute-done((f32[72,128]{1,0:T(8,128)S(1)}, f32[72,128]{1,0:T(8,128)S(1)}, u32[]{:S(2)}, u32[]{:S(2)}) %collective-permute-start.3) | collective-permute-done | bytes 36896 | tf_op jit(solution)/shard_map/ppermute | solution.py:344
  15.0 0.0 copy-done.3
  15.0 3.6 %lines.1 = (f32[32,64,128]{2,1,0:T(8,128)}, f32[32,4,128]{2,1,0:T(4,128)}) custom-call(f32[32,64,128]{2,1,0:T(8,128)S(1)} %copy-done.1, f32[32,64,128]{2,1,0:T(8,128)S(1)} %get-tuple-element.27.mu_ref, f32[32,64,128]{2,1,0:T(8,128)S(1)} %get-tuple-element.28.mobx_ref, f32[32,64,128]{2,1,0:T(8,128)S(1)} %get-tuple-element.29.moby_ref, ...), custom_call_target="tpu_custom_call" | custom-call | tf_op jit(solution)/shard_map/lines/pallas_call | solution.py:364
  18.6 0.0 copy-start.5
  18.6 12.6 %all-to-all-start = ((f32[32,4,128]{2,1,0:T(4,128)}), f32[32,4,128]{2,1,0:T(4,128)S(1)}, u32[]{:S(2)}, u32[]{:S(2)}) async-start(f32[32,4,128]{2,1,0:T(4,128)} %get-tuple-element.40), calls=%async_computation | async-start | bytes 131072 | tf_op jit(solution)/shard_map/all_to_all | solution.py:391
  31.2 0.0 copy-done
  31.2 0.0 copy-start.4
  31.2 2.6 %wide.1 = (f32[64,128]{1,0:T(8,128)S(1)}, f32[128,128]{1,0:T(8,128)S(1)}) custom-call(f32[32,64,128]{2,1,0:T(8,128)} %get-tuple-element.38.lin_hbm, f32[32,128,128]{2,1,0:T(8,128)} %by_hbm.1), custom_call_target="tpu_custom_call" | custom-call | tf_op jit(solution)/shard_map/wide/pallas_call | solution.py:377
  33.8 7.2 %all-to-all-done = f32[32,4,128]{2,1,0:T(4,128)S(1)} async-done(((f32[32,4,128]{2,1,0:T(4,128)}), f32[32,4,128]{2,1,0:T(4,128)S(1)}, u32[]{:S(2)}, u32[]{:S(2)}) %all-to-all-start) | async-done | bytes 65568 | tf_op jit(solution)/shard_map/all_to_all | solution.py:391
  41.0 0.2 reduced.1
  41.2 12.9 %all_to_all.15 = f32[32,4,128]{2,1,0:T(4,128)S(1)} all-to-all(f32[32,4,128]{2,1,0:T(4,128)S(1)} %bitcast.18), channel_id=1, replica_groups=mesh['gx'=32,'gy'=8] {'gx'}, dimensions={0} | all-to-all | bytes 131072 | tf_op jit(solution)/shard_map/all_to_all | solution.py:396
  54.1 1.1 %rims.1 = f32[8,64,128]{2,1,0:T(8,128)} custom-call(f32[64,128]{1,0:T(8,128)S(1)} %get-tuple-element.44.wrim_ref, f32[128,128]{1,0:T(8,128)S(1)} %bitcast.12, f32[128,128]{1,0:T(8,128)S(1)} %get-tuple-element.45.byr_ref, f32[128,64]{1,0:T(8,128)S(1)} %bitcast.15), custom_call_target="tpu_custom_call" | custom-call | tf_op jit(solution)/shard_map/rims/pallas_call | solution.py:398
  55.2 3.4 %all-to-all-start.2 = ((f32[8,64,128]{2,1,0:T(8,128)}), f32[8,64,128]{2,1,0:T(8,128)S(1)}, u32[]{:S(2)}, u32[]{:S(2)}) async-start(f32[8,64,128]{2,1,0:T(8,128)} %rims.1), calls=%async_computation.2 | async-start | bytes 524288 | tf_op jit(solution)/shard_map/all_to_all | solution.py:401
  58.6 0.7 %diag.1 = (bf16[128,1024]{1,0:T(8,128)(2,1)S(1)}, bf16[128,1024]{1,0:T(8,128)(2,1)S(1)}) custom-call(f32[1024,32]{1,0:T(8,128)S(1)} %bitcast.14), custom_call_target="tpu_custom_call" | custom-call | tf_op jit(solution)/shard_map/diag/pallas_call | solution.py:384
  59.3 0.0 copy-start.6
  59.3 3.9 %couple.1.u_hbm = f32[32,64,128]{2,1,0:T(8,128)} custom-call(f32[32,64,128]{2,1,0:T(8,128)} %get-tuple-element.38.lin_hbm, f32[32,128,128]{2,1,0:T(8,128)} %by_hbm.1, f32[128,128]{1,0:T(8,128)S(1)} %bitcast.13, f32[128,64]{1,0:T(8,128)S(1)} %bitcast.16), custom_call_target="tpu_custom_call" | custom-call | tf_op jit(solution)/shard_map/couple/pallas_call | solution.py:402
  63.2 1.6 %all-to-all-done.2.g_ref = f32[8,64,128]{2,1,0:T(8,128)S(1)} async-done(((f32[8,64,128]{2,1,0:T(8,128)}), f32[8,64,128]{2,1,0:T(8,128)S(1)}, u32[]{:S(2)}, u32[]{:S(2)}) %all-to-all-start.2) | async-done | bytes 262176 | tf_op jit(solution)/shard_map/all_to_all | solution.py:401
  64.8 2.8 %last.1 = f32[32,64,128]{2,1,0:T(8,128)} custom-call(f32[32,64,128]{2,1,0:T(8,128)} %couple.1.u_hbm, f32[8,64,128]{2,1,0:T(8,128)S(1)} %all-to-all-done.2.g_ref, bf16[128,1024]{1,0:T(8,128)(2,1)S(1)} %get-tuple-element.47.dh_ref, bf16[128,1024]{1,0:T(8,128)(2,1)S(1)} %get-tuple-element.48.dl_ref, f32[128,128]{1,0:T(8,128)S(1)} %bitcast.19), custom_call_target="tpu_custom_call" | custom-call | tf_op jit(solution)/shard_map/last/pallas_call | solution.py:411
  (6 shorter events, 0.0 us)
Async XLA Ops:
  0.0 31.2 %copy-start = (f32[32,128,128]{2,1,0:T(8,128)S(1)}, f32[32,128,128]{2,1,0:T(8,128)}, u32[]{:S(2)}) copy-start(f32[32,128,128]{2,1,0:T(8,128)} %param.12) | copy-start | bytes 6291460
  0.0 5.7 %copy-start.1 = (f32[32,64,128]{2,1,0:T(8,128)S(1)}, f32[32,64,128]{2,1,0:T(8,128)}, u32[]{:S(2)}) copy-start(f32[32,64,128]{2,1,0:T(8,128)} %c_ref.5) | copy-start | bytes 3145732
  0.0 5.7 %copy-start.2 = (f32[32,64,128]{2,1,0:T(8,128)S(1)}, f32[32,64,128]{2,1,0:T(8,128)}, u32[]{:S(2)}) copy-start(f32[32,64,128]{2,1,0:T(8,128)} %m_ref.3) | copy-start | bytes 3145732
  0.0 14.9 %copy-start.3 = (f32[32,64,64]{2,1,0:T(8,128)S(1)}, f32[32,64,64]{2,1,0:T(8,128)}, u32[]{:S(2)}) copy-start(f32[32,64,64]{2,1,0:T(8,128)} %bx_ref.1) | copy-start | bytes 1572868
  1.4 6.1 %collective-permute-start = (f32[96,128]{1,0:T(8,128)S(1)}, f32[96,128]{1,0:T(8,128)S(1)}, u32[]{:S(2)}, u32[]{:S(2)}) collective-permute-start(f32[96,128]{1,0:T(8,128)S(1)} %get-tuple-element.30.own0_ref), channel_id=1, source_target_pairs={{0,8},{16,24},{32,40},{48,56},{64,72},{80,88},{96,104},{112,120},{... | collective-permute-start | bytes 147464 | tf_op jit(solution)/shard_map/ppermute | solution.py:344
  4.7 5.0 %collective-permute-start.1 = (f32[96,128]{1,0:T(8,128)S(1)}, f32[96,128]{1,0:T(8,128)S(1)}, u32[]{:S(2)}, u32[]{:S(2)}) collective-permute-start(f32[96,128]{1,0:T(8,128)S(1)} %get-tuple-element.31.own1_ref), channel_id=1, source_target_pairs={{8,16},{24,32},{40,48},{56,64},{72,80},{88,96},{104,112},{120,128}... | collective-permute-start | bytes 147464 | tf_op jit(solution)/shard_map/ppermute | solution.py:344
  9.9 3.0 %collective-permute-start.2 = (f32[72,128]{1,0:T(8,128)S(1)}, f32[72,128]{1,0:T(8,128)S(1)}, u32[]{:S(2)}, u32[]{:S(2)}) collective-permute-start(f32[72,128]{1,0:T(8,128)S(1)} %get-tuple-element.34.send0_ref), channel_id=1, source_target_pairs={{0,1},{2,3},{4,5},{6,7},{1,0},{3,2},{5,4},{7,6},{8,9},{10,11},{12,... | collective-permute-start | bytes 110600 | tf_op jit(solution)/shard_map/ppermute | solution.py:344
  10.0 5.0 %collective-permute-start.3 = (f32[72,128]{1,0:T(8,128)S(1)}, f32[72,128]{1,0:T(8,128)S(1)}, u32[]{:S(2)}, u32[]{:S(2)}) collective-permute-start(f32[72,128]{1,0:T(8,128)S(1)} %get-tuple-element.35.send1_ref), channel_id=1, source_target_pairs={{1,2},{3,4},{5,6},{7,0},{2,1},{4,3},{6,5},{0,7},{9,10},{11,12},{13... | collective-permute-start | bytes 110600 | tf_op jit(solution)/shard_map/ppermute | solution.py:344
  18.6 35.5 %copy-start.5 = (f32[32,64,4]{1,2,0:T(4,128)S(1)}, f32[32,64,4]{1,2,0:T(4,128)}, u32[]{:S(2)}) copy-start(f32[32,64,4]{1,2,0:T(4,128)} %param.11) | copy-start | bytes 98308
  18.6 22.4 %all-to-all-start = ((f32[32,4,128]{2,1,0:T(4,128)}), f32[32,4,128]{2,1,0:T(4,128)S(1)}, u32[]{:S(2)}, u32[]{:S(2)}) async-start(f32[32,4,128]{2,1,0:T(4,128)} %get-tuple-element.40), calls=%async_computation | async-start | bytes 131072 | tf_op jit(solution)/shard_map/all_to_all | solution.py:391
  31.2 27.4 %copy-start.4 = (f32[32,32,32]{2,1,0:T(8,128)S(1)}, f32[32,32,32]{2,1,0:T(8,128)}, u32[]{:S(2)}) copy-start(f32[32,32,32]{2,1,0:T(8,128)} %param.15) | copy-start | bytes 393220
  55.2 9.6 %all-to-all-start.2 = ((f32[8,64,128]{2,1,0:T(8,128)}), f32[8,64,128]{2,1,0:T(8,128)S(1)}, u32[]{:S(2)}, u32[]{:S(2)}) async-start(f32[8,64,128]{2,1,0:T(8,128)} %rims.1), calls=%async_computation.2 | async-start | bytes 524288 | tf_op jit(solution)/shard_map/all_to_all | solution.py:401
  59.3 5.5 %copy-start.6 = (f32[32,128,4]{1,2,0:T(4,128)S(1)}, f32[32,128,4]{1,2,0:T(4,128)}, u32[]{:S(2)}) copy-start(f32[32,128,4]{1,2,0:T(4,128)} %param.14) | copy-start | bytes 196612
